TPU v7x, 256 devices: a whole 4x4x8 slice. The times are simulated.
256 devices in a mesh: dp: 32 (over z, x), tensor: 8 (over y, core).
Axes of the slice: x: 4, y: 4, z: 8, core: 2. Of those that a mesh axis runs over, the one named last changes fastest.
Arguments:
- tokens: bfloat16 [32768, 8192], P('dp', 'tensor'), may hold values from -6 to 6
- key_value_weight: bfloat16 [8192, 8, 256], P('tensor'), may hold values from -0.09375 to 0.09375
- key_value_bias: bfloat16 [8, 256], P('tensor'), may hold values from -3 to 3
- adapter_down_weight: bfloat16 [64, 8192, 128], P('dp', 'tensor'), may hold values from -0.0625 to 0.0625
- adapter_up_weight: bfloat16 [64, 8, 2, 64, 128], P('dp', 'tensor'), may hold values from -0.75 to 0.75
- conversation_adapter: int32 [512], replicated, may hold values from 0 to 63, as said below
- adapter_slot_table: int32 [64], replicated, may hold values from 0 to 63, as said below
- span_length: int32 [512], P('dp'), may hold values from 40 to 64, as said below
- context_length: int32 [512], P('dp'), may hold values from 0 to 4096
Outputs:
- new_kv: bfloat16 [8, 32768, 256], P('tensor', 'dp')
Inputs may be any that keep to these rules, and one draw needn't show every extreme that they name: `conversation_adapter`: the 16 conversations of each index of dp use adapters whose slots lie on 16 different owners (owner of slot p: p // 2), so an owner serves at most one conversation of each index of dp, and some owner serves one of every index. `adapter_slot_table`: A permutation: every storage slot holds exactly one adapter. `span_length`: every index of dp has a conversation whose span fills all 64 slots.
All inputs are finite; a program needn't handle non-finite values.
Results may differ from a plain program's by a relative error of at most 0.019.
Values may be sent and summed in bfloat16 or wider, within the bound.
No kernel may reach another device: no remote copies, remote signals or barrier semaphores. Data moves between devices by JAX's collectives and lax.ppermute only.
A program may use at most 128 MiB of HBM per device.

v0:
```python
import math

import jax
import jax.numpy as jnp
from jax import lax
from jax.sharding import PartitionSpec as P

rope_base = 1000000.0


def rotary(key_part, positions):
    half_dim = key_part.shape[-1] // 2
    inverse_freq = jnp.exp(
        jnp.arange(half_dim, dtype=jnp.float32) * (-2.0 * math.log(rope_base) / key_part.shape[-1])
    )
    angles = positions[:, None] * inverse_freq[None, :]
    angles = jnp.concatenate([angles, angles], axis=-1)
    turned = jnp.concatenate([-key_part[..., half_dim:], key_part[..., :half_dim]], axis=-1)
    return key_part * jnp.cos(angles) + turned * jnp.sin(angles)


def body(
    tokens,
    key_value_weight,
    key_value_bias,
    adapter_down_weight,
    adapter_up_weight,
    conversation_adapter,
    adapter_slot_table,
    span_length,
    context_length,
):
    dp_count = lax.axis_size("dp")
    owner_index = lax.axis_index("dp")
    conversation_present = span_length.shape[0]
    span_token_rows = tokens.shape[0] // conversation_present
    slice_width = tokens.shape[1]
    heads_present = key_value_bias.shape[0]
    head_span_width = key_value_bias.shape[1]
    head_dim = head_span_width // 2
    locally_stored = adapter_down_weight.shape[0]
    double_rank = adapter_down_weight.shape[2]
    adapter_ids = jnp.arange(adapter_slot_table.shape[0], dtype=jnp.int32)
    storage = jnp.sum(
        jnp.where(
            conversation_adapter[:, None] == adapter_ids[None, :], adapter_slot_table[None, :], 0
        ),
        axis=1,
    )
    owner_table = (storage // locally_stored).reshape(dp_count, conversation_present)
    local_table = (storage % locally_stored).reshape(dp_count, conversation_present)
    my_owners = lax.dynamic_slice_in_dim(owner_table, owner_index, 1, 0)[0]
    owner_ids = jnp.arange(dp_count, dtype=jnp.int32)
    routing = (my_owners[:, None] == owner_ids[None, :]).astype(jnp.bfloat16)
    served = owner_table == owner_index
    stored_ids = jnp.arange(locally_stored, dtype=jnp.int32)
    picked = served[:, :, None] & (local_table[:, :, None] == stored_ids[None, None, :])
    selector_f = jnp.sum(jnp.where(picked, 1.0, 0.0), axis=1).astype(jnp.float32)
    slot_chooser = selector_f.astype(jnp.bfloat16)
    conversation_rows = tokens.reshape(conversation_present, span_token_rows, slice_width)
    base_sum = lax.psum_scatter(
        jnp.einsum(
            "td,dhe->hte", tokens, key_value_weight, preferred_element_type=jnp.float32
        ).astype(jnp.bfloat16),
        "tensor",
        scatter_dimension=0,
        tiled=True,
    ).astype(jnp.float32)
    down_out = jnp.einsum(
        "fw,wqn->fqn", slot_chooser, adapter_down_weight, preferred_element_type=jnp.float32
    ).astype(jnp.bfloat16)
    up_out = jnp.einsum(
        "cp,ptdbi->ctdbi", slot_chooser, adapter_up_weight, preferred_element_type=jnp.float32
    ).astype(jnp.bfloat16)
    down_got, up_got = (
        lax.all_to_all(down_out, "dp", split_axis=0, concat_axis=0, tiled=True),
        lax.all_to_all(up_out, "dp", split_axis=0, concat_axis=0, tiled=True),
    )
    down_conv = jnp.einsum(
        "co,odk->cdk", routing, down_got, preferred_element_type=jnp.float32
    ).astype(jnp.bfloat16)
    up_conv = jnp.einsum(
        "co,ohgmf->chgmf", routing, up_got, preferred_element_type=jnp.float32
    ).astype(jnp.bfloat16)
    rank_part = jnp.einsum(
        "crd,cdk->crk", conversation_rows, down_conv, preferred_element_type=jnp.float32
    )
    rank_sum = lax.psum(rank_part.astype(jnp.bfloat16), "tensor")
    rank_halves = rank_sum.reshape(conversation_present, span_token_rows, 2, double_rank // 2)
    adapter_delta = jnp.einsum(
        "crgm,chgmf->crhgf", rank_halves, up_conv, preferred_element_type=jnp.float32
    ).astype(jnp.bfloat16)
    conversation_delta = adapter_delta.reshape(
        conversation_present, span_token_rows, heads_present * head_span_width
    ).astype(jnp.float32)
    delta_heads = jnp.transpose(
        conversation_delta.reshape(
            conversation_present * span_token_rows, heads_present, head_span_width
        ),
        (1, 0, 2),
    )
    projected = base_sum + key_value_bias.astype(jnp.float32)[:, None, :] + delta_heads
    positions = (
        (context_length[:, None] + jnp.arange(span_token_rows, dtype=jnp.int32)[None, :])
        .reshape(-1)
        .astype(jnp.float32)
    )
    rotated = rotary(projected[..., :head_dim], positions)
    live_mask = (
        jnp.arange(span_token_rows, dtype=jnp.int32)[None, :] < span_length[:, None]
    ).reshape(-1)
    joined = jnp.concatenate([rotated, projected[..., head_dim:]], axis=-1)
    return jnp.where(live_mask[None, :, None], joined, 0.0).astype(jnp.bfloat16)


def solution(mesh):
    placed = (
        P("dp", "tensor"),
        P("tensor", None, None),
        P("tensor", None),
        P("dp", "tensor", None),
        P("dp", "tensor", None, None, None),
        P(),
        P(),
        P("dp"),
        P("dp"),
    )
    return jax.shard_map(
        body, mesh=mesh, in_specs=placed, out_specs=P("tensor", "dp", None), check_vma=False
    )
```

profile of v0, /device:TPU:1, one launch (start us, length us, event | category | flops | bytes accessed | tf_op | source)
XLA Modules:
  0.0 360.6 jit_solution(12888447951929034178)
XLA Ops:
  6.5 0.0 copy-start
  6.5 0.9 select_reduce_fusion
  7.5 0.1 reduce_sum.21
  7.6 0.1 copy.78
  7.7 6.7 %convolution_convert_fusion = bf16[32,1024,128]{2,0,1:T(8,128)(2,1)} fusion(bf16[2,1024,128]{2,1,0:T(8,128)(2,1)} %param.12, bf16[32,2]{0,1:T(2,128)(2,1)S(1)} %select_reduce_fusion.1), kind=kOutput, calls=%fused_computation.2 | convolution fusion | flops 20971520 | bytes 8913024 | tf_op jit(solution)/shard_map/fw,wqn->fqn/dot_general | solution.py:69
  14.3 9.8 %copy.86 = bf16[32,1024,128]{2,1,0:T(8,128)(2,1)} copy(bf16[32,1024,128]{2,0,1:T(8,128)(2,1)} %convolution_convert_fusion) | data formatting | bytes 16777216 | tf_op jit(solution)/shard_map/convert_element_type | solution.py:71
  24.2 12.0 %all-to-all-start.1 = ((bf16[32,1024,128]{2,1,0:T(8,128)(2,1)}), bf16[32,1024,128]{2,1,0:T(8,128)(2,1)}, u32[]{:S(2)}, u32[]{:S(2)}) async-start(bf16[32,1024,128]{2,1,0:T(8,128)(2,1)} %copy.86), calls=%async_computation.2 | async-start | bytes 16777216 | tf_op jit(solution)/shard_map/all_to_all | solution.py:76
  36.2 0.2 all-reduce.2.cloned.1.call-start
  36.4 0.2 dynamic-slice_reduce_fusion
  36.6 187.1 %all-to-all-done.1 = bf16[32,1024,128]{2,1,0:T(8,128)(2,1)} async-done(((bf16[32,1024,128]{2,1,0:T(8,128)(2,1)}), bf16[32,1024,128]{2,1,0:T(8,128)(2,1)}, u32[]{:S(2)}, u32[]{:S(2)}) %all-to-all-start.1) | async-done | bytes 8388640 | tf_op jit(solution)/shard_map/all_to_all | solution.py:76
  223.7 8.4 %fusion.8 = bf16[16,1024,128]{2,0,1:T(8,128)(2,1)S(1)} fusion(bf16[32,1024,128]{2,1,0:T(8,128)(2,1)} %all-to-all-done.1, s32[16]{0:T(128)S(1)} %dynamic-slice_reduce_fusion), kind=kOutput, calls=%fused_computation.8 | convolution fusion | flops 136315392 | bytes 12582976 | tf_op jit(solution)/shard_map/co,odk->cdk/dot_general | solution.py:79
  232.2 0.0 copy-done
  232.2 2.4 fusion.19
  234.6 0.2 reshape.341
  234.9 0.9 copy.89
  235.8 0.0 all-reduce.2.cloned.1.call-update
  235.8 0.0 reduce-scatter.2.cloned.1.call-start
  235.9 9.1 %convert_bitcast_fusion = bf16[8,1024,256]{1,2,0:T(8,128)(2,1)} fusion(bf16[1024,8,256]{2,1,0:T(8,128)(2,1)} %param.10, bf16[1024,1024]{1,0:T(8,128)(2,1)S(1)} %copy-done), kind=kOutput, calls=%fused_computation.7 | convolution fusion | flops 4297064448 | bytes 10485760 | tf_op jit(solution)/shard_map/td,dhe->hte/dot_general | solution.py:62
  245.0 0.0 copy-start.1
  245.0 0.0 copy-start.2
  245.0 0.0 copy-start.3
  245.0 0.0 copy-start.4
  245.0 0.0 reduce-scatter.2.cloned.1.call-update
  245.0 0.8 copy-done.1
  245.8 0.5 fusion.12
  246.3 1.4 copy.83
  247.7 15.7 %all-to-all-start = ((bf16[32,1,2,64,128]{4,3,2,1,0:T(8,128)(2,1)}), bf16[32,1,2,64,128]{4,3,2,1,0:T(8,128)(2,1)S(1)}, u32[]{:S(2)}, u32[]{:S(2)}) async-start(bf16[32,1,2,64,128]{4,3,2,1,0:T(8,128)(2,1)} %copy.83), calls=%async_computation.1 | async-start | bytes 2097152 | tf_op jit(solution)/shard_map/all_to_all | solution.py:77
  263.4 0.0 copy-done.2
  263.4 0.0 copy-done.3
  263.4 0.1 add_convert_fusion
  263.5 0.1 convert_element_type.98
  263.6 0.0 copy-done.4
  263.6 0.1 iota_compare_fusion.3
  263.7 0.1 lt.34
  263.8 0.1 multiply_bitcast_fusion
  263.9 25.5 %all-to-all-done = bf16[32,1,2,64,128]{4,3,2,1,0:T(8,128)(2,1)S(1)} async-done(((bf16[32,1,2,64,128]{4,3,2,1,0:T(8,128)(2,1)}), bf16[32,1,2,64,128]{4,3,2,1,0:T(8,128)(2,1)S(1)}, u32[]{:S(2)}, u32[]{:S(2)}) %all-to-all-start) | async-done | bytes 1048608 | tf_op jit(solution)/shard_map/all_to_all | solution.py:77
  289.3 1.5 convolution_convert_fusion.3
  290.8 17.2 %all-reduce.2.cloned.1.call-done = bf16[16,64,2,64]{3,1,2,0:T(8,128)(2,1)} async-done(((bf16[16,64,2,64]{3,1,2,0:T(8,128)(2,1)}), bf16[16,64,2,64]{3,1,2,0:T(8,128)(2,1)}) %all-reduce.2.cloned.1.call-update) | async-done | bytes 262160 | tf_op jit(solution)/shard_map/psum | solution.py:88
  308.0 1.5 fusion.15
  309.5 1.8 copy.91
  311.3 2.3 copy.92
  313.6 35.8 %reduce-scatter.2.cloned.1.call-done = bf16[1,1024,256]{1,2,0:T(8,128)(2,1)} async-done(((bf16[8,1024,256]{1,2,0:T(8,128)(2,1)}), bf16[1,1024,256]{1,2,0:T(8,128)(2,1)}) %reduce-scatter.2.cloned.1.call-update) | async-done | bytes 524304 | tf_op jit(solution)/shard_map/reduce_scatter | solution.py:61
  349.4 1.2 add_add_fusion
  350.7 2.0 fusion.25
  352.7 0.1 fusion.22
  352.8 1.0 copy.93
  (6 shorter events, 0.1 us)
Async XLA Ops:
  6.5 225.6 %copy-start = (bf16[1024,1024]{1,0:T(8,128)(2,1)S(1)}, bf16[1024,1024]{1,0:T(8,128)(2,1)}, u32[]{:S(2)}) copy-start(bf16[1024,1024]{1,0:T(8,128)(2,1)} %param.9) | copy-start | bytes 6291460
  24.2 199.6 %all-to-all-start.1 = ((bf16[32,1024,128]{2,1,0:T(8,128)(2,1)}), bf16[32,1024,128]{2,1,0:T(8,128)(2,1)}, u32[]{:S(2)}, u32[]{:S(2)}) async-start(bf16[32,1024,128]{2,1,0:T(8,128)(2,1)} %copy.86), calls=%async_computation.2 | async-start | bytes 16777216 | tf_op jit(solution)/shard_map/all_to_all | solution.py:76
  36.2 271.8 %all-reduce.2.cloned.1.call-start = ((), (), s32[]{:S(2)}) async-start(), calls=%async_computation.4 | async-start | bytes 1048576 | tf_op jit(solution)/shard_map/psum | solution.py:88
  235.8 113.6 %reduce-scatter.2.cloned.1.call-start = ((), (), s32[]{:S(2)}) async-start(), calls=%async_computation.3 | async-start | bytes 4718592 | tf_op jit(solution)/shard_map/reduce_scatter | solution.py:61
  245.0 0.8 copy-start.1
  245.0 18.4 %copy-start.2 = (bf16[1,256]{1,0:T(2,128)(2,1)S(1)}, bf16[1,256]{1,0:T(2,128)(2,1)}, u32[]{:S(2)}) copy-start(bf16[1,256]{1,0:T(2,128)(2,1)} %param.11) | copy-start | bytes 1540
  245.0 18.4 %copy-start.3 = (s32[16]{0:T(128)S(1)}, s32[16]{0:T(128)}, u32[]{:S(2)}) copy-start(s32[16]{0:T(128)} %param.17) | copy-start | bytes 196
  245.0 18.6 %copy-start.4 = (s32[16]{0:T(128)S(1)}, s32[16]{0:T(128)}, u32[]{:S(2)}) copy-start(s32[16]{0:T(128)} %param.16) | copy-start | bytes 196
  247.7 41.6 %all-to-all-start = ((bf16[32,1,2,64,128]{4,3,2,1,0:T(8,128)(2,1)}), bf16[32,1,2,64,128]{4,3,2,1,0:T(8,128)(2,1)S(1)}, u32[]{:S(2)}, u32[]{:S(2)}) async-start(bf16[32,1,2,64,128]{4,3,2,1,0:T(8,128)(2,1)} %copy.83), calls=%async_computation.1 | async-start | bytes 2097152 | tf_op jit(solution)/shard_map/all_to_all | solution.py:77
Sparse Core Ops, SparseCore 0:
  235.9 72.0 all-reduce.1
  310.7 38.6 reduce-scatter.1
where the time goes:
time: 363 us; the launch traced here: 361 us
  waiting for transfers between devices  266 us (73%)
  matrix products  30.1 us (8%)
  starting transfers between devices  28 us (8%)
  local copies, waits for them, and re-layouts  18.8 us (5%)
  between operations  13.6 us (4%)
  other arithmetic  4.58 us (1%)
    all_to_all x1, waiting for transfers between devices, body(): lax.all_to_all(down_out, 'dp', split_axis=0, concat_axis=0, tiled=True)  187 us
    reduce_scatter x1, waiting for transfers between devices, body(): lax.psum_scatter(jnp.einsum('td,dhe->hte', tokens, key_value_weight, pref...  35.8 us
    all_to_all x1, waiting for transfers between devices, body(): lax.all_to_all(up_out, 'dp', split_axis=0, concat_axis=0, tiled=True)  25.5 us
    psum x1, waiting for transfers between devices, body(): rank_sum = lax.psum(rank_part.astype(jnp.bfloat16), 'tensor')  17.2 us
    all_to_all x1, starting transfers between devices, body(): lax.all_to_all(up_out, 'dp', split_axis=0, concat_axis=0, tiled=True)  15.7 us
    all_to_all x1, starting transfers between devices, body(): lax.all_to_all(down_out, 'dp', split_axis=0, concat_axis=0, tiled=True)  12 us
    convert_element_type x1, local copies, waits for them, and re-layouts, body(): down_out = jnp.einsum('fw,wqn->fqn', slot_chooser, adapter_down_weight, p...  9.84 us
    dot_general x1, matrix products, body(): jnp.einsum('td,dhe->hte', tokens, key_value_weight, preferred_element_typ...  9.13 us
  transfers between devices with their start and end apart: 4, of which 4 were waited for; matrix products, arithmetic and copies ran while one was open for 5% of the time, Pallas kernels for 0%

commit v1 on v0

v1 whole, which is shorter than its diff:
```python
import functools
import math

import jax
import jax.numpy as jnp
from jax import lax
from jax.experimental import pallas as pl
from jax.experimental.pallas import tpu as pltpu
from jax.sharding import PartitionSpec as P

rope_base = 1000000.0
NZ, NX, NY, NC = 8, 4, 4, 2
BF = jnp.bfloat16
F32 = jnp.float32


def shift_x(v, s):
    pairs = [(z * NX + x, z * NX + (x + s) % NX) for z in range(NZ) for x in range(NX)]
    return lax.ppermute(v, "dp", pairs)


def shift_z(v, s):
    pairs = [(z * NX + x, ((z + s) % NZ) * NX + x) for z in range(NZ) for x in range(NX)]
    return lax.ppermute(v, "dp", pairs)


def shift_y(v, s):
    pairs = [(y * NC + c, ((y + s) % NY) * NC + c) for y in range(NY) for c in range(NC)]
    return lax.ppermute(v, "tensor", pairs)


def swap_core(v):
    return lax.ppermute(v, "tensor", [(t, t ^ 1) for t in range(NY * NC)])


def slot_of(ca_ref, table_ref, index, z, x):
    storage = table_ref[ca_ref[index]]
    owner = storage >> 1
    across = ((owner & (NX - 1)) - x) & (NX - 1)
    along = ((owner >> 2) - z) & (NZ - 1)
    return across, along, storage & 1


def pack_kernel(ca_ref, table_ref, tok_ref, o0, o1, o2, o3, sem):
    d = lax.axis_index("dp")
    z, x = d >> 2, d & (NX - 1)
    convs = tok_ref.shape[0]

    def step(i, carry):
        across, along, _ = slot_of(ca_ref, table_ref, d * convs + i, z, x)
        for r, out in enumerate((o0, o1, o2, o3)):

            @pl.when(across == r)
            def _():
                pltpu.make_async_copy(tok_ref.at[i], out.at[along], sem).start()

        return carry

    lax.fori_loop(0, convs, step, 0)
    pltpu.make_async_copy(tok_ref, tok_ref, sem).wait()


def plan_kernel(ca_ref, table_ref, choice_ref, place_ref):
    d = lax.axis_index("dp")
    z, x = d >> 2, d & (NX - 1)
    convs = place_ref.shape[0]

    def clear(i, carry):
        choice_ref[i] = 0
        return carry

    lax.fori_loop(0, NX * NZ, clear, 0)

    def step(i, carry):
        across, along, _ = slot_of(ca_ref, table_ref, d * convs + i, z, x)
        place_ref[i] = across * NZ + along
        for r in range(NX):
            xs = (x - r) & (NX - 1)
            across_r, along_r, which = slot_of(ca_ref, table_ref, (z * NX + xs) * convs + i, z, xs)

            @pl.when(across_r == r)
            def _():
                choice_ref[r * NZ + along_r] = which

        return carry

    lax.fori_loop(0, convs, step, 0)


def rank_kernel(choice_ref, *refs):
    toks = refs[0:4]
    stacks = refs[4:13]
    ranks = refs[13:17]
    ups = refs[17:21]
    depth = toks[0].shape[2]
    width = stacks[0].shape[2]
    rows = toks[0].shape[1]
    for k in range(NZ):
        tok = jnp.concatenate([t[k] for t in toks], axis=0)
        if k == NZ // 2:
            first, second = stacks[k], stacks[NZ]
            w = jnp.concatenate([first[:depth], second[:depth]], axis=1)
        else:
            w = jnp.concatenate([stacks[k][0, :depth], stacks[k][1, :depth]], axis=1)
        res = jnp.dot(tok, w, preferred_element_type=F32)
        for r in range(NX):
            which = choice_ref[r * NZ + k]
            part = res[r * rows : (r + 1) * rows]
            ranks[r][k] = jnp.where(which == 1, part[:, width:], part[:, :width]).astype(BF)
            if k == NZ // 2:
                ups[r][k] = jnp.where(which == 1, second[depth:], first[depth:])
            else:
                ups[r][k] = stacks[k][which, depth:]


def pick(sources, place, count):
    across, along = place >> 3, place & (NZ - 1)
    value = sources[0][along]
    for r in range(1, count):
        value = jnp.where(across == r, sources[r][along], value)
    return value


def unslot_kernel(place_ref, g0, g1, g2, g3, keep, send):
    c = lax.axis_index("tensor") & 1
    half = keep.shape[0]
    for j in range(half):
        keep[j] = pick((g0, g1, g2, g3), place_ref[c * half + j], NX)
        send[j] = pick((g0, g1, g2, g3), place_ref[(1 - c) * half + j], NX)


def final_kernel(
    place_ref, span_ref, mine, other, u0, u1, u2, u3, b0, b1, b2, b3, bias, cosine, sine, out
):
    c = lax.axis_index("tensor") & 1
    step = pl.program_id(0)
    half, rows, _ = mine.shape
    rank = mine.shape[2] // 2
    per = out.shape[1] // rows
    head = out.shape[2] // 2
    for j in range(per):
        conv = step * per + j
        here = conv & (half - 1)
        act = jnp.where((conv >> 3) == c, mine[here], other[here])
        up = pick((u0, u1, u2, u3), place_ref[conv], NX)
        key_delta = jnp.dot(act[:, :rank], up[:rank], preferred_element_type=F32).astype(BF)
        value_delta = jnp.dot(act[:, rank:], up[rank:], preferred_element_type=F32).astype(BF)
        spot = pl.ds(j * rows, rows)
        base = b0[spot].astype(F32) + b1[spot].astype(F32)
        base = base + b2[spot].astype(F32) + b3[spot].astype(F32)
        base = base + bias[0:1].astype(F32)
        key = base[:, :head] + key_delta.astype(F32)
        value = base[:, head:] + value_delta.astype(F32)
        key = key * cosine[spot] + pltpu.roll(key, head // 2, 1) * sine[spot]
        live = lax.broadcasted_iota(jnp.int32, (rows, head), 0) < span_ref[conv]
        out[0, spot, :head] = jnp.where(live, key, 0.0).astype(BF)
        out[0, spot, head:] = jnp.where(live, value, 0.0).astype(BF)


VMEM_SPEC = pl.BlockSpec(memory_space=pltpu.VMEM)
ANY_SPEC = pl.BlockSpec(memory_space=pl.ANY)
SMEM_SPEC = pl.BlockSpec(memory_space=pltpu.SMEM)


def body(
    tokens,
    key_value_weight,
    key_value_bias,
    adapter_down_weight,
    adapter_up_weight,
    conversation_adapter,
    adapter_slot_table,
    span_length,
    context_length,
):
    convs = span_length.shape[0]
    total, depth = tokens.shape
    rows = total // convs
    heads, width = key_value_weight.shape[1:]
    head = width // 2
    double_rank = adapter_down_weight.shape[2]
    t = lax.axis_index("tensor")
    y, c = t // NC, t % NC
    half = convs // 2

    slots = jax.ShapeDtypeStruct((NZ, rows, depth), BF)
    packed = pl.pallas_call(
        pack_kernel,
        out_shape=[slots] * NX,
        in_specs=[SMEM_SPEC, SMEM_SPEC, ANY_SPEC],
        out_specs=[ANY_SPEC] * NX,
        scratch_shapes=[pltpu.SemaphoreType.DMA],
        name="pack",
    )(conversation_adapter, adapter_slot_table, tokens.reshape(convs, rows, depth))
    got = [packed[0]] + [shift_x(packed[r], r) for r in range(1, NX)]

    stack = jnp.concatenate(
        [
            adapter_down_weight,
            adapter_up_weight.reshape(adapter_up_weight.shape[0], double_rank, head),
        ],
        axis=1,
    )
    f1, b1 = shift_z(stack, 1), shift_z(stack, -1)
    f2, b2 = shift_z(f1, 1), shift_z(b1, -1)
    f3, b3 = shift_z(f2, 1), shift_z(b2, -1)
    f4, b4 = shift_z(f3[0], 1), shift_z(b3[1], -1)
    stacks = [stack, b1, b2, b3, f4, f3, f2, f1, b4]

    choice, place = pl.pallas_call(
        plan_kernel,
        out_shape=[
            jax.ShapeDtypeStruct((NX * NZ,), jnp.int32),
            jax.ShapeDtypeStruct((convs,), jnp.int32),
        ],
        in_specs=[SMEM_SPEC, SMEM_SPEC],
        out_specs=[SMEM_SPEC, SMEM_SPEC],
        name="plan",
    )(conversation_adapter, adapter_slot_table)

    part = jnp.einsum("td,dhe->hte", tokens, key_value_weight, preferred_element_type=F32)
    part = part.astype(BF).reshape(NY, NC, total, width)
    keep = lax.dynamic_index_in_dim(part, c, 1, keepdims=False)
    send = lax.dynamic_index_in_dim(part, 1 - c, 1, keepdims=False)
    pair = (keep.astype(F32) + swap_core(send).astype(F32)).astype(BF)
    bases = [lax.dynamic_index_in_dim(pair, y, 0, keepdims=False)]
    for s in range(1, NY):
        bases.append(shift_y(lax.dynamic_index_in_dim(pair, (y + s) % NY, 0, keepdims=False), s))

    positions = (
        (context_length[:, None] + jnp.arange(rows, dtype=jnp.int32)[None, :])
        .reshape(-1)
        .astype(F32)
    )
    inverse_freq = jnp.exp(
        jnp.arange(head // 2, dtype=F32) * (-2.0 * math.log(rope_base) / head)
    )
    angles = positions[:, None] * inverse_freq[None, :]
    cosine, sine = jnp.cos(angles), jnp.sin(angles)
    cosine = jnp.concatenate([cosine, cosine], axis=-1)
    sine = jnp.concatenate([-sine, sine], axis=-1)

    small = jax.ShapeDtypeStruct((NZ, rows, double_rank), BF)
    blocks = jax.ShapeDtypeStruct((NZ, double_rank, head), BF)
    results = pl.pallas_call(
        rank_kernel,
        out_shape=[small] * NX + [blocks] * NX,
        in_specs=[SMEM_SPEC] + [VMEM_SPEC] * 13,
        out_specs=[VMEM_SPEC] * 8,
        compiler_params=pltpu.CompilerParams(vmem_limit_bytes=40 * 1024 * 1024),
        name="rank",
    )(choice, *got, *stacks)
    ranks, ups = results[:NX], results[NX:]
    back = [ranks[0]] + [shift_x(ranks[r], -r) for r in range(1, NX)]

    kept = jax.ShapeDtypeStruct((half, rows, double_rank), BF)
    keep_r, send_r = pl.pallas_call(
        unslot_kernel,
        out_shape=[kept, kept],
        in_specs=[SMEM_SPEC] + [VMEM_SPEC] * 4,
        out_specs=[VMEM_SPEC] * 2,
        name="unslot",
    )(place, *back)
    mine = (keep_r.astype(F32) + swap_core(send_r).astype(F32)).astype(BF)
    others = [shift_y(mine, s) for s in range(1, NY)]
    total_rank = mine.astype(F32)
    for o in others:
        total_rank = total_rank + o.astype(F32)
    mine = total_rank.astype(BF)
    other = swap_core(mine)
    ups_late = lax.optimization_barrier((back, list(ups)))[1]
    up_back = [ups_late[0]] + [shift_x(ups_late[r], -r) for r in range(1, NX)]

    steps = 4
    base_spec = pl.BlockSpec((total // steps, width), lambda i, *_: (i, 0))
    trig_spec = pl.BlockSpec((total // steps, head), lambda i, *_: (i, 0))
    full = lambda a: pl.BlockSpec(a.shape, lambda i, *_: (0,) * a.ndim)
    return pl.pallas_call(
        final_kernel,
        out_shape=jax.ShapeDtypeStruct((1, total, width), BF),
        grid_spec=pltpu.PrefetchScalarGridSpec(
            num_scalar_prefetch=2,
            grid=(steps,),
            in_specs=[full(mine), full(other)]
            + [full(u) for u in up_back]
            + [base_spec] * 4
            + [full(key_value_bias), trig_spec, trig_spec],
            out_specs=pl.BlockSpec((1, total // steps, width), lambda i, *_: (0, i, 0)),
        ),
        name="final",
    )(place, span_length, mine, other, *up_back, *bases, key_value_bias, cosine, sine)


def solution(mesh):
    placed = (
        P("dp", "tensor"),
        P("tensor", None, None),
        P("tensor", None),
        P("dp", "tensor", None),
        P("dp", "tensor", None, None, None),
        P(),
        P(),
        P("dp"),
        P("dp"),
    )
    return jax.shard_map(
        body, mesh=mesh, in_specs=placed, out_specs=P("tensor", "dp", None), check_vma=False
    )
```

time: 363 us -> 242 us (0.67)
  waiting for transfers between devices: 266 us -> 92 us
  Pallas kernels: 0 us -> 78.6 us
  matrix products: 30.1 us -> 7.84 us
  between operations: 13.6 us -> 0.24 us
  starting transfers between devices: 28 us -> 35.7 us
    all_to_all x2 -> x0, waiting for transfers between devices: 213 us -> none  [the longest x1 187 us: body(): lax.all_to_all(down_out, 'dp', split_axis=0, concat_axis=0, tiled=True)]
    ppermute x0 -> x26, waiting for transfers between devices: none -> 92 us  [the longest x9 51.7 us: shift_x(): return lax.ppermute(v, 'dp', pairs)]
    pallas_call x0 -> x5, Pallas kernels: none -> 78.6 us  [the longest x1 65.4 us: body(): pl.pallas_call(pack_kernel, out_shape=[slots] * NX, in_specs=[SMEM_SPEC,...]
    reduce_scatter x1 -> x0, waiting for transfers between devices: 35.8 us -> none  [body(): lax.psum_scatter(jnp.einsum('td,dhe->hte', tokens, key_value_weight, pref...]
    ppermute x0 -> x26, starting transfers between devices: none -> 35.7 us  [the longest x8 12.5 us: shift_z(): return lax.ppermute(v, 'dp', pairs)]
    all_to_all x2 -> x0, starting transfers between devices: 27.7 us -> none  [the longest x1 15.7 us: body(): lax.all_to_all(up_out, 'dp', split_axis=0, concat_axis=0, tiled=True)]
    dot_general x6 -> x0, matrix products: 21 us -> none  [the longest x1 8.43 us: body(): jnp.einsum('co,odk->cdk', routing, down_got, preferred_element_type=jnp.f...]
    psum x1 -> x0, waiting for transfers between devices: 17.2 us -> none  [body(): rank_sum = lax.psum(rank_part.astype(jnp.bfloat16), 'tensor')]
  transfers between devices with their start and end apart: 4 -> 26, of which waited for: 4 -> 12; matrix products, arithmetic and copies ran while one was open for 5% -> 10% of each run, Pallas kernels for 0% -> 30%
where the time goes in v1:
time: 242 us; the launch traced here: 241 us
  waiting for transfers between devices  92 us (38%)
  Pallas kernels  78.6 us (32%)
  starting transfers between devices  35.7 us (15%)
  local copies, waits for them, and re-layouts  20.1 us (8%)
  matrix products  7.84 us (3%)
  other arithmetic  6.6 us (3%)
    pallas_call x1, Pallas kernels, body(): pl.pallas_call(pack_kernel, out_shape=[slots] * NX, in_specs=[SMEM_SPEC,...  65.4 us
    ppermute x9, waiting for transfers between devices, shift_x(): return lax.ppermute(v, 'dp', pairs)  51.7 us
    ppermute x6, waiting for transfers between devices, shift_y(): return lax.ppermute(v, 'tensor', pairs)  23 us
    ppermute x8, waiting for transfers between devices, shift_z(): return lax.ppermute(v, 'dp', pairs)  17.3 us
    ppermute x8, starting transfers between devices, shift_z(): return lax.ppermute(v, 'dp', pairs)  12.5 us
    unnamed x51, local copies, waits for them, and re-layouts  11.1 us
    ppermute x9, starting transfers between devices, shift_x(): return lax.ppermute(v, 'dp', pairs)  10.6 us
    ppermute x6, starting transfers between devices, shift_y(): return lax.ppermute(v, 'tensor', pairs)  8.53 us
  transfers between devices with their start and end apart: 26, of which 12 were waited for; matrix products, arithmetic and copies ran while one was open for 10% of the time, Pallas kernels for 30%

profile of v1, /device:TPU:1, one launch (start us, length us, event | category | flops | bytes accessed | tf_op | source)
XLA Modules:
  0.0 241.1 jit_solution(18180841163291459152)
XLA Ops:
  0.0 1.1 pad_maximum_fusion.refs_4_
  1.1 2.5 %collective-permute-start.6 = (bf16[2,1152,128]{2,1,0:T(8,128)(2,1)S(1)}, bf16[2,1152,128]{2,1,0:T(8,128)(2,1)S(1)}, u32[]{:S(2)}, u32[]{:S(2)}) collective-permute-start(bf16[2,1152,128]{2,1,0:T(8,128)(2,1)S(1)} %pad_maximum_fusion.refs_4_), channel_id=1, source_target_pairs={{0,32},{8,40},{16,48},{24,56},{32,64},{40,72},{48,80},{56,88},{64,... | collective-permute-start | bytes 1769480 | tf_op jit(solution)/shard_map/ppermute | solution.py:24
  3.7 4.0 %collective-permute-start.3 = (bf16[2,1152,128]{2,1,0:T(8,128)(2,1)S(1)}, bf16[2,1152,128]{2,1,0:T(8,128)(2,1)S(1)}, u32[]{:S(2)}, u32[]{:S(2)}) collective-permute-start(bf16[2,1152,128]{2,1,0:T(8,128)(2,1)S(1)} %pad_maximum_fusion.refs_4_), channel_id=1, source_target_pairs={{0,224},{8,232},{16,240},{24,248},{32,0},{40,8},{48,16},{56,24},{6... | collective-permute-start | bytes 1769480 | tf_op jit(solution)/shard_map/ppermute | solution.py:24
  7.7 13.0 %collective-permute-done.6.refs_11_ = bf16[2,1152,128]{2,1,0:T(8,128)(2,1)S(1)} collective-permute-done((bf16[2,1152,128]{2,1,0:T(8,128)(2,1)S(1)}, bf16[2,1152,128]{2,1,0:T(8,128)(2,1)S(1)}, u32[]{:S(2)}, u32[]{:S(2)}) %collective-permute-start.6) | collective-permute-done | bytes 589856 | tf_op jit(solution)/shard_map/ppermute | solution.py:24
  20.7 7.8 %fusion.3 = bf16[8,256,1024]{2,1,0:T(8,128)(2,1)S(1)} fusion(bf16[1024,8,256]{2,1,0:T(8,128)(2,1)} %param.10, bf16[1024,1024]{1,0:T(8,128)(2,1)} %param.9), kind=kOutput, calls=%fused_computation.4 | convolution fusion | flops 4297064448 | bytes 10485760 | tf_op jit(solution)/shard_map/td,dhe->hte/dot_general | solution.py:221
  28.5 2.7 %collective-permute-start.4 = (bf16[2,1152,128]{2,1,0:T(8,128)(2,1)S(1)}, bf16[2,1152,128]{2,1,0:T(8,128)(2,1)}, u32[]{:S(2)}, u32[]{:S(2)}) collective-permute-start(bf16[2,1152,128]{2,1,0:T(8,128)(2,1)S(1)} %collective-permute-done.3.refs_5_), channel_id=1, source_target_pairs={{0,224},{8,232},{16,240},{24,248},{32,0},{40,8},{48,16},{56,24},{6... | collective-permute-start | bytes 1769480 | tf_op jit(solution)/shard_map/ppermute | solution.py:24
  31.3 4.3 %collective-permute-done.7.refs_10_ = bf16[2,1152,128]{2,1,0:T(8,128)(2,1)} collective-permute-done((bf16[2,1152,128]{2,1,0:T(8,128)(2,1)S(1)}, bf16[2,1152,128]{2,1,0:T(8,128)(2,1)}, u32[]{:S(2)}, u32[]{:S(2)}) %collective-permute-start.7) | collective-permute-done | bytes 589856 | tf_op jit(solution)/shard_map/ppermute | solution.py:24
  35.6 2.6 %constant_dynamic-slice_fusion.1 = (bf16[4,1,1024,256]{2,3,1,0:T(8,128)(2,1)}, bf16[4,1,1024,256]{2,3,1,0:T(8,128)(2,1)}) fusion(bf16[4,2,1024,256]{2,3,1,0:T(8,128)(2,1)S(1)} %bitcast.24, s32[]{:T(128)S(6)} %select_n.44, s32[]{:T(128)S(6)} %select_n.45), kind=kLoop, calls=%fused_computation.22 | loop fusion | bytes 8388616 | tf_op jit(solution)/shard_map/jit(dynamic_index_in_dim)/dynamic_slice | solution.py:223
  38.1 4.0 %copy.12 = bf16[4,1,1024,256]{3,2,0,1:T(8,128)(2,1)} copy(bf16[4,1,1024,256]{2,3,1,0:T(8,128)(2,1)} %get-tuple-element.46) | data formatting | bytes 4194304 | tf_op jit(solution)/shard_map/jit(dynamic_index_in_dim)/dynamic_slice | solution.py:224
  42.1 2.1 collective-permute-start.22
  44.3 2.9 %collective-permute-start.5 = (bf16[2,1152,128]{2,1,0:T(8,128)(2,1)}, bf16[2,1152,128]{2,1,0:T(8,128)(2,1)S(1)}, u32[]{:S(2)}, u32[]{:S(2)}) collective-permute-start(bf16[2,1152,128]{2,1,0:T(8,128)(2,1)} %collective-permute-done.4.refs_6_), channel_id=1, source_target_pairs={{0,224},{8,232},{16,240},{24,248},{32,0},{40,8},{48,16},{56,24},{6... | collective-permute-start | bytes 1769480 | tf_op jit(solution)/shard_map/ppermute | solution.py:24
  47.2 65.4 %pack.1 = (bf16[8,64,1024]{2,1,0:T(8,128)(2,1)}, bf16[8,64,1024]{2,1,0:T(8,128)(2,1)}, bf16[8,64,1024]{2,1,0:T(8,128)(2,1)}, bf16[8,64,1024]{2,1,0:T(8,128)(2,1)}) custom-call(s32[512]{0:T(512)} %ca_ref.3, s32[64]{0:T(128)} %table_ref.3, bf16[16,64,1024]{2,1,0:T(8,128)(2,1)} %bitcast.25), custom_call_target="tpu_custom_call" | custom-call | tf_op jit(solution)/shard_map/pack/pallas_call | solution.py:187
  112.6 1.3 collective-permute-start
  113.8 2.5 %collective-permute-start.1 = (bf16[8,64,1024]{2,1,0:T(8,128)(2,1)}, bf16[8,64,1024]{2,1,0:T(8,128)(2,1)}, u32[]{:S(2)}, u32[]{:S(2)}) collective-permute-start(bf16[8,64,1024]{2,1,0:T(8,128)(2,1)} %get-tuple-element.29), channel_id=1, source_target_pairs={{0,16},{8,24},{16,0},{24,8},{32,48},{40,56},{48,32},{56,40},{64,80... | collective-permute-start | bytes 3145736 | tf_op jit(solution)/shard_map/ppermute | solution.py:19
  116.3 1.2 collective-permute-start.2
  117.5 0.7 slice_bitcast_fusion.1
  118.2 0.7 slice_bitcast_fusion
  118.9 18.4 %collective-permute-done.refs_1_ = bf16[8,64,1024]{2,1,0:T(8,128)(2,1)S(1)} collective-permute-done((bf16[8,64,1024]{2,1,0:T(8,128)(2,1)}, bf16[8,64,1024]{2,1,0:T(8,128)(2,1)S(1)}, u32[]{:S(2)}, u32[]{:S(2)}) %collective-permute-start) | collective-permute-done | bytes 1048608 | tf_op jit(solution)/shard_map/ppermute | solution.py:19
  137.6 1.9 plan.1
  139.5 21.4 %collective-permute-done.1.refs_2_ = bf16[8,64,1024]{2,1,0:T(8,128)(2,1)} collective-permute-done((bf16[8,64,1024]{2,1,0:T(8,128)(2,1)}, bf16[8,64,1024]{2,1,0:T(8,128)(2,1)}, u32[]{:S(2)}, u32[]{:S(2)}) %collective-permute-start.1) | collective-permute-done | bytes 1048608 | tf_op jit(solution)/shard_map/ppermute | solution.py:19
  161.4 1.2 copy-done
  162.6 1.1 copy-done.2
  164.3 4.0 %rank.1 = (bf16[8,64,128]{2,1,0:T(8,128)(2,1)S(1)}, bf16[8,64,128]{2,1,0:T(8,128)(2,1)}, bf16[8,64,128]{2,1,0:T(8,128)(2,1)}, bf16[8,64,128]{2,1,0:T(8,128)(2,1)...) custom-call(s32[32]{0:T(128)S(1)} %copy-done.5, ...), custom_call_target="tpu_custom_call" | custom-call | tf_op jit(solution)/shard_map/rank/pallas_call | solution.py:245
  168.3 0.7 copy-done.3
  169.6 0.7 copy-done.6
  170.3 0.7 copy-done.8
  171.0 0.7 copy-done.10
  171.7 3.4 %collective-permute-start.11 = (bf16[8,64,128]{2,1,0:T(8,128)(2,1)}, bf16[8,64,128]{2,1,0:T(8,128)(2,1)S(1)}, u32[]{:S(2)}, u32[]{:S(2)}) collective-permute-start(bf16[8,64,128]{2,1,0:T(8,128)(2,1)} %get-tuple-element.32), channel_id=1, source_target_pairs={{0,24},{8,0},{16,8},{24,16},{32,56},{40,32},{48,40},{56,48},{64,88... | collective-permute-start | bytes 393224 | tf_op jit(solution)/shard_map/ppermute | solution.py:19
  175.8 2.9 %copy.13 = bf16[4,1,1024,256]{3,2,0,1:T(8,128)(2,1)S(1)} copy(bf16[4,1,1024,256]{2,3,1,0:T(8,128)(2,1)} %get-tuple-element.45) | data formatting | bytes 4194304
  178.7 2.1 collective-permute-done.11.g1
  181.2 3.2 %collective-permute-done.13.g3 = bf16[8,64,128]{2,1,0:T(8,128)(2,1)S(1)} collective-permute-done((bf16[8,64,128]{2,1,0:T(8,128)(2,1)S(1)}, bf16[8,64,128]{2,1,0:T(8,128)(2,1)S(1)}, u32[]{:S(2)}, u32[]{:S(2)}) %collective-permute-start.13) | collective-permute-done | bytes 131104 | tf_op jit(solution)/shard_map/ppermute | solution.py:19
  185.0 2.0 unslot.1
  187.0 1.0 collective-permute-start.14
  188.0 2.1 fusion
  190.1 0.7 collective-permute-start.19
  190.8 2.8 %collective-permute-start.17 = (bf16[8,64,128]{2,1,0:T(8,128)(2,1)S(1)}, bf16[8,64,128]{2,1,0:T(8,128)(2,1)S(1)}, u32[]{:S(2)}, u32[]{:S(2)}) collective-permute-start(bf16[8,64,128]{2,1,0:T(8,128)(2,1)S(1)} %add_convert_fusion.1), channel_id=1, source_target_pairs={{0,6},{1,7},{2,0},{3,1},{4,2},{5,3},{6,4},{7,5},{8,14},{9,15},{10,... | collective-permute-start | bytes 393224 | tf_op jit(solution)/shard_map/ppermute | solution.py:29
  194.0 0.9 dynamic-slice_bitcast_fusion
  194.9 0.7 collective-permute-start.23
  195.6 1.9 collective-permute-start.24
  198.0 2.7 %collective-permute-start.25 = (bf16[1024,256]{1,0:T(8,128)(2,1)S(1)}, bf16[1024,256]{1,0:T(8,128)(2,1)S(1)}, u32[]{:S(2)}, u32[]{:S(2)}) collective-permute-start(bf16[1024,256]{1,0:T(8,128)(2,1)S(1)} %get-tuple-element.47), channel_id=1, source_target_pairs={{0,6},{1,7},{2,0},{3,1},{4,2},{5,3},{6,4},{7,5},{8,14},{9,15},{10,... | collective-permute-start | bytes 1572872 | tf_op jit(solution)/shard_map/ppermute | solution.py:29
  200.8 7.8 %collective-permute-done.17 = bf16[8,64,128]{2,1,0:T(8,128)(2,1)S(1)} collective-permute-done((bf16[8,64,128]{2,1,0:T(8,128)(2,1)S(1)}, bf16[8,64,128]{2,1,0:T(8,128)(2,1)S(1)}, u32[]{:S(2)}, u32[]{:S(2)}) %collective-permute-start.17) | collective-permute-done | bytes 131104 | tf_op jit(solution)/shard_map/ppermute | solution.py:29
  208.8 1.9 fusion.7
  210.7 15.2 %collective-permute-done.15 = bf16[8,64,128]{2,1,0:T(8,128)(2,1)S(1)} collective-permute-done((bf16[8,64,128]{2,1,0:T(8,128)(2,1)S(1)}, bf16[8,64,128]{2,1,0:T(8,128)(2,1)S(1)}, u32[]{:S(2)}, u32[]{:S(2)}) %collective-permute-start.15) | collective-permute-done | bytes 131104 | tf_op jit(solution)/shard_map/ppermute | solution.py:29
  225.9 0.8 collective-permute-start.21
  226.8 0.9 collective-permute-start.18
  227.7 1.3 pad_maximum_fusion.1
  229.0 5.5 %collective-permute-done.21.u3 = bf16[8,128,128]{2,1,0:T(8,128)(2,1)S(1)} collective-permute-done((bf16[8,128,128]{2,1,0:T(8,128)(2,1)S(1)}, bf16[8,128,128]{2,1,0:T(8,128)(2,1)S(1)}, u32[]{:S(2)}, u32[]{:S(2)}) %collective-permute-start.21) | collective-permute-done | bytes 262176 | tf_op jit(solution)/shard_map/ppermute | solution.py:19
  235.7 5.4 %final.1 = bf16[1,1024,256]{2,1,0:T(8,128)(2,1)} custom-call(s32[16]{0:T(128)} %get-tuple-element.25.place_ref, s32[16]{0:T(128)} %span_ref.1, bf16[8,64,128]{2,1,0:T(8,128)(2,1)} %copy-done.15, bf16[8,64,128]{2,1,0:T(8,128)(2,1)} %copy-done.22, bf16[8,128,128]{2,1,0:T(8,128)(2,1)} %copy-done.3, bf16[8,128,128]{2,1,0:T(8,128)(2,1)} %copy-done.16, ...), custom_call_target="tpu_custom_call" | custom-call | tf_op jit(solution)/shard_map/final/pallas_call | solution.py:278
  (75 shorter events, 6.2 us)
Async XLA Ops:
  1.1 19.5 %collective-permute-start.6 = (bf16[2,1152,128]{2,1,0:T(8,128)(2,1)S(1)}, bf16[2,1152,128]{2,1,0:T(8,128)(2,1)S(1)}, u32[]{:S(2)}, u32[]{:S(2)}) collective-permute-start(bf16[2,1152,128]{2,1,0:T(8,128)(2,1)S(1)} %pad_maximum_fusion.refs_4_), channel_id=1, source_target_pairs={{0,32},{8,40},{16,48},{24,56},{32,64},{40,72},{48,80},{56,88},{64,... | collective-permute-start | bytes 1769480 | tf_op jit(solution)/shard_map/ppermute | solution.py:24
  3.7 24.8 %collective-permute-start.3 = (bf16[2,1152,128]{2,1,0:T(8,128)(2,1)S(1)}, bf16[2,1152,128]{2,1,0:T(8,128)(2,1)S(1)}, u32[]{:S(2)}, u32[]{:S(2)}) collective-permute-start(bf16[2,1152,128]{2,1,0:T(8,128)(2,1)S(1)} %pad_maximum_fusion.refs_4_), channel_id=1, source_target_pairs={{0,224},{8,232},{16,240},{24,248},{32,0},{40,8},{48,16},{56,24},{6... | collective-permute-start | bytes 1769480 | tf_op jit(solution)/shard_map/ppermute | solution.py:24
  20.7 14.9 %collective-permute-start.7 = (bf16[2,1152,128]{2,1,0:T(8,128)(2,1)S(1)}, bf16[2,1152,128]{2,1,0:T(8,128)(2,1)}, u32[]{:S(2)}, u32[]{:S(2)}) collective-permute-start(bf16[2,1152,128]{2,1,0:T(8,128)(2,1)S(1)} %collective-permute-done.6.refs_11_), channel_id=1, source_target_pairs={{0,32},{8,40},{16,48},{24,56},{32,64},{40,72},{48,80},{56,88},{64,... | collective-permute-start | bytes 1769480 | tf_op jit(solution)/shard_map/ppermute | solution.py:24
  28.5 9.6 %copy-start.1 = (bf16[2,1152,128]{2,1,0:T(8,128)(2,1)}, bf16[2,1152,128]{2,1,0:T(8,128)(2,1)S(1)}, u32[]{:S(2)}) copy-start(bf16[2,1152,128]{2,1,0:T(8,128)(2,1)S(1)} %collective-permute-done.3.refs_5_) | copy-start | bytes 1769476
  28.5 15.7 %collective-permute-start.4 = (bf16[2,1152,128]{2,1,0:T(8,128)(2,1)S(1)}, bf16[2,1152,128]{2,1,0:T(8,128)(2,1)}, u32[]{:S(2)}, u32[]{:S(2)}) collective-permute-start(bf16[2,1152,128]{2,1,0:T(8,128)(2,1)S(1)} %collective-permute-done.3.refs_5_), channel_id=1, source_target_pairs={{0,224},{8,232},{16,240},{24,248},{32,0},{40,8},{48,16},{56,24},{6... | collective-permute-start | bytes 1769480 | tf_op jit(solution)/shard_map/ppermute | solution.py:24
  35.6 80.7 %collective-permute-start.8 = (bf16[2,1152,128]{2,1,0:T(8,128)(2,1)}, bf16[2,1152,128]{2,1,0:T(8,128)(2,1)S(1)}, u32[]{:S(2)}, u32[]{:S(2)}) collective-permute-start(bf16[2,1152,128]{2,1,0:T(8,128)(2,1)} %collective-permute-done.7.refs_10_), channel_id=1, source_target_pairs={{0,32},{8,40},{16,48},{24,56},{32,64},{40,72},{48,80},{56,88},{64,... | collective-permute-start | bytes 1769480 | tf_op jit(solution)/shard_map/ppermute | solution.py:24
  42.1 145.9 %collective-permute-start.22 = (bf16[4,1024,256]{2,1,0:T(8,128)(2,1)}, bf16[4,1024,256]{2,1,0:T(8,128)(2,1)}, u32[]{:S(2)}, u32[]{:S(2)}) collective-permute-start(bf16[4,1024,256]{2,1,0:T(8,128)(2,1)} %bitcast.26), channel_id=1, source_target_pairs={{0,1},{1,0},{2,3},{3,2},{4,5},{5,4},{6,7},{7,6},{8,9},{9,8},{10,11... | collective-permute-start | bytes 6291464 | tf_op jit(solution)/shard_map/ppermute | solution.py:33
  44.3 73.9 %collective-permute-start.5 = (bf16[2,1152,128]{2,1,0:T(8,128)(2,1)}, bf16[2,1152,128]{2,1,0:T(8,128)(2,1)S(1)}, u32[]{:S(2)}, u32[]{:S(2)}) collective-permute-start(bf16[2,1152,128]{2,1,0:T(8,128)(2,1)} %collective-permute-done.4.refs_6_), channel_id=1, source_target_pairs={{0,224},{8,232},{16,240},{24,248},{32,0},{40,8},{48,16},{56,24},{6... | collective-permute-start | bytes 1769480 | tf_op jit(solution)/shard_map/ppermute | solution.py:24
  112.6 24.7 %collective-permute-start = (bf16[8,64,1024]{2,1,0:T(8,128)(2,1)}, bf16[8,64,1024]{2,1,0:T(8,128)(2,1)S(1)}, u32[]{:S(2)}, u32[]{:S(2)}) collective-permute-start(bf16[8,64,1024]{2,1,0:T(8,128)(2,1)} %get-tuple-element.28), channel_id=1, source_target_pairs={{0,8},{8,16},{16,24},{24,0},{32,40},{40,48},{48,56},{56,32},{64,72... | collective-permute-start | bytes 3145736 | tf_op jit(solution)/shard_map/ppermute | solution.py:19
  113.8 47.0 %collective-permute-start.1 = (bf16[8,64,1024]{2,1,0:T(8,128)(2,1)}, bf16[8,64,1024]{2,1,0:T(8,128)(2,1)}, u32[]{:S(2)}, u32[]{:S(2)}) collective-permute-start(bf16[8,64,1024]{2,1,0:T(8,128)(2,1)} %get-tuple-element.29), channel_id=1, source_target_pairs={{0,16},{8,24},{16,0},{24,8},{32,48},{40,56},{48,32},{56,40},{64,80... | collective-permute-start | bytes 3145736 | tf_op jit(solution)/shard_map/ppermute | solution.py:19
  116.3 45.1 %collective-permute-start.2 = (bf16[8,64,1024]{2,1,0:T(8,128)(2,1)}, bf16[8,64,1024]{2,1,0:T(8,128)(2,1)}, u32[]{:S(2)}, u32[]{:S(2)}) collective-permute-start(bf16[8,64,1024]{2,1,0:T(8,128)(2,1)} %get-tuple-element.30), channel_id=1, source_target_pairs={{0,24},{8,0},{16,8},{24,16},{32,56},{40,32},{48,40},{56,48},{64,88... | collective-permute-start | bytes 3145736 | tf_op jit(solution)/shard_map/ppermute | solution.py:19
  118.2 43.2 %collective-permute-start.9 = (bf16[1152,128]{1,0:T(8,128)(2,1)}, bf16[1152,128]{1,0:T(8,128)(2,1)}, u32[]{:S(2)}, u32[]{:S(2)}) collective-permute-start(bf16[1152,128]{1,0:T(8,128)(2,1)} %slice_bitcast_fusion.1), channel_id=1, source_target_pairs={{0,32},{8,40},{16,48},{24,56},{32,64},{40,72},{48,80},{56,88},{64,... | collective-permute-start | bytes 884744 | tf_op jit(solution)/shard_map/ppermute | solution.py:24
  137.3 24.1 %collective-permute-start.10 = (bf16[1152,128]{1,0:T(8,128)(2,1)}, bf16[1152,128]{1,0:T(8,128)(2,1)}, u32[]{:S(2)}, u32[]{:S(2)}) collective-permute-start(bf16[1152,128]{1,0:T(8,128)(2,1)} %slice_bitcast_fusion), channel_id=1, source_target_pairs={{0,224},{8,232},{16,240},{24,248},{32,0},{40,8},{48,16},{56,24},{6... | collective-permute-start | bytes 884744 | tf_op jit(solution)/shard_map/ppermute | solution.py:24
  161.4 1.2 copy-start
  162.6 1.1 copy-start.2
  164.3 11.4 %copy-start.24 = (s32[16]{0:T(128)S(1)}, s32[16]{0:T(128)}, u32[]{:S(2)}) copy-start(s32[16]{0:T(128)} %param.17) | copy-start | bytes 196
  168.3 0.7 copy-start.3
  169.6 0.7 copy-start.6
  170.3 0.7 copy-start.8
  171.0 0.7 copy-start.10
  171.7 9.1 %collective-permute-start.11 = (bf16[8,64,128]{2,1,0:T(8,128)(2,1)}, bf16[8,64,128]{2,1,0:T(8,128)(2,1)S(1)}, u32[]{:S(2)}, u32[]{:S(2)}) collective-permute-start(bf16[8,64,128]{2,1,0:T(8,128)(2,1)} %get-tuple-element.32), channel_id=1, source_target_pairs={{0,24},{8,0},{16,8},{24,16},{32,56},{40,32},{48,40},{56,48},{64,88... | collective-permute-start | bytes 393224 | tf_op jit(solution)/shard_map/ppermute | solution.py:19
  175.1 6.1 %collective-permute-start.12 = (bf16[8,64,128]{2,1,0:T(8,128)(2,1)}, bf16[8,64,128]{2,1,0:T(8,128)(2,1)S(1)}, u32[]{:S(2)}, u32[]{:S(2)}) collective-permute-start(bf16[8,64,128]{2,1,0:T(8,128)(2,1)} %get-tuple-element.33), channel_id=1, source_target_pairs={{0,16},{8,24},{16,0},{24,8},{32,48},{40,56},{48,32},{56,40},{64,80... | collective-permute-start | bytes 393224 | tf_op jit(solution)/shard_map/ppermute | solution.py:19
  175.3 9.0 %collective-permute-start.13 = (bf16[8,64,128]{2,1,0:T(8,128)(2,1)S(1)}, bf16[8,64,128]{2,1,0:T(8,128)(2,1)S(1)}, u32[]{:S(2)}, u32[]{:S(2)}) collective-permute-start(bf16[8,64,128]{2,1,0:T(8,128)(2,1)S(1)} %get-tuple-element.34), channel_id=1, source_target_pairs={{0,8},{8,16},{16,24},{24,0},{32,40},{40,48},{48,56},{56,32},{64,72... | collective-permute-start | bytes 393224 | tf_op jit(solution)/shard_map/ppermute | solution.py:19
  180.8 3.6 %copy-start.19 = (bf16[8,64,128]{2,1,0:T(8,128)(2,1)}, bf16[8,64,128]{2,1,0:T(8,128)(2,1)S(1)}, u32[]{:S(2)}) copy-start(bf16[8,64,128]{2,1,0:T(8,128)(2,1)S(1)} %collective-permute-done.11.g1) | copy-start | bytes 393220
  181.2 3.2 %copy-start.20 = (bf16[8,64,128]{2,1,0:T(8,128)(2,1)}, bf16[8,64,128]{2,1,0:T(8,128)(2,1)S(1)}, u32[]{:S(2)}) copy-start(bf16[8,64,128]{2,1,0:T(8,128)(2,1)S(1)} %collective-permute-done.12.g2) | copy-start | bytes 393220
  187.0 3.1 %copy-start.11 = (bf16[8,128,128]{2,1,0:T(8,128)(2,1)S(1)}, bf16[8,128,128]{2,1,0:T(8,128)(2,1)}, u32[]{:S(2)}) copy-start(bf16[8,128,128]{2,1,0:T(8,128)(2,1)} %copy-done.10) | copy-start | bytes 786436
  187.0 3.8 %copy-start.23 = (bf16[8,64,128]{2,1,0:T(8,128)(2,1)S(1)}, bf16[8,64,128]{2,1,0:T(8,128)(2,1)}, u32[]{:S(2)}) copy-start(bf16[8,64,128]{2,1,0:T(8,128)(2,1)} %get-tuple-element.35) | copy-start | bytes 393220
  187.0 3.8 %collective-permute-start.14 = (bf16[8,64,128]{2,1,0:T(8,128)(2,1)}, bf16[8,64,128]{2,1,0:T(8,128)(2,1)S(1)}, u32[]{:S(2)}, u32[]{:S(2)}) collective-permute-start(bf16[8,64,128]{2,1,0:T(8,128)(2,1)} %get-tuple-element.36), channel_id=1, source_target_pairs={{0,1},{1,0},{2,3},{3,2},{4,5},{5,4},{6,7},{7,6},{8,9},{9,8},{10,11... | collective-permute-start | bytes 393224 | tf_op jit(solution)/shard_map/ppermute | solution.py:33
  190.1 8.0 %collective-permute-start.19 = (bf16[8,128,128]{2,1,0:T(8,128)(2,1)S(1)}, bf16[8,128,128]{2,1,0:T(8,128)(2,1)S(1)}, u32[]{:S(2)}, u32[]{:S(2)}) collective-permute-start(bf16[8,128,128]{2,1,0:T(8,128)(2,1)S(1)} %copy-done.11), channel_id=1, source_target_pairs={{0,24},{8,0},{16,8},{24,16},{32,56},{40,32},{48,40},{56,48},{64,88... | collective-permute-start | bytes 786440 | tf_op jit(solution)/shard_map/ppermute | solution.py:19
  190.8 17.8 %copy-start.9 = (bf16[8,128,128]{2,1,0:T(8,128)(2,1)S(1)}, bf16[8,128,128]{2,1,0:T(8,128)(2,1)}, u32[]{:S(2)}) copy-start(bf16[8,128,128]{2,1,0:T(8,128)(2,1)} %copy-done.8) | copy-start | bytes 786436
  190.8 35.0 %copy-start.7 = (bf16[8,128,128]{2,1,0:T(8,128)(2,1)S(1)}, bf16[8,128,128]{2,1,0:T(8,128)(2,1)}, u32[]{:S(2)}) copy-start(bf16[8,128,128]{2,1,0:T(8,128)(2,1)} %copy-done.6) | copy-start | bytes 786436
  190.8 17.8 %collective-permute-start.17 = (bf16[8,64,128]{2,1,0:T(8,128)(2,1)S(1)}, bf16[8,64,128]{2,1,0:T(8,128)(2,1)S(1)}, u32[]{:S(2)}, u32[]{:S(2)}) collective-permute-start(bf16[8,64,128]{2,1,0:T(8,128)(2,1)S(1)} %add_convert_fusion.1), channel_id=1, source_target_pairs={{0,6},{1,7},{2,0},{3,1},{4,2},{5,3},{6,4},{7,5},{8,14},{9,15},{10,... | collective-permute-start | bytes 393224 | tf_op jit(solution)/shard_map/ppermute | solution.py:29
  193.7 15.1 %collective-permute-start.16 = (bf16[8,64,128]{2,1,0:T(8,128)(2,1)S(1)}, bf16[8,64,128]{2,1,0:T(8,128)(2,1)S(1)}, u32[]{:S(2)}, u32[]{:S(2)}) collective-permute-start(bf16[8,64,128]{2,1,0:T(8,128)(2,1)S(1)} %add_convert_fusion.1), channel_id=1, source_target_pairs={{0,4},{1,5},{2,6},{3,7},{4,0},{5,1},{6,2},{7,3},{8,12},{9,13},{10,... | collective-permute-start | bytes 393224 | tf_op jit(solution)/shard_map/ppermute | solution.py:29
  194.9 39.5 %collective-permute-start.23 = (bf16[1024,256]{1,0:T(8,128)(2,1)S(1)}, bf16[1024,256]{1,0:T(8,128)(2,1)S(1)}, u32[]{:S(2)}, u32[]{:S(2)}) collective-permute-start(bf16[1024,256]{1,0:T(8,128)(2,1)S(1)} %get-tuple-element.49), channel_id=1, source_target_pairs={{0,2},{1,3},{2,4},{3,5},{4,6},{5,7},{6,0},{7,1},{8,10},{9,11},{10,... | collective-permute-start | bytes 1572872 | tf_op jit(solution)/shard_map/ppermute | solution.py:29
  195.6 38.8 %collective-permute-start.24 = (bf16[1024,256]{1,0:T(8,128)(2,1)S(1)}, bf16[1024,256]{1,0:T(8,128)(2,1)S(1)}, u32[]{:S(2)}, u32[]{:S(2)}) collective-permute-start(bf16[1024,256]{1,0:T(8,128)(2,1)S(1)} %get-tuple-element.48), channel_id=1, source_target_pairs={{0,4},{1,5},{2,6},{3,7},{4,0},{5,1},{6,2},{7,3},{8,12},{9,13},{10,... | collective-permute-start | bytes 1572872 | tf_op jit(solution)/shard_map/ppermute | solution.py:29
  198.0 31.0 %copy-start.16 = (bf16[8,128,128]{2,1,0:T(8,128)(2,1)}, bf16[8,128,128]{2,1,0:T(8,128)(2,1)S(1)}, u32[]{:S(2)}) copy-start(bf16[8,128,128]{2,1,0:T(8,128)(2,1)S(1)} %collective-permute-done.19.u1) | copy-start | bytes 786436
  198.0 36.5 %collective-permute-start.25 = (bf16[1024,256]{1,0:T(8,128)(2,1)S(1)}, bf16[1024,256]{1,0:T(8,128)(2,1)S(1)}, u32[]{:S(2)}, u32[]{:S(2)}) collective-permute-start(bf16[1024,256]{1,0:T(8,128)(2,1)S(1)} %get-tuple-element.47), channel_id=1, source_target_pairs={{0,6},{1,7},{2,0},{3,1},{4,2},{5,3},{6,4},{7,5},{8,14},{9,15},{10,... | collective-permute-start | bytes 1572872 | tf_op jit(solution)/shard_map/ppermute | solution.py:29
  208.6 18.2 %collective-permute-start.20 = (bf16[8,128,128]{2,1,0:T(8,128)(2,1)S(1)}, bf16[8,128,128]{2,1,0:T(8,128)(2,1)S(1)}, u32[]{:S(2)}, u32[]{:S(2)}) collective-permute-start(bf16[8,128,128]{2,1,0:T(8,128)(2,1)S(1)} %copy-done.9), channel_id=1, source_target_pairs={{0,16},{8,24},{16,0},{24,8},{32,48},{40,56},{48,32},{56,40},{64,80... | collective-permute-start | bytes 786440 | tf_op jit(solution)/shard_map/ppermute | solution.py:19
  208.8 17.1 %collective-permute-start.15 = (bf16[8,64,128]{2,1,0:T(8,128)(2,1)S(1)}, bf16[8,64,128]{2,1,0:T(8,128)(2,1)S(1)}, u32[]{:S(2)}, u32[]{:S(2)}) collective-permute-start(bf16[8,64,128]{2,1,0:T(8,128)(2,1)S(1)} %add_convert_fusion.1), channel_id=1, source_target_pairs={{0,2},{1,3},{2,4},{3,5},{4,6},{5,7},{6,0},{7,1},{8,10},{9,11},{10,... | collective-permute-start | bytes 393224 | tf_op jit(solution)/shard_map/ppermute | solution.py:29
  225.9 8.6 %collective-permute-start.21 = (bf16[8,128,128]{2,1,0:T(8,128)(2,1)S(1)}, bf16[8,128,128]{2,1,0:T(8,128)(2,1)S(1)}, u32[]{:S(2)}, u32[]{:S(2)}) collective-permute-start(bf16[8,128,128]{2,1,0:T(8,128)(2,1)S(1)} %copy-done.7), channel_id=1, source_target_pairs={{0,8},{8,16},{16,24},{24,0},{32,40},{40,48},{48,56},{56,32},{64,72... | collective-permute-start | bytes 786440 | tf_op jit(solution)/shard_map/ppermute | solution.py:19
  226.8 7.7 %copy-start.15 = (bf16[8,64,128]{2,1,0:T(8,128)(2,1)}, bf16[8,64,128]{2,1,0:T(8,128)(2,1)S(1)}, u32[]{:S(2)}) copy-start(bf16[8,64,128]{2,1,0:T(8,128)(2,1)S(1)} %add_convert_fusion.mine) | copy-start | bytes 393220
  226.8 7.7 %copy-start.17 = (bf16[8,128,128]{2,1,0:T(8,128)(2,1)}, bf16[8,128,128]{2,1,0:T(8,128)(2,1)S(1)}, u32[]{:S(2)}) copy-start(bf16[8,128,128]{2,1,0:T(8,128)(2,1)S(1)} %collective-permute-done.20.u2) | copy-start | bytes 786436
  226.8 7.6 %collective-permute-start.18 = (bf16[8,64,128]{2,1,0:T(8,128)(2,1)S(1)}, bf16[8,64,128]{2,1,0:T(8,128)(2,1)S(1)}, u32[]{:S(2)}, u32[]{:S(2)}) collective-permute-start(bf16[8,64,128]{2,1,0:T(8,128)(2,1)S(1)} %add_convert_fusion.mine), channel_id=1, source_target_pairs={{0,1},{1,0},{2,3},{3,2},{4,5},{5,4},{6,7},{7,6},{8,9},{9,8},{10,11... | collective-permute-start | bytes 393224 | tf_op jit(solution)/shard_map/ppermute | solution.py:33
  234.5 0.7 copy-start.18
  234.5 0.7 copy-start.22
  234.5 1.0 copy-start.12
  234.5 1.1 copy-start.13
  234.5 1.2 copy-start.14
  (3 other events, 1.9 us)

commit v2 on v1

v2 whole, which is shorter than its diff:
```python
import functools
import math

import jax
import jax.numpy as jnp
from jax import lax
from jax.experimental import pallas as pl
from jax.experimental.pallas import tpu as pltpu
from jax.sharding import PartitionSpec as P

rope_base = 1000000.0
NZ, NX, NY, NC = 8, 4, 4, 2
BF = jnp.bfloat16
F32 = jnp.float32


def shift_z(v, s):
    pairs = [(z * NX + x, ((z + s) % NZ) * NX + x) for z in range(NZ) for x in range(NX)]
    return lax.ppermute(v, "dp", pairs)


def shift_y(v, s):
    pairs = [(y * NC + c, ((y + s) % NY) * NC + c) for y in range(NY) for c in range(NC)]
    return lax.ppermute(v, "tensor", pairs)


def swap_core(v):
    return lax.ppermute(v, "tensor", [(t, t ^ 1) for t in range(NY * NC)])


def exchange_x(v):
    groups = [[z * NX + x for x in range(NX)] for z in range(NZ)]
    return lax.all_to_all(v, "dp", 0, 0, tiled=True, axis_index_groups=groups)


def slot_of(ca_ref, table_ref, index, z):
    storage = table_ref[ca_ref[index]]
    owner = storage >> 1
    column = owner & (NX - 1)
    along = ((owner >> 2) - z) & (NZ - 1)
    return column, column * NZ + along, storage & 1


def pack_kernel(ca_ref, table_ref, tok_ref, out_ref, sem):
    d = lax.axis_index("dp")
    convs = tok_ref.shape[0]

    def step(i, carry):
        _, slot, _ = slot_of(ca_ref, table_ref, d * convs + i, d >> 2)
        pltpu.make_async_copy(tok_ref.at[i], out_ref.at[slot], sem).start()
        return carry

    lax.fori_loop(0, convs, step, 0)
    pltpu.make_async_copy(tok_ref, tok_ref, sem).wait()


def plan_kernel(ca_ref, table_ref, choice_ref, place_ref):
    d = lax.axis_index("dp")
    z, x = d >> 2, d & (NX - 1)
    convs = place_ref.shape[0]

    def clear(i, carry):
        choice_ref[i] = 0
        return carry

    lax.fori_loop(0, NX * NZ, clear, 0)

    def step(i, carry):
        _, slot, _ = slot_of(ca_ref, table_ref, d * convs + i, z)
        place_ref[i] = slot
        for source in range(NX):
            column, slot, which = slot_of(ca_ref, table_ref, (z * NX + source) * convs + i, z)

            @pl.when(column == x)
            def _():
                choice_ref[source * NZ + (slot & (NZ - 1))] = which

        return carry

    lax.fori_loop(0, convs, step, 0)


def rank_kernel(choice_ref, tok_ref, *refs):
    stacks = refs[0:9]
    rank_ref, up_ref = refs[9:11]
    depth = tok_ref.shape[2]
    width = stacks[0].shape[2]
    rows = tok_ref.shape[1]
    for k in range(NZ):
        tok = jnp.concatenate([tok_ref[r * NZ + k] for r in range(NX)], axis=0)
        if k == NZ // 2:
            w = jnp.concatenate([stacks[k][:depth], stacks[NZ][:depth]], axis=1)
        else:
            w = jnp.concatenate([stacks[k][0, :depth], stacks[k][1, :depth]], axis=1)
        res = jnp.dot(tok, w, preferred_element_type=F32)
        for r in range(NX):
            slot = r * NZ + k
            which = choice_ref[slot]
            part = res[r * rows : (r + 1) * rows]
            rank_ref[slot] = jnp.where(which == 1, part[:, width:], part[:, :width]).astype(BF)
            if k == NZ // 2:
                up_ref[slot] = jnp.where(which == 1, stacks[NZ][depth:], stacks[k][depth:])
            else:
                up_ref[slot] = stacks[k][which, depth:]


def unslot_kernel(place_ref, got, keep, send):
    c = lax.axis_index("tensor") & 1
    half = keep.shape[0]
    for j in range(half):
        keep[j] = got[place_ref[c * half + j]]
        send[j] = got[place_ref[(1 - c) * half + j]]


def final_kernel(
    place_ref, span_ref, mine, other, ups, b0, b1, b2, b3, bias, cosine, sine, out
):
    c = lax.axis_index("tensor") & 1
    step = pl.program_id(0)
    half, rows, _ = mine.shape
    rank = mine.shape[2] // 2
    per = out.shape[1] // rows
    head = out.shape[2] // 2
    for j in range(per):
        conv = step * per + j
        here = conv & (half - 1)
        act = jnp.where((conv >> 3) == c, mine[here], other[here])
        up = ups[place_ref[conv]]
        key_delta = jnp.dot(act[:, :rank], up[:rank], preferred_element_type=F32).astype(BF)
        value_delta = jnp.dot(act[:, rank:], up[rank:], preferred_element_type=F32).astype(BF)
        spot = pl.ds(j * rows, rows)
        base = b0[spot].astype(F32) + b1[spot].astype(F32)
        base = base + b2[spot].astype(F32) + b3[spot].astype(F32)
        base = base + bias[0:1].astype(F32)
        key = base[:, :head] + key_delta.astype(F32)
        value = base[:, head:] + value_delta.astype(F32)
        key = key * cosine[spot] + pltpu.roll(key, head // 2, 1) * sine[spot]
        live = lax.broadcasted_iota(jnp.int32, (rows, head), 0) < span_ref[conv]
        out[0, spot, :head] = jnp.where(live, key, 0.0).astype(BF)
        out[0, spot, head:] = jnp.where(live, value, 0.0).astype(BF)


VMEM_SPEC = pl.BlockSpec(memory_space=pltpu.VMEM)
HBM_SPEC = pl.BlockSpec(memory_space=pltpu.HBM)
SMEM_SPEC = pl.BlockSpec(memory_space=pltpu.SMEM)


def body(
    tokens,
    key_value_weight,
    key_value_bias,
    adapter_down_weight,
    adapter_up_weight,
    conversation_adapter,
    adapter_slot_table,
    span_length,
    context_length,
):
    convs = span_length.shape[0]
    total, depth = tokens.shape
    rows = total // convs
    heads, width = key_value_weight.shape[1:]
    head = width // 2
    double_rank = adapter_down_weight.shape[2]
    t = lax.axis_index("tensor")
    y, c = t // NC, t % NC
    half = convs // 2

    stored = adapter_down_weight.shape[0]
    packed = pl.pallas_call(
        pack_kernel,
        out_shape=jax.ShapeDtypeStruct((NX * NZ, rows, depth), BF),
        in_specs=[SMEM_SPEC, SMEM_SPEC, VMEM_SPEC],
        out_specs=HBM_SPEC,
        scratch_shapes=[pltpu.SemaphoreType.DMA],
        compiler_params=pltpu.CompilerParams(vmem_limit_bytes=6 * 1024 * 1024),
        name="pack",
    )(conversation_adapter, adapter_slot_table, tokens.reshape(convs, rows, depth))
    got = exchange_x(packed)
    tokens = lax.optimization_barrier((tokens, packed))[0]
    part = jnp.einsum("td,dhe->hte", tokens, key_value_weight, preferred_element_type=F32)
    part = part.astype(BF).reshape(NY, NC, total, width)
    keep = lax.dynamic_index_in_dim(part, c, 1, keepdims=False)
    send = lax.dynamic_index_in_dim(part, 1 - c, 1, keepdims=False)
    stack = jnp.concatenate(
        [adapter_down_weight, adapter_up_weight.reshape(stored, double_rank, head)], axis=1
    )
    f1, b1 = lax.optimization_barrier((shift_z(stack, 1), shift_z(stack, -1)))
    f2, b2 = lax.optimization_barrier((shift_z(f1, 1), shift_z(b1, -1)))
    f3, b3 = lax.optimization_barrier((shift_z(f2, 1), shift_z(b2, -1)))
    f4, b4 = shift_z(f3[0], 1), shift_z(b3[1], -1)
    stacks = [stack, b1, b2, b3, f4, f3, f2, f1, b4]

    choice, place = pl.pallas_call(
        plan_kernel,
        out_shape=[
            jax.ShapeDtypeStruct((NX * NZ,), jnp.int32),
            jax.ShapeDtypeStruct((convs,), jnp.int32),
        ],
        in_specs=[SMEM_SPEC, SMEM_SPEC],
        out_specs=[SMEM_SPEC, SMEM_SPEC],
        compiler_params=pltpu.CompilerParams(vmem_limit_bytes=1024 * 1024),
        name="plan",
    )(conversation_adapter, adapter_slot_table)

    pair = (keep.astype(F32) + swap_core(send).astype(F32)).astype(BF)
    bases = [lax.dynamic_index_in_dim(pair, (y + s) % NY, 0, keepdims=False) for s in range(NY)]
    bases = [bases[0]] + [shift_y(bases[s], s) for s in range(1, NY)]

    positions = (
        (context_length[:, None] + jnp.arange(rows, dtype=jnp.int32)[None, :])
        .reshape(-1)
        .astype(F32)
    )
    inverse_freq = jnp.exp(
        jnp.arange(head // 2, dtype=F32) * (-2.0 * math.log(rope_base) / head)
    )
    angles = positions[:, None] * inverse_freq[None, :]
    cosine, sine = jnp.cos(angles), jnp.sin(angles)
    cosine = jnp.concatenate([cosine, cosine], axis=-1)
    sine = jnp.concatenate([-sine, sine], axis=-1)

    got, place = lax.optimization_barrier((got, place))
    slots = NX * NZ
    ranks, ups = pl.pallas_call(
        rank_kernel,
        out_shape=[
            jax.ShapeDtypeStruct((slots, rows, double_rank), BF),
            jax.ShapeDtypeStruct((slots, double_rank, head), BF),
        ],
        in_specs=[SMEM_SPEC] + [VMEM_SPEC] * 10,
        out_specs=[VMEM_SPEC] * 2,
        compiler_params=pltpu.CompilerParams(vmem_limit_bytes=12 * 1024 * 1024),
        name="rank",
    )(choice, got, *stacks)
    back = exchange_x(ranks)
    back, bases = lax.optimization_barrier((back, bases))

    kept = jax.ShapeDtypeStruct((half, rows, double_rank), BF)
    keep_r, send_r = pl.pallas_call(
        unslot_kernel,
        out_shape=[kept, kept],
        in_specs=[SMEM_SPEC, VMEM_SPEC],
        out_specs=[VMEM_SPEC] * 2,
        compiler_params=pltpu.CompilerParams(vmem_limit_bytes=4 * 1024 * 1024),
        name="unslot",
    )(place, back)
    mine = (keep_r.astype(F32) + swap_core(send_r).astype(F32)).astype(BF)
    up_back = exchange_x(ups)
    others = [shift_y(mine, s) for s in range(1, NY)]
    others, up_back = lax.optimization_barrier((others, up_back))
    total_rank = mine.astype(F32)
    for o in others:
        total_rank = total_rank + o.astype(F32)
    mine = total_rank.astype(BF)
    other = swap_core(mine)

    steps = 4
    base_spec = pl.BlockSpec((total // steps, width), lambda i, *_: (i, 0))
    trig_spec = pl.BlockSpec((total // steps, head), lambda i, *_: (i, 0))
    full = lambda a: pl.BlockSpec(a.shape, lambda i, *_: (0,) * a.ndim)
    return pl.pallas_call(
        final_kernel,
        out_shape=jax.ShapeDtypeStruct((1, total, width), BF),
        grid_spec=pltpu.PrefetchScalarGridSpec(
            num_scalar_prefetch=2,
            grid=(steps,),
            in_specs=[full(mine), full(other), full(up_back)]
            + [base_spec] * 4
            + [full(key_value_bias), trig_spec, trig_spec],
            out_specs=pl.BlockSpec((1, total // steps, width), lambda i, *_: (0, i, 0)),
        ),
        compiler_params=pltpu.CompilerParams(vmem_limit_bytes=10 * 1024 * 1024),
        name="final",
    )(place, span_length, mine, other, up_back, *bases, key_value_bias, cosine, sine)


def solution(mesh):
    placed = (
        P("dp", "tensor"),
        P("tensor", None, None),
        P("tensor", None),
        P("dp", "tensor", None),
        P("dp", "tensor", None, None, None),
        P(),
        P(),
        P("dp"),
        P("dp"),
    )
    return jax.shard_map(
        body, mesh=mesh, in_specs=placed, out_specs=P("tensor", "dp", None), check_vma=False
    )
```

time: 242 us -> 121 us (0.50)
  Pallas kernels: 78.6 us -> 14.3 us
  waiting for transfers between devices: 92 us -> 33.5 us
  blocking collectives: 0 us -> 10.5 us
  local copies, waits for them, and re-layouts: 20.1 us -> 11.8 us
  starting transfers between devices: 35.7 us -> 33 us
    pallas_call x2, Pallas kernels: 69.3 us -> 7.45 us  [the longest x1 3.92 us: body(): pl.pallas_call(rank_kernel, out_shape=[jax.ShapeDtypeStruct((slots, rows,...]
    ppermute x9 -> x0, waiting for transfers between devices: 51.7 us -> none  [shift_x(): return lax.ppermute(v, 'dp', pairs)]
    ppermute x6, waiting for transfers between devices: 23 us -> 9.78 us  [shift_y(): return lax.ppermute(v, 'tensor', pairs)]
    ppermute x9 -> x0, starting transfers between devices: 10.6 us -> none  [shift_x(): return lax.ppermute(v, 'dp', pairs)]
    all_to_all x0 -> x1, blocking collectives: none -> 10.5 us  [exchange_x(): return lax.all_to_all(v, 'dp', 0, 0, tiled=True, axis_index_groups=groups)]
    all_to_all x0 -> x2, starting transfers between devices: none -> 8.63 us  [exchange_x(): return lax.all_to_all(v, 'dp', 0, 0, tiled=True, axis_index_groups=groups)]
    dynamic_slice x2 -> x0, local copies, waits for them, and re-layouts: 6.52 us -> none  [the longest x1 3.95 us: body(): send = lax.dynamic_index_in_dim(part, 1 - c, 1, keepdims=False)]
    ppermute x8, waiting for transfers between devices: 17.3 us -> 22.9 us  [shift_z(): return lax.ppermute(v, 'dp', pairs)]
  transfers between devices with their start and end apart: 26 -> 19, of which waited for: 12 -> 8; matrix products, arithmetic and copies ran while one was open for 10% -> 18% of each run, Pallas kernels for 30% -> 8%
where the time goes in v2:
time: 121 us; the launch traced here: 120 us
  waiting for transfers between devices  33.5 us (28%)
  starting transfers between devices  33 us (27%)
  Pallas kernels  14.3 us (12%)
  local copies, waits for them, and re-layouts  11.8 us (10%)
  blocking collectives  10.5 us (9%)
  other arithmetic  8.74 us (7%)
  matrix products  8.3 us (7%)
    ppermute x8, waiting for transfers between devices, shift_z(): return lax.ppermute(v, 'dp', pairs)  22.9 us
    ppermute x8, starting transfers between devices, shift_z(): return lax.ppermute(v, 'dp', pairs)  13.3 us
    all_to_all x1, blocking collectives, exchange_x(): return lax.all_to_all(v, 'dp', 0, 0, tiled=True, axis_index_groups=groups)  10.5 us
    ppermute x6, waiting for transfers between devices, shift_y(): return lax.ppermute(v, 'tensor', pairs)  9.78 us
    all_to_all x2, starting transfers between devices, exchange_x(): return lax.all_to_all(v, 'dp', 0, 0, tiled=True, axis_index_groups=groups)  8.63 us
    dot_general x1, matrix products, body(): jnp.einsum('td,dhe->hte', tokens, key_value_weight, preferred_element_typ...  8.3 us
    ppermute x6, starting transfers between devices, shift_y(): return lax.ppermute(v, 'tensor', pairs)  7.25 us
    unnamed x26, local copies, waits for them, and re-layouts  6.04 us
  transfers between devices with their start and end apart: 19, of which 8 were waited for; matrix products, arithmetic and copies ran while one was open for 18% of the time, Pallas kernels for 8%

profile of v2, /device:TPU:1, one launch (start us, length us, event | category | flops | bytes accessed | tf_op | source)
XLA Modules:
  0.0 120.2 jit_solution(6644981172811956954)
XLA Ops:
  0.0 1.1 pad_maximum_fusion.refs_0_
  1.1 6.5 %collective-permute-start.1 = (bf16[2,1152,128]{2,1,0:T(8,128)(2,1)S(1)}, bf16[2,1152,128]{2,1,0:T(8,128)(2,1)S(1)}, u32[]{:S(2)}, u32[]{:S(2)}) collective-permute-start(bf16[2,1152,128]{2,1,0:T(8,128)(2,1)S(1)} %pad_maximum_fusion.refs_0_), channel_id=1, source_target_pairs={{0,224},{8,232},{16,240},{24,248},{32,0},{40,8},{48,16},{56,24},{6... | collective-permute-start | bytes 1769480 | tf_op jit(solution)/shard_map/ppermute | solution.py:19
  7.6 0.0 collective-permute-start
  7.6 1.6 %copy-done.1 = bf16[1024,1024]{1,0:T(8,128)(2,1)S(1)} copy-done((bf16[1024,1024]{1,0:T(8,128)(2,1)S(1)}, bf16[1024,1024]{1,0:T(8,128)(2,1)}, u32[]{:S(2)}) %copy-start.1) | copy-done | bytes 2097176
  9.2 0.7 copy-done.6
  9.9 0.7 copy-done.8
  10.5 3.5 %pack.1 = bf16[32,64,1024]{2,1,0:T(8,128)(2,1)S(1)} custom-call(s32[512]{0:T(512)S(1)} %copy-done.6, s32[64]{0:T(128)S(1)} %copy-done.8, bf16[16,64,1024]{2,1,0:T(8,128)(2,1)S(1)} %bitcast.27), custom_call_target="tpu_custom_call" | custom-call | tf_op jit(solution)/shard_map/pack/pallas_call | solution.py:170
  14.1 2.0 %copy-done = bf16[32,64,1024]{2,1,0:T(8,128)(2,1)} copy-done((bf16[32,64,1024]{2,1,0:T(8,128)(2,1)}, bf16[32,64,1024]{2,1,0:T(8,128)(2,1)S(1)}, u32[]{:S(2)}) %copy-start) | copy-done | bytes 4194328
  16.1 5.0 %all-to-all-start = ((bf16[32,64,1024]{2,1,0:T(8,128)(2,1)}), bf16[32,64,1024]{2,1,0:T(8,128)(2,1)}, u32[]{:S(2)}, u32[]{:S(2)}) async-start(bf16[32,64,1024]{2,1,0:T(8,128)(2,1)} %copy-done), calls=%async_computation | async-start | bytes 8388608 | tf_op jit(solution)/shard_map/all_to_all | solution.py:33
  21.1 8.3 %fusion.3 = bf16[1024,8,256]{2,0,1:T(8,128)(2,1)} fusion(bf16[1024,8,256]{2,1,0:T(8,128)(2,1)} %param.10, bf16[1024,1024]{1,0:T(8,128)(2,1)S(1)} %copy-done.2), kind=kOutput, calls=%fused_computation.4 | convolution fusion | flops 4297064448 | bytes 10485760 | tf_op jit(solution)/shard_map/td,dhe->hte/dot_general | solution.py:181
  29.4 0.0 collective-permute-done.1.refs_1_
  29.4 2.7 %collective-permute-start.3 = (bf16[2,1152,128]{2,1,0:T(8,128)(2,1)S(1)}, bf16[2,1152,128]{2,1,0:T(8,128)(2,1)S(1)}, u32[]{:S(2)}, u32[]{:S(2)}) collective-permute-start(bf16[2,1152,128]{2,1,0:T(8,128)(2,1)S(1)} %collective-permute-done.1.refs_1_), channel_id=1, source_target_pairs={{0,224},{8,232},{16,240},{24,248},{32,0},{40,8},{48,16},{56,24},{6... | collective-permute-start | bytes 1769480 | tf_op jit(solution)/shard_map/ppermute | solution.py:19
  32.1 3.0 %dynamic-slice_bitcast_fusion = bf16[4,1024,256]{2,1,0:T(8,128)(2,1)} fusion(bf16[4,2,1024,256]{3,2,1,0:T(8,128)(2,1)} %bitcast.28, s32[]{:T(128)S(6)} %select_n.49), kind=kLoop, calls=%fused_computation.6 | loop fusion | bytes 4194308 | tf_op jit(solution)/shard_map/jit(dynamic_index_in_dim)/squeeze | solution.py:184
  35.1 1.5 %collective-permute-start.8 = (bf16[4,1024,256]{2,1,0:T(8,128)(2,1)}, bf16[4,1024,256]{2,1,0:T(8,128)(2,1)}, u32[]{:S(2)}, u32[]{:S(2)}) collective-permute-start(bf16[4,1024,256]{2,1,0:T(8,128)(2,1)} %dynamic-slice_bitcast_fusion), channel_id=1, source_target_pairs={{0,1},{1,0},{2,3},{3,2},{4,5},{5,4},{6,7},{7,6},{8,9},{9,8},{10,11... | collective-permute-start | bytes 6291464 | tf_op jit(solution)/shard_map/ppermute | solution.py:28
  36.6 6.8 %collective-permute-done.3.refs_2_ = bf16[2,1152,128]{2,1,0:T(8,128)(2,1)S(1)} collective-permute-done((bf16[2,1152,128]{2,1,0:T(8,128)(2,1)S(1)}, bf16[2,1152,128]{2,1,0:T(8,128)(2,1)S(1)}, u32[]{:S(2)}, u32[]{:S(2)}) %collective-permute-start.3) | collective-permute-done | bytes 589856 | tf_op jit(solution)/shard_map/ppermute | solution.py:19
  43.5 3.4 %collective-permute-done.2.refs_6_ = bf16[2,1152,128]{2,1,0:T(8,128)(2,1)} collective-permute-done((bf16[2,1152,128]{2,1,0:T(8,128)(2,1)}, bf16[2,1152,128]{2,1,0:T(8,128)(2,1)}, u32[]{:S(2)}, u32[]{:S(2)}) %collective-permute-start.2) | collective-permute-done | bytes 589856 | tf_op jit(solution)/shard_map/ppermute | solution.py:19
  46.9 0.1 collective-permute-start.5
  47.0 1.4 %collective-permute-start.4 = (bf16[2,1152,128]{2,1,0:T(8,128)(2,1)}, bf16[2,1152,128]{2,1,0:T(8,128)(2,1)S(1)}, u32[]{:S(2)}, u32[]{:S(2)}) collective-permute-start(bf16[2,1152,128]{2,1,0:T(8,128)(2,1)} %collective-permute-done.2.refs_6_), channel_id=1, source_target_pairs={{0,32},{8,40},{16,48},{24,56},{32,64},{40,72},{48,80},{56,88},{64,... | collective-permute-start | bytes 1769480 | tf_op jit(solution)/shard_map/ppermute | solution.py:19
  48.4 11.0 %collective-permute-done.5.refs_3_ = bf16[2,1152,128]{2,1,0:T(8,128)(2,1)S(1)} collective-permute-done((bf16[2,1152,128]{2,1,0:T(8,128)(2,1)S(1)}, bf16[2,1152,128]{2,1,0:T(8,128)(2,1)S(1)}, u32[]{:S(2)}, u32[]{:S(2)}) %collective-permute-start.5) | collective-permute-done | bytes 589856 | tf_op jit(solution)/shard_map/ppermute | solution.py:19
  59.4 1.6 %collective-permute-done.4.refs_5_ = bf16[2,1152,128]{2,1,0:T(8,128)(2,1)S(1)} collective-permute-done((bf16[2,1152,128]{2,1,0:T(8,128)(2,1)}, bf16[2,1152,128]{2,1,0:T(8,128)(2,1)S(1)}, u32[]{:S(2)}, u32[]{:S(2)}) %collective-permute-start.4) | collective-permute-done | bytes 589856 | tf_op jit(solution)/shard_map/ppermute | solution.py:19
  61.0 0.7 slice_bitcast_fusion.1
  61.7 0.7 slice_bitcast_fusion
  62.5 2.7 %collective-permute-start.7 = (bf16[1152,128]{1,0:T(8,128)(2,1)}, bf16[1152,128]{1,0:T(8,128)(2,1)}, u32[]{:S(2)}, u32[]{:S(2)}) collective-permute-start(bf16[1152,128]{1,0:T(8,128)(2,1)} %slice_bitcast_fusion), channel_id=1, source_target_pairs={{0,224},{8,232},{16,240},{24,248},{32,0},{40,8},{48,16},{56,24},{6... | collective-permute-start | bytes 884744 | tf_op jit(solution)/shard_map/ppermute | solution.py:19
  65.1 2.7 %fusion = bf16[4,1024,256]{2,1,0:T(8,128)(2,1)S(1)} fusion(bf16[4,1024,256]{2,1,0:T(8,128)(2,1)} %collective-permute-done.8, bf16[4,2,1024,256]{3,2,1,0:T(8,128)(2,1)} %bitcast.29, s32[]{:T(128)S(6)} %select_n.48), kind=kLoop, calls=%fused_computation.1 | loop fusion | flops 4194304 | bytes 6291460 | tf_op jit(solution)/shard_map/convert_element_type | solution.py:206
  67.8 1.2 dynamic-slice_bitcast_fusion.1
  69.0 2.7 %collective-permute-start.11 = (bf16[1024,256]{1,0:T(8,128)(2,1)}, bf16[1024,256]{1,0:T(8,128)(2,1)}, u32[]{:S(2)}, u32[]{:S(2)}) collective-permute-start(bf16[1024,256]{1,0:T(8,128)(2,1)} %get-tuple-element.53), channel_id=1, source_target_pairs={{0,6},{1,7},{2,0},{3,1},{4,2},{5,3},{6,4},{7,5},{8,14},{9,15},{10,... | collective-permute-start | bytes 1572872 | tf_op jit(solution)/shard_map/ppermute | solution.py:24
  71.8 0.3 collective-permute-start.10
  72.1 0.7 collective-permute-start.9
  72.8 1.8 %plan.1 = (s32[32]{0:T(128)S(1)}, s32[16]{0:T(128)S(1)}) custom-call(s32[512]{0:T(512)S(1)} %copy-done.7, s32[64]{0:T(128)S(1)} %copy-done.9), custom_call_target="tpu_custom_call" | custom-call | tf_op jit(solution)/shard_map/plan/pallas_call | solution.py:194
  74.7 1.1 copy-done.5
  75.7 3.9 %rank.1 = (bf16[32,64,128]{2,1,0:T(8,128)(2,1)S(1)}, bf16[32,128,128]{2,1,0:T(8,128)(2,1)S(1)}) custom-call(s32[32]{0:T(128)S(1)} %get-tuple-element.31.choice_ref, bf16[32,64,1024]{2,1,0:T(8,128)(2,1)} %all-to-all-done.tok_ref, bf16[2,1152,128]{2,1,0:T(8,128)(2,1)S(1)} %pad_maximum_fusion.refs_0_, bf16[2,1152,128]{2,1,0:T(8,128)(2,1)S(1)} %collective-permute-done.1.refs_1_, ...), custom_call_target="tpu_custom_call" | custom-call | tf_op jit(solution)/shard_map/rank/pallas_call | solution.py:225
  79.7 10.5 %all_to_all.15.got = bf16[32,64,128]{2,1,0:T(8,128)(2,1)S(1)} all-to-all(bf16[32,64,128]{2,1,0:T(8,128)(2,1)S(1)} %get-tuple-element.39), channel_id=1, replica_groups={{0,8,16,24},{32,40,48,56},{64,72,80,88},{96,104,112,120},{128,136,144,1..., dimensions={0} | all-to-all | bytes 1048576 | tf_op jit(solution)/shard_map/all_to_all | solution.py:33
  90.1 3.6 %all-to-all-start.2 = ((bf16[32,128,128]{2,1,0:T(8,128)(2,1)}), bf16[32,128,128]{2,1,0:T(8,128)(2,1)S(1)}, u32[]{:S(2)}, u32[]{:S(2)}) async-start(bf16[32,128,128]{2,1,0:T(8,128)(2,1)} %copy-done.3), calls=%async_computation.2 | async-start | bytes 2097152 | tf_op jit(solution)/shard_map/all_to_all | solution.py:33
  93.8 4.8 %collective-permute-done.9.b1 = bf16[1024,256]{1,0:T(8,128)(2,1)} collective-permute-done((bf16[1024,256]{1,0:T(8,128)(2,1)}, bf16[1024,256]{1,0:T(8,128)(2,1)}, u32[]{:S(2)}, u32[]{:S(2)}) %collective-permute-start.9) | collective-permute-done | bytes 524320 | tf_op jit(solution)/shard_map/ppermute | solution.py:24
  98.7 0.6 unslot.1
  99.2 1.3 %collective-permute-start.12 = (bf16[8,64,128]{2,1,0:T(8,128)(2,1)S(1)}, bf16[8,64,128]{2,1,0:T(8,128)(2,1)S(1)}, u32[]{:S(2)}, u32[]{:S(2)}) collective-permute-start(bf16[8,64,128]{2,1,0:T(8,128)(2,1)S(1)} %get-tuple-element.43), channel_id=1, source_target_pairs={{0,1},{1,0},{2,3},{3,2},{4,5},{5,4},{6,7},{7,6},{8,9},{9,8},{10,11... | collective-permute-start | bytes 393224 | tf_op jit(solution)/shard_map/ppermute | solution.py:28
  100.6 0.1 add_convert_fusion.2
  100.6 0.1 convert_element_type.67
  100.7 0.8 collective-permute-done.12
  101.6 2.1 %collective-permute-start.15 = (bf16[8,64,128]{2,1,0:T(8,128)(2,1)S(1)}, bf16[8,64,128]{2,1,0:T(8,128)(2,1)S(1)}, u32[]{:S(2)}, u32[]{:S(2)}) collective-permute-start(bf16[8,64,128]{2,1,0:T(8,128)(2,1)S(1)} %add_convert_fusion.1), channel_id=1, source_target_pairs={{0,6},{1,7},{2,0},{3,1},{4,2},{5,3},{6,4},{7,5},{8,14},{9,15},{10,... | collective-permute-start | bytes 393224 | tf_op jit(solution)/shard_map/ppermute | solution.py:24
  103.7 1.4 %collective-permute-start.14 = (bf16[8,64,128]{2,1,0:T(8,128)(2,1)S(1)}, bf16[8,64,128]{2,1,0:T(8,128)(2,1)S(1)}, u32[]{:S(2)}, u32[]{:S(2)}) collective-permute-start(bf16[8,64,128]{2,1,0:T(8,128)(2,1)S(1)} %add_convert_fusion.1), channel_id=1, source_target_pairs={{0,4},{1,5},{2,6},{3,7},{4,0},{5,1},{6,2},{7,3},{8,12},{9,13},{10,... | collective-permute-start | bytes 393224 | tf_op jit(solution)/shard_map/ppermute | solution.py:24
  105.1 3.0 %fusion.7 = (f32[1024,64]{1,0:T(8,128)S(1)}, f32[1024,64]{1,0:T(8,128)}, f32[1024,64]{1,0:T(8,128)}) fusion(f32[64]{0:T(128)S(1)} %multiply_exponential_fusion, f32[1024]{0:T(1024)S(1)} %convert_element_type.67), kind=kLoop, calls=%fused_computation.20 | loop fusion | flops 131072 | bytes 790784 | tf_op jit(solution)/shard_map/neg | solution.py:221
  108.1 1.5 %collective-permute-done.14 = bf16[8,64,128]{2,1,0:T(8,128)(2,1)S(1)} collective-permute-done((bf16[8,64,128]{2,1,0:T(8,128)(2,1)S(1)}, bf16[8,64,128]{2,1,0:T(8,128)(2,1)S(1)}, u32[]{:S(2)}, u32[]{:S(2)}) %collective-permute-start.14) | collective-permute-done | bytes 131104 | tf_op jit(solution)/shard_map/ppermute | solution.py:24
  109.6 3.5 %collective-permute-done.13 = bf16[8,64,128]{2,1,0:T(8,128)(2,1)S(1)} collective-permute-done((bf16[8,64,128]{2,1,0:T(8,128)(2,1)S(1)}, bf16[8,64,128]{2,1,0:T(8,128)(2,1)S(1)}, u32[]{:S(2)}, u32[]{:S(2)}) %collective-permute-start.13) | collective-permute-done | bytes 131104 | tf_op jit(solution)/shard_map/ppermute | solution.py:24
  113.0 0.1 add_convert_fusion.mine
  113.1 0.9 collective-permute-start.16
  114.1 1.7 %pad_maximum_fusion.1 = (f32[1024,128]{1,0:T(8,128)S(1)}, f32[1024,128]{1,0:T(8,128)S(1)}) fusion(f32[1024,64]{1,0:T(8,128)} %get-tuple-element.59, f32[1024,64]{1,0:T(8,128)} %get-tuple-element.58, f32[1024,64]{1,0:T(8,128)S(1)} %get-tuple-element.57), kind=kLoop, calls=%fused_computation.10 | loop fusion | flops 262144 | bytes 1835008 | tf_op jit(solution)/shard_map/concatenate | solution.py:220
  115.8 4.4 %final.1 = bf16[1,1024,256]{2,1,0:T(8,128)(2,1)} custom-call(s32[16]{0:T(128)S(1)} %get-tuple-element.30.place_ref, s32[16]{0:T(128)S(1)} %copy-done.11, bf16[8,64,128]{2,1,0:T(8,128)(2,1)S(1)} %add_convert_fusion.mine, bf16[8,64,128]{2,1,0:T(8,128)(2,1)S(1)} %collective-permute-done.16.other, bf16[32,128,128]{2,1,0:T(8,128)(2,1)S(1)} %all-to-all-done.2.ups, ...), custom_call_target="tpu_custom_call" | custom-call | tf_op jit(solution)/shard_map/final/pallas_call | solution.py:262
  (36 shorter events, 0.1 us)
Async XLA Ops:
  1.1 28.3 %collective-permute-start.1 = (bf16[2,1152,128]{2,1,0:T(8,128)(2,1)S(1)}, bf16[2,1152,128]{2,1,0:T(8,128)(2,1)S(1)}, u32[]{:S(2)}, u32[]{:S(2)}) collective-permute-start(bf16[2,1152,128]{2,1,0:T(8,128)(2,1)S(1)} %pad_maximum_fusion.refs_0_), channel_id=1, source_target_pairs={{0,224},{8,232},{16,240},{24,248},{32,0},{40,8},{48,16},{56,24},{6... | collective-permute-start | bytes 1769480 | tf_op jit(solution)/shard_map/ppermute | solution.py:19
  7.6 21.8 %collective-permute-start = (bf16[2,1152,128]{2,1,0:T(8,128)(2,1)S(1)}, bf16[2,1152,128]{2,1,0:T(8,128)(2,1)}, u32[]{:S(2)}, u32[]{:S(2)}) collective-permute-start(bf16[2,1152,128]{2,1,0:T(8,128)(2,1)S(1)} %pad_maximum_fusion.refs_0_), channel_id=1, source_target_pairs={{0,32},{8,40},{16,48},{24,56},{32,64},{40,72},{48,80},{56,88},{64,... | collective-permute-start | bytes 1769480 | tf_op jit(solution)/shard_map/ppermute | solution.py:19
  7.6 1.6 %copy-start.1 = (bf16[1024,1024]{1,0:T(8,128)(2,1)S(1)}, bf16[1024,1024]{1,0:T(8,128)(2,1)}, u32[]{:S(2)}) copy-start(bf16[1024,1024]{1,0:T(8,128)(2,1)} %param.9) | copy-start | bytes 6291460
  9.2 0.7 copy-start.6
  9.9 0.7 copy-start.8
  14.1 2.0 %copy-start = (bf16[32,64,1024]{2,1,0:T(8,128)(2,1)}, bf16[32,64,1024]{2,1,0:T(8,128)(2,1)S(1)}, u32[]{:S(2)}) copy-start(bf16[32,64,1024]{2,1,0:T(8,128)(2,1)S(1)} %pack.1) | copy-start | bytes 12582916
  16.1 5.0 %copy-start.2 = (bf16[1024,1024]{1,0:T(8,128)(2,1)S(1)}, bf16[1024,1024]{1,0:T(8,128)(2,1)}, u32[]{:S(2)}) copy-start(bf16[1024,1024]{1,0:T(8,128)(2,1)} %param.9) | copy-start | bytes 6291460
  16.1 58.5 %all-to-all-start = ((bf16[32,64,1024]{2,1,0:T(8,128)(2,1)}), bf16[32,64,1024]{2,1,0:T(8,128)(2,1)}, u32[]{:S(2)}, u32[]{:S(2)}) async-start(bf16[32,64,1024]{2,1,0:T(8,128)(2,1)} %copy-done), calls=%async_computation | async-start | bytes 8388608 | tf_op jit(solution)/shard_map/all_to_all | solution.py:33
  29.4 14.1 %collective-permute-start.3 = (bf16[2,1152,128]{2,1,0:T(8,128)(2,1)S(1)}, bf16[2,1152,128]{2,1,0:T(8,128)(2,1)S(1)}, u32[]{:S(2)}, u32[]{:S(2)}) collective-permute-start(bf16[2,1152,128]{2,1,0:T(8,128)(2,1)S(1)} %collective-permute-done.1.refs_1_), channel_id=1, source_target_pairs={{0,224},{8,232},{16,240},{24,248},{32,0},{40,8},{48,16},{56,24},{6... | collective-permute-start | bytes 1769480 | tf_op jit(solution)/shard_map/ppermute | solution.py:19
  32.1 14.8 %collective-permute-start.2 = (bf16[2,1152,128]{2,1,0:T(8,128)(2,1)}, bf16[2,1152,128]{2,1,0:T(8,128)(2,1)}, u32[]{:S(2)}, u32[]{:S(2)}) collective-permute-start(bf16[2,1152,128]{2,1,0:T(8,128)(2,1)} %collective-permute-done.refs_7_), channel_id=1, source_target_pairs={{0,32},{8,40},{16,48},{24,56},{32,64},{40,72},{48,80},{56,88},{64,... | collective-permute-start | bytes 1769480 | tf_op jit(solution)/shard_map/ppermute | solution.py:19
  35.1 30.0 %collective-permute-start.8 = (bf16[4,1024,256]{2,1,0:T(8,128)(2,1)}, bf16[4,1024,256]{2,1,0:T(8,128)(2,1)}, u32[]{:S(2)}, u32[]{:S(2)}) collective-permute-start(bf16[4,1024,256]{2,1,0:T(8,128)(2,1)} %dynamic-slice_bitcast_fusion), channel_id=1, source_target_pairs={{0,1},{1,0},{2,3},{3,2},{4,5},{5,4},{6,7},{7,6},{8,9},{9,8},{10,11... | collective-permute-start | bytes 6291464 | tf_op jit(solution)/shard_map/ppermute | solution.py:28
  43.5 21.7 %copy-start.4 = (bf16[2,1152,128]{2,1,0:T(8,128)(2,1)}, bf16[2,1152,128]{2,1,0:T(8,128)(2,1)S(1)}, u32[]{:S(2)}) copy-start(bf16[2,1152,128]{2,1,0:T(8,128)(2,1)S(1)} %collective-permute-done.3.refs_2_) | copy-start | bytes 1769476
  46.9 12.5 %collective-permute-start.5 = (bf16[2,1152,128]{2,1,0:T(8,128)(2,1)S(1)}, bf16[2,1152,128]{2,1,0:T(8,128)(2,1)S(1)}, u32[]{:S(2)}, u32[]{:S(2)}) collective-permute-start(bf16[2,1152,128]{2,1,0:T(8,128)(2,1)S(1)} %collective-permute-done.3.refs_2_), channel_id=1, source_target_pairs={{0,224},{8,232},{16,240},{24,248},{32,0},{40,8},{48,16},{56,24},{6... | collective-permute-start | bytes 1769480 | tf_op jit(solution)/shard_map/ppermute | solution.py:19
  47.0 14.0 %collective-permute-start.4 = (bf16[2,1152,128]{2,1,0:T(8,128)(2,1)}, bf16[2,1152,128]{2,1,0:T(8,128)(2,1)S(1)}, u32[]{:S(2)}, u32[]{:S(2)}) collective-permute-start(bf16[2,1152,128]{2,1,0:T(8,128)(2,1)} %collective-permute-done.2.refs_6_), channel_id=1, source_target_pairs={{0,32},{8,40},{16,48},{24,56},{32,64},{40,72},{48,80},{56,88},{64,... | collective-permute-start | bytes 1769480 | tf_op jit(solution)/shard_map/ppermute | solution.py:19
  61.7 12.9 %collective-permute-start.6 = (bf16[1152,128]{1,0:T(8,128)(2,1)}, bf16[1152,128]{1,0:T(8,128)(2,1)}, u32[]{:S(2)}, u32[]{:S(2)}) collective-permute-start(bf16[1152,128]{1,0:T(8,128)(2,1)} %slice_bitcast_fusion.1), channel_id=1, source_target_pairs={{0,32},{8,40},{16,48},{24,56},{32,64},{40,72},{48,80},{56,88},{64,... | collective-permute-start | bytes 884744 | tf_op jit(solution)/shard_map/ppermute | solution.py:19
  62.4 10.4 %copy-start.7 = (s32[512]{0:T(512)S(1)}, s32[512]{0:T(512)}, u32[]{:S(2)}) copy-start(s32[512]{0:T(512)} %ca_ref.3) | copy-start | bytes 6148
  62.5 10.4 %copy-start.9 = (s32[64]{0:T(128)S(1)}, s32[64]{0:T(128)}, u32[]{:S(2)}) copy-start(s32[64]{0:T(128)} %table_ref.3) | copy-start | bytes 772
  62.5 12.2 %collective-permute-start.7 = (bf16[1152,128]{1,0:T(8,128)(2,1)}, bf16[1152,128]{1,0:T(8,128)(2,1)}, u32[]{:S(2)}, u32[]{:S(2)}) collective-permute-start(bf16[1152,128]{1,0:T(8,128)(2,1)} %slice_bitcast_fusion), channel_id=1, source_target_pairs={{0,224},{8,232},{16,240},{24,248},{32,0},{40,8},{48,16},{56,24},{6... | collective-permute-start | bytes 884744 | tf_op jit(solution)/shard_map/ppermute | solution.py:19
  69.0 24.8 %collective-permute-start.11 = (bf16[1024,256]{1,0:T(8,128)(2,1)}, bf16[1024,256]{1,0:T(8,128)(2,1)}, u32[]{:S(2)}, u32[]{:S(2)}) collective-permute-start(bf16[1024,256]{1,0:T(8,128)(2,1)} %get-tuple-element.53), channel_id=1, source_target_pairs={{0,6},{1,7},{2,0},{3,1},{4,2},{5,3},{6,4},{7,5},{8,14},{9,15},{10,... | collective-permute-start | bytes 1572872 | tf_op jit(solution)/shard_map/ppermute | solution.py:24
  71.8 22.1 %collective-permute-start.10 = (bf16[1024,256]{1,0:T(8,128)(2,1)}, bf16[1024,256]{1,0:T(8,128)(2,1)}, u32[]{:S(2)}, u32[]{:S(2)}) collective-permute-start(bf16[1024,256]{1,0:T(8,128)(2,1)} %get-tuple-element.54), channel_id=1, source_target_pairs={{0,4},{1,5},{2,6},{3,7},{4,0},{5,1},{6,2},{7,3},{8,12},{9,13},{10,... | collective-permute-start | bytes 1572872 | tf_op jit(solution)/shard_map/ppermute | solution.py:24
  72.1 26.6 %collective-permute-start.9 = (bf16[1024,256]{1,0:T(8,128)(2,1)}, bf16[1024,256]{1,0:T(8,128)(2,1)}, u32[]{:S(2)}, u32[]{:S(2)}) collective-permute-start(bf16[1024,256]{1,0:T(8,128)(2,1)} %get-tuple-element.55), channel_id=1, source_target_pairs={{0,2},{1,3},{2,4},{3,5},{4,6},{5,7},{6,0},{7,1},{8,10},{9,11},{10,... | collective-permute-start | bytes 1572872 | tf_op jit(solution)/shard_map/ppermute | solution.py:24
  74.6 1.1 copy-start.5
  75.7 24.9 %copy-start.12 = (s32[16]{0:T(128)S(1)}, s32[16]{0:T(128)}, u32[]{:S(2)}) copy-start(s32[16]{0:T(128)} %param.17) | copy-start | bytes 196
  79.6 10.5 %copy-start.3 = (bf16[32,128,128]{2,1,0:T(8,128)(2,1)}, bf16[32,128,128]{2,1,0:T(8,128)(2,1)S(1)}, u32[]{:S(2)}) copy-start(bf16[32,128,128]{2,1,0:T(8,128)(2,1)S(1)} %get-tuple-element.44) | copy-start | bytes 3145732
  90.1 25.6 %copy-start.10 = (bf16[1,256]{1,0:T(2,128)(2,1)S(1)}, bf16[1,256]{1,0:T(2,128)(2,1)}, u32[]{:S(2)}) copy-start(bf16[1,256]{1,0:T(2,128)(2,1)} %bias.1) | copy-start | bytes 1540
  90.1 25.6 %copy-start.11 = (s32[16]{0:T(128)S(1)}, s32[16]{0:T(128)}, u32[]{:S(2)}) copy-start(s32[16]{0:T(128)} %span_ref.1) | copy-start | bytes 196
  90.1 22.9 %all-to-all-start.2 = ((bf16[32,128,128]{2,1,0:T(8,128)(2,1)}), bf16[32,128,128]{2,1,0:T(8,128)(2,1)S(1)}, u32[]{:S(2)}, u32[]{:S(2)}) async-start(bf16[32,128,128]{2,1,0:T(8,128)(2,1)} %copy-done.3), calls=%async_computation.2 | async-start | bytes 2097152 | tf_op jit(solution)/shard_map/all_to_all | solution.py:33
  99.2 2.3 %collective-permute-start.12 = (bf16[8,64,128]{2,1,0:T(8,128)(2,1)S(1)}, bf16[8,64,128]{2,1,0:T(8,128)(2,1)S(1)}, u32[]{:S(2)}, u32[]{:S(2)}) collective-permute-start(bf16[8,64,128]{2,1,0:T(8,128)(2,1)S(1)} %get-tuple-element.43), channel_id=1, source_target_pairs={{0,1},{1,0},{2,3},{3,2},{4,5},{5,4},{6,7},{7,6},{8,9},{9,8},{10,11... | collective-permute-start | bytes 393224 | tf_op jit(solution)/shard_map/ppermute | solution.py:28
  101.6 6.5 %collective-permute-start.15 = (bf16[8,64,128]{2,1,0:T(8,128)(2,1)S(1)}, bf16[8,64,128]{2,1,0:T(8,128)(2,1)S(1)}, u32[]{:S(2)}, u32[]{:S(2)}) collective-permute-start(bf16[8,64,128]{2,1,0:T(8,128)(2,1)S(1)} %add_convert_fusion.1), channel_id=1, source_target_pairs={{0,6},{1,7},{2,0},{3,1},{4,2},{5,3},{6,4},{7,5},{8,14},{9,15},{10,... | collective-permute-start | bytes 393224 | tf_op jit(solution)/shard_map/ppermute | solution.py:24
  103.7 5.9 %collective-permute-start.14 = (bf16[8,64,128]{2,1,0:T(8,128)(2,1)S(1)}, bf16[8,64,128]{2,1,0:T(8,128)(2,1)S(1)}, u32[]{:S(2)}, u32[]{:S(2)}) collective-permute-start(bf16[8,64,128]{2,1,0:T(8,128)(2,1)S(1)} %add_convert_fusion.1), channel_id=1, source_target_pairs={{0,4},{1,5},{2,6},{3,7},{4,0},{5,1},{6,2},{7,3},{8,12},{9,13},{10,... | collective-permute-start | bytes 393224 | tf_op jit(solution)/shard_map/ppermute | solution.py:24
  105.1 8.0 %collective-permute-start.13 = (bf16[8,64,128]{2,1,0:T(8,128)(2,1)S(1)}, bf16[8,64,128]{2,1,0:T(8,128)(2,1)S(1)}, u32[]{:S(2)}, u32[]{:S(2)}) collective-permute-start(bf16[8,64,128]{2,1,0:T(8,128)(2,1)S(1)} %add_convert_fusion.1), channel_id=1, source_target_pairs={{0,2},{1,3},{2,4},{3,5},{4,6},{5,7},{6,0},{7,1},{8,10},{9,11},{10,... | collective-permute-start | bytes 393224 | tf_op jit(solution)/shard_map/ppermute | solution.py:24
  113.1 2.6 %collective-permute-start.16 = (bf16[8,64,128]{2,1,0:T(8,128)(2,1)S(1)}, bf16[8,64,128]{2,1,0:T(8,128)(2,1)S(1)}, u32[]{:S(2)}, u32[]{:S(2)}) collective-permute-start(bf16[8,64,128]{2,1,0:T(8,128)(2,1)S(1)} %add_convert_fusion.mine), channel_id=1, source_target_pairs={{0,1},{1,0},{2,3},{3,2},{4,5},{5,4},{6,7},{7,6},{8,9},{9,8},{10,11... | collective-permute-start | bytes 393224 | tf_op jit(solution)/shard_map/ppermute | solution.py:28

commit v3 on v2

--- a/solution.py
+++ b/solution.py
@@ -14,6 +14,11 @@
 F32 = jnp.float32
 
 
+def shift_x(v, s):
+    pairs = [(z * NX + x, z * NX + (x + s) % NX) for z in range(NZ) for x in range(NX)]
+    return lax.ppermute(v, "dp", pairs)
+
+
 def shift_z(v, s):
     pairs = [(z * NX + x, ((z + s) % NZ) * NX + x) for z in range(NZ) for x in range(NX)]
     return lax.ppermute(v, "dp", pairs)
@@ -66,8 +71,8 @@
     lax.fori_loop(0, NX * NZ, clear, 0)
 
     def step(i, carry):
-        _, slot, _ = slot_of(ca_ref, table_ref, d * convs + i, z)
-        place_ref[i] = slot
+        column, slot, _ = slot_of(ca_ref, table_ref, d * convs + i, z)
+        place_ref[i] = ((column - x) & (NX - 1)) * NZ + (slot & (NZ - 1))
         for source in range(NX):
             column, slot, which = slot_of(ca_ref, table_ref, (z * NX + source) * convs + i, z)
 
@@ -80,40 +85,70 @@
     lax.fori_loop(0, convs, step, 0)
 
 
-def rank_kernel(choice_ref, tok_ref, *refs):
-    stacks = refs[0:9]
-    rank_ref, up_ref = refs[9:11]
+def rank_rows(k, tok_ref, choice_ref, weights, blocks, ranks, ups):
+    x = lax.axis_index("dp") & (NX - 1)
+    rows = tok_ref.shape[1]
+    slots = [((x - r) & (NX - 1)) * NZ + k for r in range(NX)]
+    tok = jnp.concatenate([tok_ref[slot] for slot in slots], axis=0)
+    width = weights[0].shape[1]
+    res = jnp.dot(tok, jnp.concatenate(weights, axis=1), preferred_element_type=F32)
+    for r in range(NX):
+        second = choice_ref[slots[r]] == 1
+        part = res[r * rows : (r + 1) * rows]
+        ranks[r][k] = jnp.where(second, part[:, width:], part[:, :width]).astype(BF)
+        ups[r][k] = jnp.where(second, blocks[1], blocks[0])
+
+
+def rank_kernel(choice_ref, tok_ref, own, b1, b2, b3, f3, f2, f1, *refs):
+    ranks, ups = refs[0:4], refs[4:8]
+    held, sems = refs[8:10]
     depth = tok_ref.shape[2]
-    width = stacks[0].shape[2]
+    copies = [pltpu.make_async_copy(v, held.at[i], sems.at[i]) for i, v in enumerate((b3, f3))]
+    for copy in copies:
+        copy.start()
+    for k, v in ((0, own), (1, b1), (2, b2), (6, f2), (7, f1), (3, held.at[0]), (5, held.at[1])):
+        if k == 3:
+            copies[0].wait()
+        if k == 5:
+            copies[1].wait()
+        weights = [v[i, :depth] for i in range(2)]
+        rank_rows(k, tok_ref, choice_ref, weights, [v[i, depth:] for i in range(2)], ranks, ups)
+
+
+def opposite_kernel(choice_ref, tok_ref, f4, b4, *refs):
+    ranks, ups = refs[8:12], refs[12:16]
+    depth = tok_ref.shape[2]
+    x = lax.axis_index("dp") & (NX - 1)
     rows = tok_ref.shape[1]
-    for k in range(NZ):
-        tok = jnp.concatenate([tok_ref[r * NZ + k] for r in range(NX)], axis=0)
-        if k == NZ // 2:
-            w = jnp.concatenate([stacks[k][:depth], stacks[NZ][:depth]], axis=1)
-        else:
-            w = jnp.concatenate([stacks[k][0, :depth], stacks[k][1, :depth]], axis=1)
-        res = jnp.dot(tok, w, preferred_element_type=F32)
-        for r in range(NX):
-            slot = r * NZ + k
-            which = choice_ref[slot]
-            part = res[r * rows : (r + 1) * rows]
-            rank_ref[slot] = jnp.where(which == 1, part[:, width:], part[:, :width]).astype(BF)
-            if k == NZ // 2:
-                up_ref[slot] = jnp.where(which == 1, stacks[NZ][depth:], stacks[k][depth:])
-            else:
-                up_ref[slot] = stacks[k][which, depth:]
-
-
-def unslot_kernel(place_ref, got, keep, send):
+    tok = jnp.concatenate([tok_ref[(x - r) & (NX - 1)] for r in range(NX)], axis=0)
+    weights = jnp.concatenate([f4[:depth], b4[:depth]], axis=1)
+    width = f4.shape[1]
+    res = jnp.dot(tok, weights, preferred_element_type=F32)
+    for r in range(NX):
+        second = choice_ref[((x - r) & (NX - 1)) * NZ + NZ // 2] == 1
+        part = res[r * rows : (r + 1) * rows]
+        ranks[r][0] = jnp.where(second, part[:, width:], part[:, :width]).astype(BF)
+        ups[r][0] = jnp.where(second, b4[depth:], f4[depth:])
+
+
+def pick(sources, place, count):
+    across, along = place >> 3, place & (NZ - 1)
+    value = sources[0][along]
+    for r in range(1, count):
+        value = jnp.where(across == r, sources[r][along], value)
+    return value
+
+
+def unslot_kernel(place_ref, g0, g1, g2, g3, keep, send):
     c = lax.axis_index("tensor") & 1
     half = keep.shape[0]
     for j in range(half):
-        keep[j] = got[place_ref[c * half + j]]
-        send[j] = got[place_ref[(1 - c) * half + j]]
+        keep[j] = pick((g0, g1, g2, g3), place_ref[c * half + j], NX)
+        send[j] = pick((g0, g1, g2, g3), place_ref[(1 - c) * half + j], NX)
 
 
 def final_kernel(
-    place_ref, span_ref, mine, other, ups, b0, b1, b2, b3, bias, cosine, sine, out
+    place_ref, span_ref, mine, other, u0, u1, u2, u3, b0, b1, b2, b3, bias, cosine, sine, out
 ):
     c = lax.axis_index("tensor") & 1
     step = pl.program_id(0)
@@ -125,7 +160,7 @@
         conv = step * per + j
         here = conv & (half - 1)
         act = jnp.where((conv >> 3) == c, mine[here], other[here])
-        up = ups[place_ref[conv]]
+        up = pick((u0, u1, u2, u3), place_ref[conv], NX)
         key_delta = jnp.dot(act[:, :rank], up[:rank], preferred_element_type=F32).astype(BF)
         value_delta = jnp.dot(act[:, rank:], up[rank:], preferred_element_type=F32).astype(BF)
         spot = pl.ds(j * rows, rows)
@@ -141,6 +176,7 @@
 
 
 VMEM_SPEC = pl.BlockSpec(memory_space=pltpu.VMEM)
+ANY_SPEC = pl.BlockSpec(memory_space=pl.ANY)
 HBM_SPEC = pl.BlockSpec(memory_space=pltpu.HBM)
 SMEM_SPEC = pl.BlockSpec(memory_space=pltpu.SMEM)
 
@@ -173,24 +209,25 @@
         in_specs=[SMEM_SPEC, SMEM_SPEC, VMEM_SPEC],
         out_specs=HBM_SPEC,
         scratch_shapes=[pltpu.SemaphoreType.DMA],
-        compiler_params=pltpu.CompilerParams(vmem_limit_bytes=6 * 1024 * 1024),
+        compiler_params=pltpu.CompilerParams(vmem_limit_bytes=60 * 1024 * 1024),
         name="pack",
     )(conversation_adapter, adapter_slot_table, tokens.reshape(convs, rows, depth))
     got = exchange_x(packed)
-    tokens = lax.optimization_barrier((tokens, packed))[0]
+    stack = jnp.concatenate(
+        [adapter_down_weight, adapter_up_weight.reshape(stored, double_rank, head)], axis=1
+    )
+    f1, b1 = lax.optimization_barrier((shift_z(stack, 1), shift_z(stack, -1)))
+    tokens = lax.optimization_barrier((tokens, packed, f1, b1))[0]
     part = jnp.einsum("td,dhe->hte", tokens, key_value_weight, preferred_element_type=F32)
     part = part.astype(BF).reshape(NY, NC, total, width)
-    keep = lax.dynamic_index_in_dim(part, c, 1, keepdims=False)
-    send = lax.dynamic_index_in_dim(part, 1 - c, 1, keepdims=False)
-    stack = jnp.concatenate(
-        [adapter_down_weight, adapter_up_weight.reshape(stored, double_rank, head)], axis=1
-    )
-    f1, b1 = lax.optimization_barrier((shift_z(stack, 1), shift_z(stack, -1)))
-    f2, b2 = lax.optimization_barrier((shift_z(f1, 1), shift_z(b1, -1)))
-    f3, b3 = lax.optimization_barrier((shift_z(f2, 1), shift_z(b2, -1)))
-    f4, b4 = shift_z(f3[0], 1), shift_z(b3[1], -1)
-    stacks = [stack, b1, b2, b3, f4, f3, f2, f1, b4]
-
+    flat = part.reshape(NY * NC, total, width)
+    keep, send = [
+        [
+            lax.dynamic_index_in_dim(flat, (y + s) % NY * NC + core, 0, keepdims=False)
+            for s in range(NY)
+        ]
+        for core in (c, 1 - c)
+    ]
     choice, place = pl.pallas_call(
         plan_kernel,
         out_shape=[
@@ -203,50 +240,71 @@
         name="plan",
     )(conversation_adapter, adapter_slot_table)
 
-    pair = (keep.astype(F32) + swap_core(send).astype(F32)).astype(BF)
-    bases = [lax.dynamic_index_in_dim(pair, (y + s) % NY, 0, keepdims=False) for s in range(NY)]
-    bases = [bases[0]] + [shift_y(bases[s], s) for s in range(1, NY)]
+    bases = [(k.astype(F32) + swap_core(v).astype(F32)).astype(BF) for k, v in zip(keep, send)]
 
     positions = (
         (context_length[:, None] + jnp.arange(rows, dtype=jnp.int32)[None, :])
         .reshape(-1)
         .astype(F32)
     )
+    lane = jnp.arange(head, dtype=jnp.int32)
     inverse_freq = jnp.exp(
-        jnp.arange(head // 2, dtype=F32) * (-2.0 * math.log(rope_base) / head)
+        (lane % (head // 2)).astype(F32) * (-2.0 * math.log(rope_base) / head)
     )
     angles = positions[:, None] * inverse_freq[None, :]
-    cosine, sine = jnp.cos(angles), jnp.sin(angles)
-    cosine = jnp.concatenate([cosine, cosine], axis=-1)
-    sine = jnp.concatenate([-sine, sine], axis=-1)
-
-    got, place = lax.optimization_barrier((got, place))
-    slots = NX * NZ
-    ranks, ups = pl.pallas_call(
+    cosine = jnp.cos(angles)
+    sine = jnp.where(lane < head // 2, -1.0, 1.0) * jnp.sin(angles)
+
+    f2, b2 = lax.optimization_barrier((shift_z(f1, 1), shift_z(b1, -1)))
+    f3, b3 = lax.optimization_barrier((shift_z(f2, 1), shift_z(b2, -1)))
+    f3_first, b3_second = lax.optimization_barrier((f3[0], b3[1], bases))[:2]
+    f4, b4 = shift_z(f3_first, 1), shift_z(b3_second, -1)
+
+    bases = [bases[0]] + [shift_y(bases[s], s) for s in range(1, NY)]
+    choice = lax.optimization_barrier((choice, place))[0]
+    small = jax.ShapeDtypeStruct((NZ, rows, double_rank), BF)
+    blocks = jax.ShapeDtypeStruct((NZ, double_rank, head), BF)
+    results = pl.pallas_call(
         rank_kernel,
-        out_shape=[
-            jax.ShapeDtypeStruct((slots, rows, double_rank), BF),
-            jax.ShapeDtypeStruct((slots, double_rank, head), BF),
+        out_shape=[small] * NX + [blocks] * NX,
+        in_specs=[SMEM_SPEC] + [VMEM_SPEC] * 4 + [ANY_SPEC] * 2 + [VMEM_SPEC] * 2,
+        out_specs=[VMEM_SPEC] * 8,
+        scratch_shapes=[
+            pltpu.VMEM((2, *stack.shape), BF),
+            pltpu.SemaphoreType.DMA((2,)),
         ],
-        in_specs=[SMEM_SPEC] + [VMEM_SPEC] * 10,
-        out_specs=[VMEM_SPEC] * 2,
         compiler_params=pltpu.CompilerParams(vmem_limit_bytes=12 * 1024 * 1024),
         name="rank",
-    )(choice, got, *stacks)
-    back = exchange_x(ranks)
-    back, bases = lax.optimization_barrier((back, bases))
+    )(choice, got, stack, b1, b2, b3, f3, f2, f1)
+    opposite = NZ // 2
+    whole = lambda n: pl.BlockSpec(memory_space=pltpu.VMEM)
+    one = lambda a: pl.BlockSpec((1, *a.shape[1:]), lambda i: (opposite,) + (0,) * (a.ndim - 1))
+    tok_spec = pl.BlockSpec((NX, pl.Squeezed(), rows, depth), lambda i: (0, opposite, 0, 0))
+    results = pl.pallas_call(
+        opposite_kernel,
+        grid=(1,),
+        out_shape=[small] * NX + [blocks] * NX,
+        in_specs=[SMEM_SPEC, tok_spec, whole(0), whole(0)] + [ANY_SPEC] * 8,
+        out_specs=[one(v) for v in results],
+        input_output_aliases={4 + i: i for i in range(8)},
+        compiler_params=pltpu.CompilerParams(vmem_limit_bytes=6 * 1024 * 1024),
+        name="opposite",
+    )(choice, got.reshape(NX, NZ, rows, depth), f4, b4, *results)
+    ranks, ups = results[:NX], results[NX:]
+    back = [ranks[0]] + [shift_x(ranks[r], -r) for r in range(1, NX)]
+    back = lax.optimization_barrier((back, bases))[0]
 
     kept = jax.ShapeDtypeStruct((half, rows, double_rank), BF)
     keep_r, send_r = pl.pallas_call(
         unslot_kernel,
         out_shape=[kept, kept],
-        in_specs=[SMEM_SPEC, VMEM_SPEC],
+        in_specs=[SMEM_SPEC] + [VMEM_SPEC] * 4,
         out_specs=[VMEM_SPEC] * 2,
         compiler_params=pltpu.CompilerParams(vmem_limit_bytes=4 * 1024 * 1024),
         name="unslot",
-    )(place, back)
+    )(place, *back)
     mine = (keep_r.astype(F32) + swap_core(send_r).astype(F32)).astype(BF)
-    up_back = exchange_x(ups)
+    up_back = [ups[0]] + [shift_x(ups[r], -r) for r in range(1, NX)]
     others = [shift_y(mine, s) for s in range(1, NY)]
     others, up_back = lax.optimization_barrier((others, up_back))
     total_rank = mine.astype(F32)
@@ -265,14 +323,15 @@
         grid_spec=pltpu.PrefetchScalarGridSpec(
             num_scalar_prefetch=2,
             grid=(steps,),
-            in_specs=[full(mine), full(other), full(up_back)]
+            in_specs=[full(mine), full(other)]
+            + [full(u) for u in up_back]
             + [base_spec] * 4
             + [full(key_value_bias), trig_spec, trig_spec],
             out_specs=pl.BlockSpec((1, total // steps, width), lambda i, *_: (0, i, 0)),
         ),
         compiler_params=pltpu.CompilerParams(vmem_limit_bytes=10 * 1024 * 1024),
         name="final",
-    )(place, span_length, mine, other, up_back, *bases, key_value_bias, cosine, sine)
+    )(place, span_length, mine, other, *up_back, *bases, key_value_bias, cosine, sine)
 
 
 def solution(mesh):

time: 121 us -> 107 us (0.88)
  starting transfers between devices: 33 us -> 44 us
  blocking collectives: 10.5 us -> 0 us
  local copies, waits for them, and re-layouts: 11.8 us -> 4.12 us
  waiting for transfers between devices: 33.5 us -> 26.9 us
  Pallas kernels: 14.3 us -> 17.2 us
  other arithmetic: 8.74 us -> 6.84 us
    ppermute x0 -> x6, waiting for transfers between devices: none -> 12.8 us  [shift_x(): return lax.ppermute(v, 'dp', pairs)]
    ppermute x8, waiting for transfers between devices: 22.9 us -> 10.6 us  [shift_z(): return lax.ppermute(v, 'dp', pairs)]
    all_to_all x1 -> x0, blocking collectives: 10.5 us -> none  [exchange_x(): return lax.all_to_all(v, 'dp', 0, 0, tiled=True, axis_index_groups=groups)]
    ppermute x6, waiting for transfers between devices: 9.78 us -> 0.02 us  [shift_y(): return lax.ppermute(v, 'tensor', pairs)]
    ppermute x6, starting transfers between devices: 7.25 us -> 11.7 us  [shift_y(): return lax.ppermute(v, 'tensor', pairs)]
    ppermute x3 -> x6, starting transfers between devices: 3.78 us -> 8.18 us  [swap_core(): return lax.ppermute(v, 'tensor', [(t, t ^ 1) for t in range(NY * NC)])]
    unnamed x26 -> x18, local copies, waits for them, and re-layouts: 6.04 us -> 1.89 us
    ppermute x0 -> x6, starting transfers between devices: none -> 4.13 us  [shift_x(): return lax.ppermute(v, 'dp', pairs)]
  transfers between devices with their start and end apart: 19 -> 27, of which waited for: 8 -> 9; matrix products, arithmetic and copies ran while one was open for 18% -> 14% of each run, Pallas kernels for 8% -> 11%
where the time goes in v3:
time: 107 us
  starting transfers between devices  44 us (41%)
  waiting for transfers between devices  26.9 us (25%)
  Pallas kernels  17.2 us (16%)
  matrix products  7.33 us (7%)
  other arithmetic  6.84 us (6%)
  local copies, waits for them, and re-layouts  4.12 us (4%)
    ppermute x8, starting transfers between devices, shift_z(): return lax.ppermute(v, 'dp', pairs)  15.1 us
    ppermute x6, waiting for transfers between devices, shift_x(): return lax.ppermute(v, 'dp', pairs)  12.8 us
    ppermute x6, starting transfers between devices, shift_y(): return lax.ppermute(v, 'tensor', pairs)  11.7 us
    ppermute x8, waiting for transfers between devices, shift_z(): return lax.ppermute(v, 'dp', pairs)  10.6 us
    ppermute x6, starting transfers between devices, swap_core(): return lax.ppermute(v, 'tensor', [(t, t ^ 1) for t in range(NY * NC)])  8.18 us
    dot_general x1, matrix products, body(): jnp.einsum('td,dhe->hte', tokens, key_value_weight, preferred_element_typ...  7.33 us
    pallas_call x1, Pallas kernels, body(): pl.pallas_call(rank_kernel, out_shape=[small] * NX + [blocks] * NX, in_sp...  5.21 us
    all_to_all x1, starting transfers between devices, exchange_x(): return lax.all_to_all(v, 'dp', 0, 0, tiled=True, axis_index_groups=groups)  4.88 us
  transfers between devices with their start and end apart: 27, of which 9 were waited for; matrix products, arithmetic and copies ran while one was open for 14% of the time, Pallas kernels for 11%

profile of v3, /device:TPU:1, one launch (start us, length us, event | category | flops | bytes accessed | tf_op | source)
XLA Modules:
  0.0 106.8 jit_solution(11710045327249003366)
XLA Ops:
  0.0 1.1 %pad_maximum_fusion.own = bf16[2,1152,128]{2,1,0:T(8,128)(2,1)S(1)} fusion(bf16[2,128,128]{2,1,0:T(8,128)(2,1)} %bitcast.31, bf16[2,1024,128]{2,1,0:T(8,128)(2,1)} %param.12), kind=kLoop, calls=%fused_computation.14 | loop fusion | flops 1179648 | bytes 1179648 | tf_op jit(solution)/shard_map/concatenate | solution.py:216
  1.1 2.5 %collective-permute-start = (bf16[2,1152,128]{2,1,0:T(8,128)(2,1)S(1)}, bf16[2,1152,128]{2,1,0:T(8,128)(2,1)S(1)}, u32[]{:S(2)}, u32[]{:S(2)}) collective-permute-start(bf16[2,1152,128]{2,1,0:T(8,128)(2,1)S(1)} %pad_maximum_fusion.own), channel_id=1, source_target_pairs={{0,32},{8,40},{16,48},{24,56},{32,64},{40,72},{48,80},{56,88},{64,... | collective-permute-start | bytes 1769480 | tf_op jit(solution)/shard_map/ppermute | solution.py:24
  3.7 4.0 %collective-permute-start.1 = (bf16[2,1152,128]{2,1,0:T(8,128)(2,1)S(1)}, bf16[2,1152,128]{2,1,0:T(8,128)(2,1)S(1)}, u32[]{:S(2)}, u32[]{:S(2)}) collective-permute-start(bf16[2,1152,128]{2,1,0:T(8,128)(2,1)S(1)} %pad_maximum_fusion.own), channel_id=1, source_target_pairs={{0,224},{8,232},{16,240},{24,248},{32,0},{40,8},{48,16},{56,24},{6... | collective-permute-start | bytes 1769480 | tf_op jit(solution)/shard_map/ppermute | solution.py:24
  7.7 3.0 %pack.1 = bf16[32,64,1024]{2,1,0:T(8,128)(2,1)} custom-call(s32[512]{0:T(512)} %ca_ref.3, s32[64]{0:T(128)} %table_ref.3, bf16[16,64,1024]{2,1,0:T(8,128)(2,1)} %bitcast.30), custom_call_target="tpu_custom_call" | custom-call | tf_op jit(solution)/shard_map/pack/pallas_call | solution.py:206
  10.7 4.9 %all-to-all-start = ((bf16[32,64,1024]{2,1,0:T(8,128)(2,1)}), bf16[32,64,1024]{2,1,0:T(8,128)(2,1)}, u32[]{:S(2)}, u32[]{:S(2)}) async-start(bf16[32,64,1024]{2,1,0:T(8,128)(2,1)} %pack.1), calls=%async_computation | async-start | bytes 8388608 | tf_op jit(solution)/shard_map/all_to_all | solution.py:38
  15.7 4.9 %collective-permute-done.f1 = bf16[2,1152,128]{2,1,0:T(8,128)(2,1)S(1)} collective-permute-done((bf16[2,1152,128]{2,1,0:T(8,128)(2,1)S(1)}, bf16[2,1152,128]{2,1,0:T(8,128)(2,1)S(1)}, u32[]{:S(2)}, u32[]{:S(2)}) %collective-permute-start) | collective-permute-done | bytes 589856 | tf_op jit(solution)/shard_map/ppermute | solution.py:24
  20.7 2.7 %collective-permute-start.3 = (bf16[2,1152,128]{2,1,0:T(8,128)(2,1)S(1)}, bf16[2,1152,128]{2,1,0:T(8,128)(2,1)}, u32[]{:S(2)}, u32[]{:S(2)}) collective-permute-start(bf16[2,1152,128]{2,1,0:T(8,128)(2,1)S(1)} %collective-permute-done.1.b1), channel_id=1, source_target_pairs={{0,224},{8,232},{16,240},{24,248},{32,0},{40,8},{48,16},{56,24},{6... | collective-permute-start | bytes 1769480 | tf_op jit(solution)/shard_map/ppermute | solution.py:24
  23.3 7.3 %fusion.2 = bf16[1024,8,256]{2,0,1:T(8,128)(2,1)S(1)} fusion(bf16[1024,8,256]{2,1,0:T(8,128)(2,1)} %param.10, bf16[1024,1024]{1,0:T(8,128)(2,1)} %param.9), kind=kOutput, calls=%fused_computation.2 | convolution fusion | flops 4297064448 | bytes 10485760 | tf_op jit(solution)/shard_map/td,dhe->hte/dot_general | solution.py:221
  30.7 1.3 %dynamic-slice_bitcast_fusion = (bf16[1024,256]{1,0:T(8,128)(2,1)}, bf16[1024,256]{1,0:T(8,128)(2,1)}, bf16[1024,256]{1,0:T(8,128)(2,1)}, bf16[1024,256]{1,0:T(8,128)(2,1)S(1)}) fusion(bf16[1024,8,256]{2,0,1:T(8,128)(2,1)S(1)} %fusion.2, s32[]{:T(128)S(6)} %select_n.91, s32[]{:T(128)S(6)} %select_n.88, s32[]{:T(128)S(6)} %select_n.85, s32[]{:T(128)S(6)} %select_n.82), kind=kLoop, calls=%fused_computation.16 | loop fusion | bytes 4194320 | tf_op jit(solution)/shard_map/jit(dynamic_index_in_dim)/squeeze | solution.py:226
  32.0 1.8 %collective-permute-start.6 = (bf16[1024,256]{1,0:T(8,128)(2,1)S(1)}, bf16[1024,256]{1,0:T(8,128)(2,1)S(1)}, u32[]{:S(2)}, u32[]{:S(2)}) collective-permute-start(bf16[1024,256]{1,0:T(8,128)(2,1)S(1)} %get-tuple-element.93), channel_id=1, source_target_pairs={{0,1},{1,0},{2,3},{3,2},{4,5},{5,4},{6,7},{7,6},{8,9},{9,8},{10,11... | collective-permute-start | bytes 1572872 | tf_op jit(solution)/shard_map/ppermute | solution.py:33
  33.8 0.1 collective-permute-start.7
  33.9 0.4 collective-permute-start.8
  34.3 1.3 %collective-permute-done.2.f2 = bf16[2,1152,128]{2,1,0:T(8,128)(2,1)} collective-permute-done((bf16[2,1152,128]{2,1,0:T(8,128)(2,1)S(1)}, bf16[2,1152,128]{2,1,0:T(8,128)(2,1)}, u32[]{:S(2)}, u32[]{:S(2)}) %collective-permute-start.2) | collective-permute-done | bytes 589856 | tf_op jit(solution)/shard_map/ppermute | solution.py:24
  35.6 2.1 %collective-permute-start.9 = (bf16[1024,256]{1,0:T(8,128)(2,1)}, bf16[1024,256]{1,0:T(8,128)(2,1)}, u32[]{:S(2)}, u32[]{:S(2)}) collective-permute-start(bf16[1024,256]{1,0:T(8,128)(2,1)} %get-tuple-element.90), channel_id=1, source_target_pairs={{0,1},{1,0},{2,3},{3,2},{4,5},{5,4},{6,7},{7,6},{8,9},{9,8},{10,11... | collective-permute-start | bytes 1572872 | tf_op jit(solution)/shard_map/ppermute | solution.py:33
  37.8 0.8 copy-done.7
  38.5 2.7 %collective-permute-start.5 = (bf16[2,1152,128]{2,1,0:T(8,128)(2,1)}, bf16[2,1152,128]{2,1,0:T(8,128)(2,1)S(1)}, u32[]{:S(2)}, u32[]{:S(2)}) collective-permute-start(bf16[2,1152,128]{2,1,0:T(8,128)(2,1)} %collective-permute-done.3.b2), channel_id=1, source_target_pairs={{0,224},{8,232},{16,240},{24,248},{32,0},{40,8},{48,16},{56,24},{6... | collective-permute-start | bytes 1769480 | tf_op jit(solution)/shard_map/ppermute | solution.py:24
  41.2 3.6 %fusion.6 = (bf16[1024,256]{1,0:T(8,128)(2,1)}, bf16[1024,256]{1,0:T(8,128)(2,1)}, bf16[1024,256]{1,0:T(8,128)(2,1)}, bf16[1024,256]{1,0:T(8,128)(2,1)S(1)}) fusion(bf16[1024,256]{1,0:T(8,128)(2,1)} %collective-permute-done.9, bf16[1024,8,256]{2,0,1:T(8,128)(2,1)} %copy-done.6, s32[]{:T(128)S(6)} %select_n.90, bf16[1024,256]{1,0:T(8,128)(2,1)} %collective-permute-done.8, ...), kind=kLoop, calls=%fused_computation.5 | loop fusion | flops 4194304 | bytes 6291472 | tf_op jit(solution)/shard_map/convert_element_type | solution.py:243
  44.9 1.3 %collective-permute-start.15 = (bf16[1024,256]{1,0:T(8,128)(2,1)}, bf16[1024,256]{1,0:T(8,128)(2,1)}, u32[]{:S(2)}, u32[]{:S(2)}) collective-permute-start(bf16[1024,256]{1,0:T(8,128)(2,1)} %get-tuple-element.88), channel_id=1, source_target_pairs={{0,2},{1,3},{2,4},{3,5},{4,6},{5,7},{6,0},{7,1},{8,10},{9,11},{10,... | collective-permute-start | bytes 1572872 | tf_op jit(solution)/shard_map/ppermute | solution.py:29
  46.2 2.6 %collective-permute-start.16 = (bf16[1024,256]{1,0:T(8,128)(2,1)}, bf16[1024,256]{1,0:T(8,128)(2,1)}, u32[]{:S(2)}, u32[]{:S(2)}) collective-permute-start(bf16[1024,256]{1,0:T(8,128)(2,1)} %get-tuple-element.87), channel_id=1, source_target_pairs={{0,4},{1,5},{2,6},{3,7},{4,0},{5,1},{6,2},{7,3},{8,12},{9,13},{10,... | collective-permute-start | bytes 1572872 | tf_op jit(solution)/shard_map/ppermute | solution.py:29
  48.8 1.1 %collective-permute-start.17 = (bf16[1024,256]{1,0:T(8,128)(2,1)}, bf16[1024,256]{1,0:T(8,128)(2,1)}, u32[]{:S(2)}, u32[]{:S(2)}) collective-permute-start(bf16[1024,256]{1,0:T(8,128)(2,1)} %get-tuple-element.86), channel_id=1, source_target_pairs={{0,6},{1,7},{2,0},{3,1},{4,2},{5,3},{6,4},{7,5},{8,14},{9,15},{10,... | collective-permute-start | bytes 1572872 | tf_op jit(solution)/shard_map/ppermute | solution.py:29
  49.8 4.4 %collective-permute-done.4.f3 = bf16[2,1152,128]{2,1,0:T(8,128)(2,1)S(1)} collective-permute-done((bf16[2,1152,128]{2,1,0:T(8,128)(2,1)}, bf16[2,1152,128]{2,1,0:T(8,128)(2,1)S(1)}, u32[]{:S(2)}, u32[]{:S(2)}) %collective-permute-start.4) | collective-permute-done | bytes 589856 | tf_op jit(solution)/shard_map/ppermute | solution.py:24
  54.2 0.9 slice_bitcast_fusion
  55.1 3.2 %collective-permute-start.11 = (bf16[1152,128]{1,0:T(8,128)(2,1)}, bf16[1152,128]{1,0:T(8,128)(2,1)}, u32[]{:S(2)}, u32[]{:S(2)}) collective-permute-start(bf16[1152,128]{1,0:T(8,128)(2,1)} %get-tuple-element.56), channel_id=1, source_target_pairs={{0,224},{8,232},{16,240},{24,248},{32,0},{40,8},{48,16},{56,24},{6... | collective-permute-start | bytes 884744 | tf_op jit(solution)/shard_map/ppermute | solution.py:24
  58.3 1.8 %plan.1 = (s32[32]{0:T(128)S(1)}, s32[16]{0:T(128)S(1)}) custom-call(s32[512]{0:T(512)S(1)} %copy-done.2, s32[64]{0:T(128)S(1)} %copy-done.3), custom_call_target="tpu_custom_call" | custom-call | tf_op jit(solution)/shard_map/plan/pallas_call | solution.py:231
  60.1 3.5 %all-to-all-done.tok_ref = bf16[32,64,1024]{2,1,0:T(8,128)(2,1)} async-done(((bf16[32,64,1024]{2,1,0:T(8,128)(2,1)}), bf16[32,64,1024]{2,1,0:T(8,128)(2,1)}, u32[]{:S(2)}, u32[]{:S(2)}) %all-to-all-start) | async-done | bytes 4194336 | tf_op jit(solution)/shard_map/all_to_all | solution.py:38
  63.6 1.1 copy-done.1
  64.6 5.2 %rank.1 = (bf16[8,64,128]{2,1,0:T(8,128)(2,1)S(1)}, bf16[8,64,128]{2,1,0:T(8,128)(2,1)S(1)}, bf16[8,64,128]{2,1,0:T(8,128)(2,1)S(1)}, bf16[8,64,128]{2,1,0:T(8,1...) custom-call(s32[32]{0:T(128)S(1)} %get-tuple-element.47.choice_ref, ...), custom_call_target="tpu_custom_call" | custom-call | tf_op jit(solution)/shard_map/rank/pallas_call | solution.py:267
  69.9 2.0 %opposite.1 = (bf16[8,64,128]{2,1,0:T(8,128)(2,1)S(1)}, bf16[8,64,128]{2,1,0:T(8,128)(2,1)S(1)}, bf16[8,64,128]{2,1,0:T(8,128)(2,1)S(1)}, bf16[8,64,128]{2,1,0:T...) custom-call(s32[32]{0:T(128)S(1)} %get-tuple-element.47.choice_ref, ...), custom_call_target="tpu_custom_call", output_to_operand_aliasing={{0}: (4, {}), {1}: (5, {}), {2}: (6, {}), {3}: (7, {}), {4}... | custom-call | tf_op jit(solution)/shard_map/opposite/pallas_call | solution.py:283
  71.9 0.9 collective-permute-start.12
  72.8 1.2 %collective-permute-start.13 = (bf16[8,64,128]{2,1,0:T(8,128)(2,1)S(1)}, bf16[8,64,128]{2,1,0:T(8,128)(2,1)S(1)}, u32[]{:S(2)}, u32[]{:S(2)}) collective-permute-start(bf16[8,64,128]{2,1,0:T(8,128)(2,1)S(1)} %get-tuple-element.67), channel_id=1, source_target_pairs={{0,16},{8,24},{16,0},{24,8},{32,48},{40,56},{48,32},{56,40},{64,80... | collective-permute-start | bytes 393224 | tf_op jit(solution)/shard_map/ppermute | solution.py:19
  74.0 1.7 %collective-permute-done.12.g1 = bf16[8,64,128]{2,1,0:T(8,128)(2,1)S(1)} collective-permute-done((bf16[8,64,128]{2,1,0:T(8,128)(2,1)S(1)}, bf16[8,64,128]{2,1,0:T(8,128)(2,1)S(1)}, u32[]{:S(2)}, u32[]{:S(2)}) %collective-permute-start.12) | collective-permute-done | bytes 131104 | tf_op jit(solution)/shard_map/ppermute | solution.py:19
  75.7 2.4 %collective-permute-done.13.g2 = bf16[8,64,128]{2,1,0:T(8,128)(2,1)S(1)} collective-permute-done((bf16[8,64,128]{2,1,0:T(8,128)(2,1)S(1)}, bf16[8,64,128]{2,1,0:T(8,128)(2,1)S(1)}, u32[]{:S(2)}, u32[]{:S(2)}) %collective-permute-start.13) | collective-permute-done | bytes 131104 | tf_op jit(solution)/shard_map/ppermute | solution.py:19
  78.2 1.8 %collective-permute-done.14.g3 = bf16[8,64,128]{2,1,0:T(8,128)(2,1)S(1)} collective-permute-done((bf16[8,64,128]{2,1,0:T(8,128)(2,1)S(1)}, bf16[8,64,128]{2,1,0:T(8,128)(2,1)S(1)}, u32[]{:S(2)}, u32[]{:S(2)}) %collective-permute-start.14) | collective-permute-done | bytes 131104 | tf_op jit(solution)/shard_map/ppermute | solution.py:19
  79.9 0.7 unslot.1
  80.6 3.2 %collective-permute-start.18 = (bf16[8,64,128]{2,1,0:T(8,128)(2,1)S(1)}, bf16[8,64,128]{2,1,0:T(8,128)(2,1)S(1)}, u32[]{:S(2)}, u32[]{:S(2)}) collective-permute-start(bf16[8,64,128]{2,1,0:T(8,128)(2,1)S(1)} %get-tuple-element.74), channel_id=1, source_target_pairs={{0,1},{1,0},{2,3},{3,2},{4,5},{5,4},{6,7},{7,6},{8,9},{9,8},{10,11... | collective-permute-start | bytes 393224 | tf_op jit(solution)/shard_map/ppermute | solution.py:33
  83.8 0.3 collective-permute-start.22
  84.1 1.2 %collective-permute-start.23 = (bf16[8,128,128]{2,1,0:T(8,128)(2,1)}, bf16[8,128,128]{2,1,0:T(8,128)(2,1)S(1)}, u32[]{:S(2)}, u32[]{:S(2)}) collective-permute-start(bf16[8,128,128]{2,1,0:T(8,128)(2,1)} %get-tuple-element.77), channel_id=1, source_target_pairs={{0,16},{8,24},{16,0},{24,8},{32,48},{40,56},{48,32},{56,40},{64,80... | collective-permute-start | bytes 786440 | tf_op jit(solution)/shard_map/ppermute | solution.py:19
  85.3 0.6 collective-permute-start.24
  85.9 1.4 %collective-permute-start.19 = (bf16[8,64,128]{2,1,0:T(8,128)(2,1)S(1)}, bf16[8,64,128]{2,1,0:T(8,128)(2,1)S(1)}, u32[]{:S(2)}, u32[]{:S(2)}) collective-permute-start(bf16[8,64,128]{2,1,0:T(8,128)(2,1)S(1)} %add_convert_fusion.1), channel_id=1, source_target_pairs={{0,2},{1,3},{2,4},{3,5},{4,6},{5,7},{6,0},{7,1},{8,10},{9,11},{10,... | collective-permute-start | bytes 393224 | tf_op jit(solution)/shard_map/ppermute | solution.py:29
  87.3 2.6 %collective-permute-start.20 = (bf16[8,64,128]{2,1,0:T(8,128)(2,1)S(1)}, bf16[8,64,128]{2,1,0:T(8,128)(2,1)S(1)}, u32[]{:S(2)}, u32[]{:S(2)}) collective-permute-start(bf16[8,64,128]{2,1,0:T(8,128)(2,1)S(1)} %add_convert_fusion.1), channel_id=1, source_target_pairs={{0,4},{1,5},{2,6},{3,7},{4,0},{5,1},{6,2},{7,3},{8,12},{9,13},{10,... | collective-permute-start | bytes 393224 | tf_op jit(solution)/shard_map/ppermute | solution.py:29
  89.9 1.8 %collective-permute-done.22.u1 = bf16[8,128,128]{2,1,0:T(8,128)(2,1)S(1)} collective-permute-done((bf16[8,128,128]{2,1,0:T(8,128)(2,1)S(1)}, bf16[8,128,128]{2,1,0:T(8,128)(2,1)S(1)}, u32[]{:S(2)}, u32[]{:S(2)}) %collective-permute-start.22) | collective-permute-done | bytes 262176 | tf_op jit(solution)/shard_map/ppermute | solution.py:19
  91.7 2.7 %collective-permute-start.21 = (bf16[8,64,128]{2,1,0:T(8,128)(2,1)S(1)}, bf16[8,64,128]{2,1,0:T(8,128)(2,1)S(1)}, u32[]{:S(2)}, u32[]{:S(2)}) collective-permute-start(bf16[8,64,128]{2,1,0:T(8,128)(2,1)S(1)} %add_convert_fusion.1), channel_id=1, source_target_pairs={{0,6},{1,7},{2,0},{3,1},{4,2},{5,3},{6,4},{7,5},{8,14},{9,15},{10,... | collective-permute-start | bytes 393224 | tf_op jit(solution)/shard_map/ppermute | solution.py:29
  94.5 0.1 convert_element_type.123
  94.6 5.1 %collective-permute-done.24.u3 = bf16[8,128,128]{2,1,0:T(8,128)(2,1)S(1)} collective-permute-done((bf16[8,128,128]{2,1,0:T(8,128)(2,1)}, bf16[8,128,128]{2,1,0:T(8,128)(2,1)S(1)}, u32[]{:S(2)}, u32[]{:S(2)}) %collective-permute-start.24) | collective-permute-done | bytes 262176 | tf_op jit(solution)/shard_map/ppermute | solution.py:19
  99.7 0.1 add_convert_fusion.mine
  99.7 0.6 collective-permute-start.25
  100.3 1.9 %fusion.10 = (f32[1024,128]{1,0:T(8,128)S(1)}, f32[1024,128]{1,0:T(8,128)S(1)}) fusion(f32[128]{0:T(128)S(1)} %get-tuple-element.98, f32[128]{0:T(128)S(1)} %get-tuple-element.99, f32[1024]{0:T(1024)S(1)} %convert_element_type.123), kind=kLoop, calls=%fused_computation.15 | loop fusion | flops 262144 | bytes 1053696 | tf_op jit(solution)/shard_map/mul | solution.py:256
  102.3 4.5 %final.1 = bf16[1,1024,256]{2,1,0:T(8,128)(2,1)} custom-call(s32[16]{0:T(128)S(1)} %get-tuple-element.46.place_ref, s32[16]{0:T(128)S(1)} %copy-done.5, bf16[8,64,128]{2,1,0:T(8,128)(2,1)S(1)} %add_convert_fusion.mine, bf16[8,64,128]{2,1,0:T(8,128)(2,1)S(1)} %collective-permute-done.25.other, bf16[8,128,128]{2,1,0:T(8,128)(2,1)S(1)} %get-tuple-element.82.u0, ...), custom_call_target="tpu_custom_call" | custom-call | tf_op jit(solution)/shard_map/final/pallas_call | solution.py:320
  (41 shorter events, 0.2 us)
Async XLA Ops:
  1.1 19.5 %collective-permute-start = (bf16[2,1152,128]{2,1,0:T(8,128)(2,1)S(1)}, bf16[2,1152,128]{2,1,0:T(8,128)(2,1)S(1)}, u32[]{:S(2)}, u32[]{:S(2)}) collective-permute-start(bf16[2,1152,128]{2,1,0:T(8,128)(2,1)S(1)} %pad_maximum_fusion.own), channel_id=1, source_target_pairs={{0,32},{8,40},{16,48},{24,56},{32,64},{40,72},{48,80},{56,88},{64,... | collective-permute-start | bytes 1769480 | tf_op jit(solution)/shard_map/ppermute | solution.py:24
  3.7 17.0 %collective-permute-start.1 = (bf16[2,1152,128]{2,1,0:T(8,128)(2,1)S(1)}, bf16[2,1152,128]{2,1,0:T(8,128)(2,1)S(1)}, u32[]{:S(2)}, u32[]{:S(2)}) collective-permute-start(bf16[2,1152,128]{2,1,0:T(8,128)(2,1)S(1)} %pad_maximum_fusion.own), channel_id=1, source_target_pairs={{0,224},{8,232},{16,240},{24,248},{32,0},{40,8},{48,16},{56,24},{6... | collective-permute-start | bytes 1769480 | tf_op jit(solution)/shard_map/ppermute | solution.py:24
  10.7 52.8 %all-to-all-start = ((bf16[32,64,1024]{2,1,0:T(8,128)(2,1)}), bf16[32,64,1024]{2,1,0:T(8,128)(2,1)}, u32[]{:S(2)}, u32[]{:S(2)}) async-start(bf16[32,64,1024]{2,1,0:T(8,128)(2,1)} %pack.1), calls=%async_computation | async-start | bytes 8388608 | tf_op jit(solution)/shard_map/all_to_all | solution.py:38
  20.7 10.0 %copy-start = (bf16[2,1152,128]{2,1,0:T(8,128)(2,1)}, bf16[2,1152,128]{2,1,0:T(8,128)(2,1)S(1)}, u32[]{:S(2)}) copy-start(bf16[2,1152,128]{2,1,0:T(8,128)(2,1)S(1)} %collective-permute-done.1.b1) | copy-start | bytes 1769476
  20.7 14.9 %collective-permute-start.2 = (bf16[2,1152,128]{2,1,0:T(8,128)(2,1)S(1)}, bf16[2,1152,128]{2,1,0:T(8,128)(2,1)}, u32[]{:S(2)}, u32[]{:S(2)}) collective-permute-start(bf16[2,1152,128]{2,1,0:T(8,128)(2,1)S(1)} %collective-permute-done.f1), channel_id=1, source_target_pairs={{0,32},{8,40},{16,48},{24,56},{32,64},{40,72},{48,80},{56,88},{64,... | collective-permute-start | bytes 1769480 | tf_op jit(solution)/shard_map/ppermute | solution.py:24
  20.7 17.1 %collective-permute-start.3 = (bf16[2,1152,128]{2,1,0:T(8,128)(2,1)S(1)}, bf16[2,1152,128]{2,1,0:T(8,128)(2,1)}, u32[]{:S(2)}, u32[]{:S(2)}) collective-permute-start(bf16[2,1152,128]{2,1,0:T(8,128)(2,1)S(1)} %collective-permute-done.1.b1), channel_id=1, source_target_pairs={{0,224},{8,232},{16,240},{24,248},{32,0},{40,8},{48,16},{56,24},{6... | collective-permute-start | bytes 1769480 | tf_op jit(solution)/shard_map/ppermute | solution.py:24
  30.7 7.0 %copy-start.6 = (bf16[1024,8,256]{2,0,1:T(8,128)(2,1)}, bf16[1024,8,256]{2,0,1:T(8,128)(2,1)S(1)}, u32[]{:S(2)}) copy-start(bf16[1024,8,256]{2,0,1:T(8,128)(2,1)S(1)} %fusion.2) | copy-start | bytes 12582916
  32.0 26.3 %copy-start.2 = (s32[512]{0:T(512)S(1)}, s32[512]{0:T(512)}, u32[]{:S(2)}) copy-start(s32[512]{0:T(512)} %ca_ref.3) | copy-start | bytes 6148
  32.0 26.3 %copy-start.3 = (s32[64]{0:T(128)S(1)}, s32[64]{0:T(128)}, u32[]{:S(2)}) copy-start(s32[64]{0:T(128)} %table_ref.3) | copy-start | bytes 772
  32.0 5.7 %collective-permute-start.6 = (bf16[1024,256]{1,0:T(8,128)(2,1)S(1)}, bf16[1024,256]{1,0:T(8,128)(2,1)S(1)}, u32[]{:S(2)}, u32[]{:S(2)}) collective-permute-start(bf16[1024,256]{1,0:T(8,128)(2,1)S(1)} %get-tuple-element.93), channel_id=1, source_target_pairs={{0,1},{1,0},{2,3},{3,2},{4,5},{5,4},{6,7},{7,6},{8,9},{9,8},{10,11... | collective-permute-start | bytes 1572872 | tf_op jit(solution)/shard_map/ppermute | solution.py:33
  33.8 7.4 %collective-permute-start.7 = (bf16[1024,256]{1,0:T(8,128)(2,1)}, bf16[1024,256]{1,0:T(8,128)(2,1)}, u32[]{:S(2)}, u32[]{:S(2)}) collective-permute-start(bf16[1024,256]{1,0:T(8,128)(2,1)} %get-tuple-element.92), channel_id=1, source_target_pairs={{0,1},{1,0},{2,3},{3,2},{4,5},{5,4},{6,7},{7,6},{8,9},{9,8},{10,11... | collective-permute-start | bytes 1572872 | tf_op jit(solution)/shard_map/ppermute | solution.py:33
  33.9 7.3 %collective-permute-start.8 = (bf16[1024,256]{1,0:T(8,128)(2,1)}, bf16[1024,256]{1,0:T(8,128)(2,1)}, u32[]{:S(2)}, u32[]{:S(2)}) collective-permute-start(bf16[1024,256]{1,0:T(8,128)(2,1)} %get-tuple-element.91), channel_id=1, source_target_pairs={{0,1},{1,0},{2,3},{3,2},{4,5},{5,4},{6,7},{7,6},{8,9},{9,8},{10,11... | collective-permute-start | bytes 1572872 | tf_op jit(solution)/shard_map/ppermute | solution.py:33
  35.6 5.6 %collective-permute-start.9 = (bf16[1024,256]{1,0:T(8,128)(2,1)}, bf16[1024,256]{1,0:T(8,128)(2,1)}, u32[]{:S(2)}, u32[]{:S(2)}) collective-permute-start(bf16[1024,256]{1,0:T(8,128)(2,1)} %get-tuple-element.90), channel_id=1, source_target_pairs={{0,1},{1,0},{2,3},{3,2},{4,5},{5,4},{6,7},{7,6},{8,9},{9,8},{10,11... | collective-permute-start | bytes 1572872 | tf_op jit(solution)/shard_map/ppermute | solution.py:33
  37.7 16.5 %collective-permute-start.4 = (bf16[2,1152,128]{2,1,0:T(8,128)(2,1)}, bf16[2,1152,128]{2,1,0:T(8,128)(2,1)S(1)}, u32[]{:S(2)}, u32[]{:S(2)}) collective-permute-start(bf16[2,1152,128]{2,1,0:T(8,128)(2,1)} %collective-permute-done.2.f2), channel_id=1, source_target_pairs={{0,32},{8,40},{16,48},{24,56},{32,64},{40,72},{48,80},{56,88},{64,... | collective-permute-start | bytes 1769480 | tf_op jit(solution)/shard_map/ppermute | solution.py:24
  37.7 0.8 copy-start.7
  38.5 15.7 %collective-permute-start.5 = (bf16[2,1152,128]{2,1,0:T(8,128)(2,1)}, bf16[2,1152,128]{2,1,0:T(8,128)(2,1)S(1)}, u32[]{:S(2)}, u32[]{:S(2)}) collective-permute-start(bf16[2,1152,128]{2,1,0:T(8,128)(2,1)} %collective-permute-done.3.b2), channel_id=1, source_target_pairs={{0,224},{8,232},{16,240},{24,248},{32,0},{40,8},{48,16},{56,24},{6... | collective-permute-start | bytes 1769480 | tf_op jit(solution)/shard_map/ppermute | solution.py:24
  44.9 29.1 %collective-permute-start.15 = (bf16[1024,256]{1,0:T(8,128)(2,1)}, bf16[1024,256]{1,0:T(8,128)(2,1)}, u32[]{:S(2)}, u32[]{:S(2)}) collective-permute-start(bf16[1024,256]{1,0:T(8,128)(2,1)} %get-tuple-element.88), channel_id=1, source_target_pairs={{0,2},{1,3},{2,4},{3,5},{4,6},{5,7},{6,0},{7,1},{8,10},{9,11},{10,... | collective-permute-start | bytes 1572872 | tf_op jit(solution)/shard_map/ppermute | solution.py:29
  46.2 27.8 %collective-permute-start.16 = (bf16[1024,256]{1,0:T(8,128)(2,1)}, bf16[1024,256]{1,0:T(8,128)(2,1)}, u32[]{:S(2)}, u32[]{:S(2)}) collective-permute-start(bf16[1024,256]{1,0:T(8,128)(2,1)} %get-tuple-element.87), channel_id=1, source_target_pairs={{0,4},{1,5},{2,6},{3,7},{4,0},{5,1},{6,2},{7,3},{8,12},{9,13},{10,... | collective-permute-start | bytes 1572872 | tf_op jit(solution)/shard_map/ppermute | solution.py:29
  48.8 25.2 %collective-permute-start.17 = (bf16[1024,256]{1,0:T(8,128)(2,1)}, bf16[1024,256]{1,0:T(8,128)(2,1)}, u32[]{:S(2)}, u32[]{:S(2)}) collective-permute-start(bf16[1024,256]{1,0:T(8,128)(2,1)} %get-tuple-element.86), channel_id=1, source_target_pairs={{0,6},{1,7},{2,0},{3,1},{4,2},{5,3},{6,4},{7,5},{8,14},{9,15},{10,... | collective-permute-start | bytes 1572872 | tf_op jit(solution)/shard_map/ppermute | solution.py:29
  55.1 14.8 %collective-permute-start.10 = (bf16[1152,128]{1,0:T(8,128)(2,1)}, bf16[1152,128]{1,0:T(8,128)(2,1)S(1)}, u32[]{:S(2)}, u32[]{:S(2)}) collective-permute-start(bf16[1152,128]{1,0:T(8,128)(2,1)} %get-tuple-element.55), channel_id=1, source_target_pairs={{0,32},{8,40},{16,48},{24,56},{32,64},{40,72},{48,80},{56,88},{64,... | collective-permute-start | bytes 884744 | tf_op jit(solution)/shard_map/ppermute | solution.py:24
  55.1 14.8 %collective-permute-start.11 = (bf16[1152,128]{1,0:T(8,128)(2,1)}, bf16[1152,128]{1,0:T(8,128)(2,1)}, u32[]{:S(2)}, u32[]{:S(2)}) collective-permute-start(bf16[1152,128]{1,0:T(8,128)(2,1)} %get-tuple-element.56), channel_id=1, source_target_pairs={{0,224},{8,232},{16,240},{24,248},{32,0},{40,8},{48,16},{56,24},{6... | collective-permute-start | bytes 884744 | tf_op jit(solution)/shard_map/ppermute | solution.py:24
  63.6 1.1 copy-start.1
  69.9 24.5 %copy-start.8 = (s32[16]{0:T(128)S(1)}, s32[16]{0:T(128)}, u32[]{:S(2)}) copy-start(s32[16]{0:T(128)} %param.17) | copy-start | bytes 196
  69.9 32.3 %copy-start.4 = (bf16[1,256]{1,0:T(2,128)(2,1)S(1)}, bf16[1,256]{1,0:T(2,128)(2,1)}, u32[]{:S(2)}) copy-start(bf16[1,256]{1,0:T(2,128)(2,1)} %bias.1) | copy-start | bytes 1540
  69.9 32.3 %copy-start.5 = (s32[16]{0:T(128)S(1)}, s32[16]{0:T(128)}, u32[]{:S(2)}) copy-start(s32[16]{0:T(128)} %span_ref.1) | copy-start | bytes 196
  71.9 3.8 %collective-permute-start.12 = (bf16[8,64,128]{2,1,0:T(8,128)(2,1)S(1)}, bf16[8,64,128]{2,1,0:T(8,128)(2,1)S(1)}, u32[]{:S(2)}, u32[]{:S(2)}) collective-permute-start(bf16[8,64,128]{2,1,0:T(8,128)(2,1)S(1)} %get-tuple-element.66), channel_id=1, source_target_pairs={{0,24},{8,0},{16,8},{24,16},{32,56},{40,32},{48,40},{56,48},{64,88... | collective-permute-start | bytes 393224 | tf_op jit(solution)/shard_map/ppermute | solution.py:19
  72.8 5.4 %collective-permute-start.13 = (bf16[8,64,128]{2,1,0:T(8,128)(2,1)S(1)}, bf16[8,64,128]{2,1,0:T(8,128)(2,1)S(1)}, u32[]{:S(2)}, u32[]{:S(2)}) collective-permute-start(bf16[8,64,128]{2,1,0:T(8,128)(2,1)S(1)} %get-tuple-element.67), channel_id=1, source_target_pairs={{0,16},{8,24},{16,0},{24,8},{32,48},{40,56},{48,32},{56,40},{64,80... | collective-permute-start | bytes 393224 | tf_op jit(solution)/shard_map/ppermute | solution.py:19
  74.0 6.0 %collective-permute-start.14 = (bf16[8,64,128]{2,1,0:T(8,128)(2,1)S(1)}, bf16[8,64,128]{2,1,0:T(8,128)(2,1)S(1)}, u32[]{:S(2)}, u32[]{:S(2)}) collective-permute-start(bf16[8,64,128]{2,1,0:T(8,128)(2,1)S(1)} %get-tuple-element.68), channel_id=1, source_target_pairs={{0,8},{8,16},{16,24},{24,0},{32,40},{40,48},{48,56},{56,32},{64,72... | collective-permute-start | bytes 393224 | tf_op jit(solution)/shard_map/ppermute | solution.py:19
  80.6 5.2 %collective-permute-start.18 = (bf16[8,64,128]{2,1,0:T(8,128)(2,1)S(1)}, bf16[8,64,128]{2,1,0:T(8,128)(2,1)S(1)}, u32[]{:S(2)}, u32[]{:S(2)}) collective-permute-start(bf16[8,64,128]{2,1,0:T(8,128)(2,1)S(1)} %get-tuple-element.74), channel_id=1, source_target_pairs={{0,1},{1,0},{2,3},{3,2},{4,5},{5,4},{6,7},{7,6},{8,9},{9,8},{10,11... | collective-permute-start | bytes 393224 | tf_op jit(solution)/shard_map/ppermute | solution.py:33
  83.8 7.9 %collective-permute-start.22 = (bf16[8,128,128]{2,1,0:T(8,128)(2,1)S(1)}, bf16[8,128,128]{2,1,0:T(8,128)(2,1)S(1)}, u32[]{:S(2)}, u32[]{:S(2)}) collective-permute-start(bf16[8,128,128]{2,1,0:T(8,128)(2,1)S(1)} %get-tuple-element.76), channel_id=1, source_target_pairs={{0,24},{8,0},{16,8},{24,16},{32,56},{40,32},{48,40},{56,48},{64,88... | collective-permute-start | bytes 786440 | tf_op jit(solution)/shard_map/ppermute | solution.py:19
  84.1 10.5 %collective-permute-start.23 = (bf16[8,128,128]{2,1,0:T(8,128)(2,1)}, bf16[8,128,128]{2,1,0:T(8,128)(2,1)S(1)}, u32[]{:S(2)}, u32[]{:S(2)}) collective-permute-start(bf16[8,128,128]{2,1,0:T(8,128)(2,1)} %get-tuple-element.77), channel_id=1, source_target_pairs={{0,16},{8,24},{16,0},{24,8},{32,48},{40,56},{48,32},{56,40},{64,80... | collective-permute-start | bytes 786440 | tf_op jit(solution)/shard_map/ppermute | solution.py:19
  85.3 14.4 %collective-permute-start.24 = (bf16[8,128,128]{2,1,0:T(8,128)(2,1)}, bf16[8,128,128]{2,1,0:T(8,128)(2,1)S(1)}, u32[]{:S(2)}, u32[]{:S(2)}) collective-permute-start(bf16[8,128,128]{2,1,0:T(8,128)(2,1)} %get-tuple-element.78), channel_id=1, source_target_pairs={{0,8},{8,16},{16,24},{24,0},{32,40},{40,48},{48,56},{56,32},{64,72... | collective-permute-start | bytes 786440 | tf_op jit(solution)/shard_map/ppermute | solution.py:19
  85.9 13.8 %collective-permute-start.19 = (bf16[8,64,128]{2,1,0:T(8,128)(2,1)S(1)}, bf16[8,64,128]{2,1,0:T(8,128)(2,1)S(1)}, u32[]{:S(2)}, u32[]{:S(2)}) collective-permute-start(bf16[8,64,128]{2,1,0:T(8,128)(2,1)S(1)} %add_convert_fusion.1), channel_id=1, source_target_pairs={{0,2},{1,3},{2,4},{3,5},{4,6},{5,7},{6,0},{7,1},{8,10},{9,11},{10,... | collective-permute-start | bytes 393224 | tf_op jit(solution)/shard_map/ppermute | solution.py:29
  87.3 12.4 %collective-permute-start.20 = (bf16[8,64,128]{2,1,0:T(8,128)(2,1)S(1)}, bf16[8,64,128]{2,1,0:T(8,128)(2,1)S(1)}, u32[]{:S(2)}, u32[]{:S(2)}) collective-permute-start(bf16[8,64,128]{2,1,0:T(8,128)(2,1)S(1)} %add_convert_fusion.1), channel_id=1, source_target_pairs={{0,4},{1,5},{2,6},{3,7},{4,0},{5,1},{6,2},{7,3},{8,12},{9,13},{10,... | collective-permute-start | bytes 393224 | tf_op jit(solution)/shard_map/ppermute | solution.py:29
  91.7 8.0 %collective-permute-start.21 = (bf16[8,64,128]{2,1,0:T(8,128)(2,1)S(1)}, bf16[8,64,128]{2,1,0:T(8,128)(2,1)S(1)}, u32[]{:S(2)}, u32[]{:S(2)}) collective-permute-start(bf16[8,64,128]{2,1,0:T(8,128)(2,1)S(1)} %add_convert_fusion.1), channel_id=1, source_target_pairs={{0,6},{1,7},{2,0},{3,1},{4,2},{5,3},{6,4},{7,5},{8,14},{9,15},{10,... | collective-permute-start | bytes 393224 | tf_op jit(solution)/shard_map/ppermute | solution.py:29
  99.7 2.5 %collective-permute-start.25 = (bf16[8,64,128]{2,1,0:T(8,128)(2,1)S(1)}, bf16[8,64,128]{2,1,0:T(8,128)(2,1)S(1)}, u32[]{:S(2)}, u32[]{:S(2)}) collective-permute-start(bf16[8,64,128]{2,1,0:T(8,128)(2,1)S(1)} %add_convert_fusion.mine), channel_id=1, source_target_pairs={{0,1},{1,0},{2,3},{3,2},{4,5},{5,4},{6,7},{7,6},{8,9},{9,8},{10,11... | collective-permute-start | bytes 393224 | tf_op jit(solution)/shard_map/ppermute | solution.py:33

commit v4 on v3

--- a/solution.py
+++ b/solution.py
@@ -313,7 +313,7 @@
     mine = total_rank.astype(BF)
     other = swap_core(mine)
 
-    steps = 4
+    steps = 2
     base_spec = pl.BlockSpec((total // steps, width), lambda i, *_: (i, 0))
     trig_spec = pl.BlockSpec((total // steps, head), lambda i, *_: (i, 0))
     full = lambda a: pl.BlockSpec(a.shape, lambda i, *_: (0,) * a.ndim)

time: 107 us -> 106 us (level)
  Pallas kernels: 17.2 us -> 16 us
    pallas_call x1, Pallas kernels: 4.5 us -> 3.3 us  [body(): pl.pallas_call(final_kernel, out_shape=jax.ShapeDtypeStruct((1, total, wi...]
where the time goes in v4:
time: 106 us
  starting transfers between devices  44.2 us (42%)
  waiting for transfers between devices  26.9 us (25%)
  Pallas kernels  16 us (15%)
  matrix products  7.33 us (7%)
  other arithmetic  6.84 us (6%)
  local copies, waits for them, and re-layouts  4.12 us (4%)
    ppermute x8, starting transfers between devices, shift_z(): return lax.ppermute(v, 'dp', pairs)  15.1 us
    ppermute x6, waiting for transfers between devices, shift_x(): return lax.ppermute(v, 'dp', pairs)  12.8 us
    ppermute x6, starting transfers between devices, shift_y(): return lax.ppermute(v, 'tensor', pairs)  11.7 us
    ppermute x8, waiting for transfers between devices, shift_z(): return lax.ppermute(v, 'dp', pairs)  10.7 us
    ppermute x6, starting transfers between devices, swap_core(): return lax.ppermute(v, 'tensor', [(t, t ^ 1) for t in range(NY * NC)])  8.4 us
    dot_general x1, matrix products, body(): jnp.einsum('td,dhe->hte', tokens, key_value_weight, preferred_element_typ...  7.33 us
    pallas_call x1, Pallas kernels, body(): pl.pallas_call(rank_kernel, out_shape=[small] * NX + [blocks] * NX, in_sp...  5.21 us
    all_to_all x1, starting transfers between devices, exchange_x(): return lax.all_to_all(v, 'dp', 0, 0, tiled=True, axis_index_groups=groups)  4.88 us
  transfers between devices with their start and end apart: 27, of which 9 were waited for; matrix products, arithmetic and copies ran while one was open for 14% of the time, Pallas kernels for 11%

profile of v4, /device:TPU:1, one launch (start us, length us, event | category | flops | bytes accessed | tf_op | source)
XLA Modules:
  0.0 105.7 jit_solution(9389320525503800722)
XLA Ops:
  0.0 1.1 %pad_maximum_fusion.own = bf16[2,1152,128]{2,1,0:T(8,128)(2,1)S(1)} fusion(bf16[2,128,128]{2,1,0:T(8,128)(2,1)} %bitcast.31, bf16[2,1024,128]{2,1,0:T(8,128)(2,1)} %param.12), kind=kLoop, calls=%fused_computation.14 | loop fusion | flops 1179648 | bytes 1179648 | tf_op jit(solution)/shard_map/concatenate | solution.py:216
  1.1 2.5 %collective-permute-start = (bf16[2,1152,128]{2,1,0:T(8,128)(2,1)S(1)}, bf16[2,1152,128]{2,1,0:T(8,128)(2,1)S(1)}, u32[]{:S(2)}, u32[]{:S(2)}) collective-permute-start(bf16[2,1152,128]{2,1,0:T(8,128)(2,1)S(1)} %pad_maximum_fusion.own), channel_id=1, source_target_pairs={{0,32},{8,40},{16,48},{24,56},{32,64},{40,72},{48,80},{56,88},{64,... | collective-permute-start | bytes 1769480 | tf_op jit(solution)/shard_map/ppermute | solution.py:24
  3.7 4.0 %collective-permute-start.1 = (bf16[2,1152,128]{2,1,0:T(8,128)(2,1)S(1)}, bf16[2,1152,128]{2,1,0:T(8,128)(2,1)S(1)}, u32[]{:S(2)}, u32[]{:S(2)}) collective-permute-start(bf16[2,1152,128]{2,1,0:T(8,128)(2,1)S(1)} %pad_maximum_fusion.own), channel_id=1, source_target_pairs={{0,224},{8,232},{16,240},{24,248},{32,0},{40,8},{48,16},{56,24},{6... | collective-permute-start | bytes 1769480 | tf_op jit(solution)/shard_map/ppermute | solution.py:24
  7.7 3.0 %pack.1 = bf16[32,64,1024]{2,1,0:T(8,128)(2,1)} custom-call(s32[512]{0:T(512)} %ca_ref.3, s32[64]{0:T(128)} %table_ref.3, bf16[16,64,1024]{2,1,0:T(8,128)(2,1)} %bitcast.30), custom_call_target="tpu_custom_call" | custom-call | tf_op jit(solution)/shard_map/pack/pallas_call | solution.py:206
  10.7 4.9 %all-to-all-start = ((bf16[32,64,1024]{2,1,0:T(8,128)(2,1)}), bf16[32,64,1024]{2,1,0:T(8,128)(2,1)}, u32[]{:S(2)}, u32[]{:S(2)}) async-start(bf16[32,64,1024]{2,1,0:T(8,128)(2,1)} %pack.1), calls=%async_computation | async-start | bytes 8388608 | tf_op jit(solution)/shard_map/all_to_all | solution.py:38
  15.7 5.0 %collective-permute-done.f1 = bf16[2,1152,128]{2,1,0:T(8,128)(2,1)S(1)} collective-permute-done((bf16[2,1152,128]{2,1,0:T(8,128)(2,1)S(1)}, bf16[2,1152,128]{2,1,0:T(8,128)(2,1)S(1)}, u32[]{:S(2)}, u32[]{:S(2)}) %collective-permute-start) | collective-permute-done | bytes 589856 | tf_op jit(solution)/shard_map/ppermute | solution.py:24
  20.7 2.7 %collective-permute-start.3 = (bf16[2,1152,128]{2,1,0:T(8,128)(2,1)S(1)}, bf16[2,1152,128]{2,1,0:T(8,128)(2,1)}, u32[]{:S(2)}, u32[]{:S(2)}) collective-permute-start(bf16[2,1152,128]{2,1,0:T(8,128)(2,1)S(1)} %collective-permute-done.1.b1), channel_id=1, source_target_pairs={{0,224},{8,232},{16,240},{24,248},{32,0},{40,8},{48,16},{56,24},{6... | collective-permute-start | bytes 1769480 | tf_op jit(solution)/shard_map/ppermute | solution.py:24
  23.3 7.3 %fusion.2 = bf16[1024,8,256]{2,0,1:T(8,128)(2,1)S(1)} fusion(bf16[1024,8,256]{2,1,0:T(8,128)(2,1)} %param.10, bf16[1024,1024]{1,0:T(8,128)(2,1)} %param.9), kind=kOutput, calls=%fused_computation.2 | convolution fusion | flops 4297064448 | bytes 10485760 | tf_op jit(solution)/shard_map/td,dhe->hte/dot_general | solution.py:221
  30.7 1.3 %dynamic-slice_bitcast_fusion = (bf16[1024,256]{1,0:T(8,128)(2,1)}, bf16[1024,256]{1,0:T(8,128)(2,1)}, bf16[1024,256]{1,0:T(8,128)(2,1)}, bf16[1024,256]{1,0:T(8,128)(2,1)S(1)}) fusion(bf16[1024,8,256]{2,0,1:T(8,128)(2,1)S(1)} %fusion.2, s32[]{:T(128)S(6)} %select_n.91, s32[]{:T(128)S(6)} %select_n.88, s32[]{:T(128)S(6)} %select_n.85, s32[]{:T(128)S(6)} %select_n.82), kind=kLoop, calls=%fused_computation.16 | loop fusion | bytes 4194320 | tf_op jit(solution)/shard_map/jit(dynamic_index_in_dim)/squeeze | solution.py:226
  32.0 1.8 %collective-permute-start.6 = (bf16[1024,256]{1,0:T(8,128)(2,1)S(1)}, bf16[1024,256]{1,0:T(8,128)(2,1)S(1)}, u32[]{:S(2)}, u32[]{:S(2)}) collective-permute-start(bf16[1024,256]{1,0:T(8,128)(2,1)S(1)} %get-tuple-element.93), channel_id=1, source_target_pairs={{0,1},{1,0},{2,3},{3,2},{4,5},{5,4},{6,7},{7,6},{8,9},{9,8},{10,11... | collective-permute-start | bytes 1572872 | tf_op jit(solution)/shard_map/ppermute | solution.py:33
  33.8 0.1 collective-permute-start.7
  33.9 0.4 collective-permute-start.8
  34.3 1.3 %collective-permute-done.2.f2 = bf16[2,1152,128]{2,1,0:T(8,128)(2,1)} collective-permute-done((bf16[2,1152,128]{2,1,0:T(8,128)(2,1)S(1)}, bf16[2,1152,128]{2,1,0:T(8,128)(2,1)}, u32[]{:S(2)}, u32[]{:S(2)}) %collective-permute-start.2) | collective-permute-done | bytes 589856 | tf_op jit(solution)/shard_map/ppermute | solution.py:24
  35.6 2.1 %collective-permute-start.9 = (bf16[1024,256]{1,0:T(8,128)(2,1)}, bf16[1024,256]{1,0:T(8,128)(2,1)}, u32[]{:S(2)}, u32[]{:S(2)}) collective-permute-start(bf16[1024,256]{1,0:T(8,128)(2,1)} %get-tuple-element.90), channel_id=1, source_target_pairs={{0,1},{1,0},{2,3},{3,2},{4,5},{5,4},{6,7},{7,6},{8,9},{9,8},{10,11... | collective-permute-start | bytes 1572872 | tf_op jit(solution)/shard_map/ppermute | solution.py:33
  37.8 0.8 copy-done.7
  38.5 2.7 %collective-permute-start.5 = (bf16[2,1152,128]{2,1,0:T(8,128)(2,1)}, bf16[2,1152,128]{2,1,0:T(8,128)(2,1)S(1)}, u32[]{:S(2)}, u32[]{:S(2)}) collective-permute-start(bf16[2,1152,128]{2,1,0:T(8,128)(2,1)} %collective-permute-done.3.b2), channel_id=1, source_target_pairs={{0,224},{8,232},{16,240},{24,248},{32,0},{40,8},{48,16},{56,24},{6... | collective-permute-start | bytes 1769480 | tf_op jit(solution)/shard_map/ppermute | solution.py:24
  41.2 3.6 %fusion.6 = (bf16[1024,256]{1,0:T(8,128)(2,1)}, bf16[1024,256]{1,0:T(8,128)(2,1)}, bf16[1024,256]{1,0:T(8,128)(2,1)}, bf16[1024,256]{1,0:T(8,128)(2,1)S(1)}) fusion(bf16[1024,256]{1,0:T(8,128)(2,1)} %collective-permute-done.9, bf16[1024,8,256]{2,0,1:T(8,128)(2,1)} %copy-done.6, s32[]{:T(128)S(6)} %select_n.90, bf16[1024,256]{1,0:T(8,128)(2,1)} %collective-permute-done.8, ...), kind=kLoop, calls=%fused_computation.5 | loop fusion | flops 4194304 | bytes 6291472 | tf_op jit(solution)/shard_map/convert_element_type | solution.py:243
  44.9 1.3 %collective-permute-start.15 = (bf16[1024,256]{1,0:T(8,128)(2,1)}, bf16[1024,256]{1,0:T(8,128)(2,1)}, u32[]{:S(2)}, u32[]{:S(2)}) collective-permute-start(bf16[1024,256]{1,0:T(8,128)(2,1)} %get-tuple-element.88), channel_id=1, source_target_pairs={{0,2},{1,3},{2,4},{3,5},{4,6},{5,7},{6,0},{7,1},{8,10},{9,11},{10,... | collective-permute-start | bytes 1572872 | tf_op jit(solution)/shard_map/ppermute | solution.py:29
  46.2 2.6 %collective-permute-start.16 = (bf16[1024,256]{1,0:T(8,128)(2,1)}, bf16[1024,256]{1,0:T(8,128)(2,1)}, u32[]{:S(2)}, u32[]{:S(2)}) collective-permute-start(bf16[1024,256]{1,0:T(8,128)(2,1)} %get-tuple-element.87), channel_id=1, source_target_pairs={{0,4},{1,5},{2,6},{3,7},{4,0},{5,1},{6,2},{7,3},{8,12},{9,13},{10,... | collective-permute-start | bytes 1572872 | tf_op jit(solution)/shard_map/ppermute | solution.py:29
  48.8 1.1 %collective-permute-start.17 = (bf16[1024,256]{1,0:T(8,128)(2,1)}, bf16[1024,256]{1,0:T(8,128)(2,1)}, u32[]{:S(2)}, u32[]{:S(2)}) collective-permute-start(bf16[1024,256]{1,0:T(8,128)(2,1)} %get-tuple-element.86), channel_id=1, source_target_pairs={{0,6},{1,7},{2,0},{3,1},{4,2},{5,3},{6,4},{7,5},{8,14},{9,15},{10,... | collective-permute-start | bytes 1572872 | tf_op jit(solution)/shard_map/ppermute | solution.py:29
  49.8 4.4 %collective-permute-done.4.f3 = bf16[2,1152,128]{2,1,0:T(8,128)(2,1)S(1)} collective-permute-done((bf16[2,1152,128]{2,1,0:T(8,128)(2,1)}, bf16[2,1152,128]{2,1,0:T(8,128)(2,1)S(1)}, u32[]{:S(2)}, u32[]{:S(2)}) %collective-permute-start.4) | collective-permute-done | bytes 589856 | tf_op jit(solution)/shard_map/ppermute | solution.py:24
  54.2 0.9 slice_bitcast_fusion
  55.1 3.2 %collective-permute-start.11 = (bf16[1152,128]{1,0:T(8,128)(2,1)}, bf16[1152,128]{1,0:T(8,128)(2,1)}, u32[]{:S(2)}, u32[]{:S(2)}) collective-permute-start(bf16[1152,128]{1,0:T(8,128)(2,1)} %get-tuple-element.56), channel_id=1, source_target_pairs={{0,224},{8,232},{16,240},{24,248},{32,0},{40,8},{48,16},{56,24},{6... | collective-permute-start | bytes 884744 | tf_op jit(solution)/shard_map/ppermute | solution.py:24
  58.3 1.8 %plan.1 = (s32[32]{0:T(128)S(1)}, s32[16]{0:T(128)S(1)}) custom-call(s32[512]{0:T(512)S(1)} %copy-done.2, s32[64]{0:T(128)S(1)} %copy-done.3), custom_call_target="tpu_custom_call" | custom-call | tf_op jit(solution)/shard_map/plan/pallas_call | solution.py:231
  60.1 3.4 %all-to-all-done.tok_ref = bf16[32,64,1024]{2,1,0:T(8,128)(2,1)} async-done(((bf16[32,64,1024]{2,1,0:T(8,128)(2,1)}), bf16[32,64,1024]{2,1,0:T(8,128)(2,1)}, u32[]{:S(2)}, u32[]{:S(2)}) %all-to-all-start) | async-done | bytes 4194336 | tf_op jit(solution)/shard_map/all_to_all | solution.py:38
  63.5 1.1 %copy-done.1 = bf16[2,1152,128]{2,1,0:T(8,128)(2,1)S(1)} copy-done((bf16[2,1152,128]{2,1,0:T(8,128)(2,1)S(1)}, bf16[2,1152,128]{2,1,0:T(8,128)(2,1)}, u32[]{:S(2)}) %copy-start.1) | copy-done | bytes 589848
  64.6 5.2 %rank.1 = (bf16[8,64,128]{2,1,0:T(8,128)(2,1)S(1)}, bf16[8,64,128]{2,1,0:T(8,128)(2,1)S(1)}, bf16[8,64,128]{2,1,0:T(8,128)(2,1)S(1)}, bf16[8,64,128]{2,1,0:T(8,1...) custom-call(s32[32]{0:T(128)S(1)} %get-tuple-element.47.choice_ref, ...), custom_call_target="tpu_custom_call" | custom-call | tf_op jit(solution)/shard_map/rank/pallas_call | solution.py:267
  69.9 2.0 %opposite.1 = (bf16[8,64,128]{2,1,0:T(8,128)(2,1)S(1)}, bf16[8,64,128]{2,1,0:T(8,128)(2,1)S(1)}, bf16[8,64,128]{2,1,0:T(8,128)(2,1)S(1)}, bf16[8,64,128]{2,1,0:T...) custom-call(s32[32]{0:T(128)S(1)} %get-tuple-element.47.choice_ref, ...), custom_call_target="tpu_custom_call", output_to_operand_aliasing={{0}: (4, {}), {1}: (5, {}), {2}: (6, {}), {3}: (7, {}), {4}... | custom-call | tf_op jit(solution)/shard_map/opposite/pallas_call | solution.py:283
  71.8 0.9 collective-permute-start.12
  72.7 1.2 %collective-permute-start.13 = (bf16[8,64,128]{2,1,0:T(8,128)(2,1)S(1)}, bf16[8,64,128]{2,1,0:T(8,128)(2,1)S(1)}, u32[]{:S(2)}, u32[]{:S(2)}) collective-permute-start(bf16[8,64,128]{2,1,0:T(8,128)(2,1)S(1)} %get-tuple-element.67), channel_id=1, source_target_pairs={{0,16},{8,24},{16,0},{24,8},{32,48},{40,56},{48,32},{56,40},{64,80... | collective-permute-start | bytes 393224 | tf_op jit(solution)/shard_map/ppermute | solution.py:19
  73.9 1.7 %collective-permute-done.12.g1 = bf16[8,64,128]{2,1,0:T(8,128)(2,1)S(1)} collective-permute-done((bf16[8,64,128]{2,1,0:T(8,128)(2,1)S(1)}, bf16[8,64,128]{2,1,0:T(8,128)(2,1)S(1)}, u32[]{:S(2)}, u32[]{:S(2)}) %collective-permute-start.12) | collective-permute-done | bytes 131104 | tf_op jit(solution)/shard_map/ppermute | solution.py:19
  75.6 2.4 %collective-permute-done.13.g2 = bf16[8,64,128]{2,1,0:T(8,128)(2,1)S(1)} collective-permute-done((bf16[8,64,128]{2,1,0:T(8,128)(2,1)S(1)}, bf16[8,64,128]{2,1,0:T(8,128)(2,1)S(1)}, u32[]{:S(2)}, u32[]{:S(2)}) %collective-permute-start.13) | collective-permute-done | bytes 131104 | tf_op jit(solution)/shard_map/ppermute | solution.py:19
  78.1 1.8 %collective-permute-done.14.g3 = bf16[8,64,128]{2,1,0:T(8,128)(2,1)S(1)} collective-permute-done((bf16[8,64,128]{2,1,0:T(8,128)(2,1)S(1)}, bf16[8,64,128]{2,1,0:T(8,128)(2,1)S(1)}, u32[]{:S(2)}, u32[]{:S(2)}) %collective-permute-start.14) | collective-permute-done | bytes 131104 | tf_op jit(solution)/shard_map/ppermute | solution.py:19
  79.9 0.7 unslot.1
  80.6 3.1 %collective-permute-start.18 = (bf16[8,64,128]{2,1,0:T(8,128)(2,1)S(1)}, bf16[8,64,128]{2,1,0:T(8,128)(2,1)S(1)}, u32[]{:S(2)}, u32[]{:S(2)}) collective-permute-start(bf16[8,64,128]{2,1,0:T(8,128)(2,1)S(1)} %get-tuple-element.74), channel_id=1, source_target_pairs={{0,1},{1,0},{2,3},{3,2},{4,5},{5,4},{6,7},{7,6},{8,9},{9,8},{10,11... | collective-permute-start | bytes 393224 | tf_op jit(solution)/shard_map/ppermute | solution.py:33
  83.7 0.3 collective-permute-start.22
  84.0 1.2 %collective-permute-start.23 = (bf16[8,128,128]{2,1,0:T(8,128)(2,1)}, bf16[8,128,128]{2,1,0:T(8,128)(2,1)S(1)}, u32[]{:S(2)}, u32[]{:S(2)}) collective-permute-start(bf16[8,128,128]{2,1,0:T(8,128)(2,1)} %get-tuple-element.77), channel_id=1, source_target_pairs={{0,16},{8,24},{16,0},{24,8},{32,48},{40,56},{48,32},{56,40},{64,80... | collective-permute-start | bytes 786440 | tf_op jit(solution)/shard_map/ppermute | solution.py:19
  85.2 0.6 collective-permute-start.24
  85.8 1.4 %collective-permute-start.19 = (bf16[8,64,128]{2,1,0:T(8,128)(2,1)S(1)}, bf16[8,64,128]{2,1,0:T(8,128)(2,1)S(1)}, u32[]{:S(2)}, u32[]{:S(2)}) collective-permute-start(bf16[8,64,128]{2,1,0:T(8,128)(2,1)S(1)} %add_convert_fusion.1), channel_id=1, source_target_pairs={{0,2},{1,3},{2,4},{3,5},{4,6},{5,7},{6,0},{7,1},{8,10},{9,11},{10,... | collective-permute-start | bytes 393224 | tf_op jit(solution)/shard_map/ppermute | solution.py:29
  87.2 2.6 %collective-permute-start.20 = (bf16[8,64,128]{2,1,0:T(8,128)(2,1)S(1)}, bf16[8,64,128]{2,1,0:T(8,128)(2,1)S(1)}, u32[]{:S(2)}, u32[]{:S(2)}) collective-permute-start(bf16[8,64,128]{2,1,0:T(8,128)(2,1)S(1)} %add_convert_fusion.1), channel_id=1, source_target_pairs={{0,4},{1,5},{2,6},{3,7},{4,0},{5,1},{6,2},{7,3},{8,12},{9,13},{10,... | collective-permute-start | bytes 393224 | tf_op jit(solution)/shard_map/ppermute | solution.py:29
  89.8 1.8 %collective-permute-done.22.u1 = bf16[8,128,128]{2,1,0:T(8,128)(2,1)S(1)} collective-permute-done((bf16[8,128,128]{2,1,0:T(8,128)(2,1)S(1)}, bf16[8,128,128]{2,1,0:T(8,128)(2,1)S(1)}, u32[]{:S(2)}, u32[]{:S(2)}) %collective-permute-start.22) | collective-permute-done | bytes 262176 | tf_op jit(solution)/shard_map/ppermute | solution.py:19
  91.6 2.7 %collective-permute-start.21 = (bf16[8,64,128]{2,1,0:T(8,128)(2,1)S(1)}, bf16[8,64,128]{2,1,0:T(8,128)(2,1)S(1)}, u32[]{:S(2)}, u32[]{:S(2)}) collective-permute-start(bf16[8,64,128]{2,1,0:T(8,128)(2,1)S(1)} %add_convert_fusion.1), channel_id=1, source_target_pairs={{0,6},{1,7},{2,0},{3,1},{4,2},{5,3},{6,4},{7,5},{8,14},{9,15},{10,... | collective-permute-start | bytes 393224 | tf_op jit(solution)/shard_map/ppermute | solution.py:29
  94.4 0.1 convert_element_type.123
  94.5 5.1 %collective-permute-done.24.u3 = bf16[8,128,128]{2,1,0:T(8,128)(2,1)S(1)} collective-permute-done((bf16[8,128,128]{2,1,0:T(8,128)(2,1)}, bf16[8,128,128]{2,1,0:T(8,128)(2,1)S(1)}, u32[]{:S(2)}, u32[]{:S(2)}) %collective-permute-start.24) | collective-permute-done | bytes 262176 | tf_op jit(solution)/shard_map/ppermute | solution.py:19
  99.6 0.1 add_convert_fusion.mine
  99.7 0.8 collective-permute-start.25
  100.5 1.9 %fusion.10 = (f32[1024,128]{1,0:T(8,128)S(1)}, f32[1024,128]{1,0:T(8,128)S(1)}) fusion(f32[128]{0:T(128)S(1)} %get-tuple-element.98, f32[128]{0:T(128)S(1)} %get-tuple-element.99, f32[1024]{0:T(1024)S(1)} %convert_element_type.123), kind=kLoop, calls=%fused_computation.15 | loop fusion | flops 262144 | bytes 1053696 | tf_op jit(solution)/shard_map/mul | solution.py:256
  102.4 3.3 %final.1 = bf16[1,1024,256]{2,1,0:T(8,128)(2,1)} custom-call(s32[16]{0:T(128)S(1)} %get-tuple-element.46.place_ref, s32[16]{0:T(128)S(1)} %copy-done.5, bf16[8,64,128]{2,1,0:T(8,128)(2,1)S(1)} %add_convert_fusion.mine, bf16[8,64,128]{2,1,0:T(8,128)(2,1)S(1)} %collective-permute-done.25.other, bf16[8,128,128]{2,1,0:T(8,128)(2,1)S(1)} %get-tuple-element.82.u0, ...), custom_call_target="tpu_custom_call" | custom-call | tf_op jit(solution)/shard_map/final/pallas_call | solution.py:320
  (41 shorter events, 0.2 us)
Async XLA Ops:
  1.1 19.5 %collective-permute-start = (bf16[2,1152,128]{2,1,0:T(8,128)(2,1)S(1)}, bf16[2,1152,128]{2,1,0:T(8,128)(2,1)S(1)}, u32[]{:S(2)}, u32[]{:S(2)}) collective-permute-start(bf16[2,1152,128]{2,1,0:T(8,128)(2,1)S(1)} %pad_maximum_fusion.own), channel_id=1, source_target_pairs={{0,32},{8,40},{16,48},{24,56},{32,64},{40,72},{48,80},{56,88},{64,... | collective-permute-start | bytes 1769480 | tf_op jit(solution)/shard_map/ppermute | solution.py:24
  3.7 17.0 %collective-permute-start.1 = (bf16[2,1152,128]{2,1,0:T(8,128)(2,1)S(1)}, bf16[2,1152,128]{2,1,0:T(8,128)(2,1)S(1)}, u32[]{:S(2)}, u32[]{:S(2)}) collective-permute-start(bf16[2,1152,128]{2,1,0:T(8,128)(2,1)S(1)} %pad_maximum_fusion.own), channel_id=1, source_target_pairs={{0,224},{8,232},{16,240},{24,248},{32,0},{40,8},{48,16},{56,24},{6... | collective-permute-start | bytes 1769480 | tf_op jit(solution)/shard_map/ppermute | solution.py:24
  10.7 52.8 %all-to-all-start = ((bf16[32,64,1024]{2,1,0:T(8,128)(2,1)}), bf16[32,64,1024]{2,1,0:T(8,128)(2,1)}, u32[]{:S(2)}, u32[]{:S(2)}) async-start(bf16[32,64,1024]{2,1,0:T(8,128)(2,1)} %pack.1), calls=%async_computation | async-start | bytes 8388608 | tf_op jit(solution)/shard_map/all_to_all | solution.py:38
  20.7 10.0 %copy-start = (bf16[2,1152,128]{2,1,0:T(8,128)(2,1)}, bf16[2,1152,128]{2,1,0:T(8,128)(2,1)S(1)}, u32[]{:S(2)}) copy-start(bf16[2,1152,128]{2,1,0:T(8,128)(2,1)S(1)} %collective-permute-done.1.b1) | copy-start | bytes 1769476
  20.7 14.9 %collective-permute-start.2 = (bf16[2,1152,128]{2,1,0:T(8,128)(2,1)S(1)}, bf16[2,1152,128]{2,1,0:T(8,128)(2,1)}, u32[]{:S(2)}, u32[]{:S(2)}) collective-permute-start(bf16[2,1152,128]{2,1,0:T(8,128)(2,1)S(1)} %collective-permute-done.f1), channel_id=1, source_target_pairs={{0,32},{8,40},{16,48},{24,56},{32,64},{40,72},{48,80},{56,88},{64,... | collective-permute-start | bytes 1769480 | tf_op jit(solution)/shard_map/ppermute | solution.py:24
  20.7 17.1 %collective-permute-start.3 = (bf16[2,1152,128]{2,1,0:T(8,128)(2,1)S(1)}, bf16[2,1152,128]{2,1,0:T(8,128)(2,1)}, u32[]{:S(2)}, u32[]{:S(2)}) collective-permute-start(bf16[2,1152,128]{2,1,0:T(8,128)(2,1)S(1)} %collective-permute-done.1.b1), channel_id=1, source_target_pairs={{0,224},{8,232},{16,240},{24,248},{32,0},{40,8},{48,16},{56,24},{6... | collective-permute-start | bytes 1769480 | tf_op jit(solution)/shard_map/ppermute | solution.py:24
  30.7 7.0 %copy-start.6 = (bf16[1024,8,256]{2,0,1:T(8,128)(2,1)}, bf16[1024,8,256]{2,0,1:T(8,128)(2,1)S(1)}, u32[]{:S(2)}) copy-start(bf16[1024,8,256]{2,0,1:T(8,128)(2,1)S(1)} %fusion.2) | copy-start | bytes 12582916
  32.0 26.3 %copy-start.2 = (s32[512]{0:T(512)S(1)}, s32[512]{0:T(512)}, u32[]{:S(2)}) copy-start(s32[512]{0:T(512)} %ca_ref.3) | copy-start | bytes 6148
  32.0 26.3 %copy-start.3 = (s32[64]{0:T(128)S(1)}, s32[64]{0:T(128)}, u32[]{:S(2)}) copy-start(s32[64]{0:T(128)} %table_ref.3) | copy-start | bytes 772
  32.0 5.7 %collective-permute-start.6 = (bf16[1024,256]{1,0:T(8,128)(2,1)S(1)}, bf16[1024,256]{1,0:T(8,128)(2,1)S(1)}, u32[]{:S(2)}, u32[]{:S(2)}) collective-permute-start(bf16[1024,256]{1,0:T(8,128)(2,1)S(1)} %get-tuple-element.93), channel_id=1, source_target_pairs={{0,1},{1,0},{2,3},{3,2},{4,5},{5,4},{6,7},{7,6},{8,9},{9,8},{10,11... | collective-permute-start | bytes 1572872 | tf_op jit(solution)/shard_map/ppermute | solution.py:33
  33.8 7.4 %collective-permute-start.7 = (bf16[1024,256]{1,0:T(8,128)(2,1)}, bf16[1024,256]{1,0:T(8,128)(2,1)}, u32[]{:S(2)}, u32[]{:S(2)}) collective-permute-start(bf16[1024,256]{1,0:T(8,128)(2,1)} %get-tuple-element.92), channel_id=1, source_target_pairs={{0,1},{1,0},{2,3},{3,2},{4,5},{5,4},{6,7},{7,6},{8,9},{9,8},{10,11... | collective-permute-start | bytes 1572872 | tf_op jit(solution)/shard_map/ppermute | solution.py:33
  33.9 7.3 %collective-permute-start.8 = (bf16[1024,256]{1,0:T(8,128)(2,1)}, bf16[1024,256]{1,0:T(8,128)(2,1)}, u32[]{:S(2)}, u32[]{:S(2)}) collective-permute-start(bf16[1024,256]{1,0:T(8,128)(2,1)} %get-tuple-element.91), channel_id=1, source_target_pairs={{0,1},{1,0},{2,3},{3,2},{4,5},{5,4},{6,7},{7,6},{8,9},{9,8},{10,11... | collective-permute-start | bytes 1572872 | tf_op jit(solution)/shard_map/ppermute | solution.py:33
  35.6 5.6 %collective-permute-start.9 = (bf16[1024,256]{1,0:T(8,128)(2,1)}, bf16[1024,256]{1,0:T(8,128)(2,1)}, u32[]{:S(2)}, u32[]{:S(2)}) collective-permute-start(bf16[1024,256]{1,0:T(8,128)(2,1)} %get-tuple-element.90), channel_id=1, source_target_pairs={{0,1},{1,0},{2,3},{3,2},{4,5},{5,4},{6,7},{7,6},{8,9},{9,8},{10,11... | collective-permute-start | bytes 1572872 | tf_op jit(solution)/shard_map/ppermute | solution.py:33
  37.7 16.5 %collective-permute-start.4 = (bf16[2,1152,128]{2,1,0:T(8,128)(2,1)}, bf16[2,1152,128]{2,1,0:T(8,128)(2,1)S(1)}, u32[]{:S(2)}, u32[]{:S(2)}) collective-permute-start(bf16[2,1152,128]{2,1,0:T(8,128)(2,1)} %collective-permute-done.2.f2), channel_id=1, source_target_pairs={{0,32},{8,40},{16,48},{24,56},{32,64},{40,72},{48,80},{56,88},{64,... | collective-permute-start | bytes 1769480 | tf_op jit(solution)/shard_map/ppermute | solution.py:24
  37.7 0.8 copy-start.7
  38.5 15.7 %collective-permute-start.5 = (bf16[2,1152,128]{2,1,0:T(8,128)(2,1)}, bf16[2,1152,128]{2,1,0:T(8,128)(2,1)S(1)}, u32[]{:S(2)}, u32[]{:S(2)}) collective-permute-start(bf16[2,1152,128]{2,1,0:T(8,128)(2,1)} %collective-permute-done.3.b2), channel_id=1, source_target_pairs={{0,224},{8,232},{16,240},{24,248},{32,0},{40,8},{48,16},{56,24},{6... | collective-permute-start | bytes 1769480 | tf_op jit(solution)/shard_map/ppermute | solution.py:24
  44.9 29.0 %collective-permute-start.15 = (bf16[1024,256]{1,0:T(8,128)(2,1)}, bf16[1024,256]{1,0:T(8,128)(2,1)}, u32[]{:S(2)}, u32[]{:S(2)}) collective-permute-start(bf16[1024,256]{1,0:T(8,128)(2,1)} %get-tuple-element.88), channel_id=1, source_target_pairs={{0,2},{1,3},{2,4},{3,5},{4,6},{5,7},{6,0},{7,1},{8,10},{9,11},{10,... | collective-permute-start | bytes 1572872 | tf_op jit(solution)/shard_map/ppermute | solution.py:29
  46.2 27.8 %collective-permute-start.16 = (bf16[1024,256]{1,0:T(8,128)(2,1)}, bf16[1024,256]{1,0:T(8,128)(2,1)}, u32[]{:S(2)}, u32[]{:S(2)}) collective-permute-start(bf16[1024,256]{1,0:T(8,128)(2,1)} %get-tuple-element.87), channel_id=1, source_target_pairs={{0,4},{1,5},{2,6},{3,7},{4,0},{5,1},{6,2},{7,3},{8,12},{9,13},{10,... | collective-permute-start | bytes 1572872 | tf_op jit(solution)/shard_map/ppermute | solution.py:29
  48.8 25.1 %collective-permute-start.17 = (bf16[1024,256]{1,0:T(8,128)(2,1)}, bf16[1024,256]{1,0:T(8,128)(2,1)}, u32[]{:S(2)}, u32[]{:S(2)}) collective-permute-start(bf16[1024,256]{1,0:T(8,128)(2,1)} %get-tuple-element.86), channel_id=1, source_target_pairs={{0,6},{1,7},{2,0},{3,1},{4,2},{5,3},{6,4},{7,5},{8,14},{9,15},{10,... | collective-permute-start | bytes 1572872 | tf_op jit(solution)/shard_map/ppermute | solution.py:29
  55.1 14.7 %collective-permute-start.10 = (bf16[1152,128]{1,0:T(8,128)(2,1)}, bf16[1152,128]{1,0:T(8,128)(2,1)S(1)}, u32[]{:S(2)}, u32[]{:S(2)}) collective-permute-start(bf16[1152,128]{1,0:T(8,128)(2,1)} %get-tuple-element.55), channel_id=1, source_target_pairs={{0,32},{8,40},{16,48},{24,56},{32,64},{40,72},{48,80},{56,88},{64,... | collective-permute-start | bytes 884744 | tf_op jit(solution)/shard_map/ppermute | solution.py:24
  55.1 14.7 %collective-permute-start.11 = (bf16[1152,128]{1,0:T(8,128)(2,1)}, bf16[1152,128]{1,0:T(8,128)(2,1)}, u32[]{:S(2)}, u32[]{:S(2)}) collective-permute-start(bf16[1152,128]{1,0:T(8,128)(2,1)} %get-tuple-element.56), channel_id=1, source_target_pairs={{0,224},{8,232},{16,240},{24,248},{32,0},{40,8},{48,16},{56,24},{6... | collective-permute-start | bytes 884744 | tf_op jit(solution)/shard_map/ppermute | solution.py:24
  63.5 1.1 %copy-start.1 = (bf16[2,1152,128]{2,1,0:T(8,128)(2,1)S(1)}, bf16[2,1152,128]{2,1,0:T(8,128)(2,1)}, u32[]{:S(2)}) copy-start(bf16[2,1152,128]{2,1,0:T(8,128)(2,1)} %copy-done) | copy-start | bytes 1769476
  69.8 24.5 %copy-start.8 = (s32[16]{0:T(128)S(1)}, s32[16]{0:T(128)}, u32[]{:S(2)}) copy-start(s32[16]{0:T(128)} %param.17) | copy-start | bytes 196
  69.8 32.6 %copy-start.4 = (bf16[1,256]{1,0:T(2,128)(2,1)S(1)}, bf16[1,256]{1,0:T(2,128)(2,1)}, u32[]{:S(2)}) copy-start(bf16[1,256]{1,0:T(2,128)(2,1)} %bias.1) | copy-start | bytes 1540
  69.8 32.6 %copy-start.5 = (s32[16]{0:T(128)S(1)}, s32[16]{0:T(128)}, u32[]{:S(2)}) copy-start(s32[16]{0:T(128)} %span_ref.1) | copy-start | bytes 196
  71.8 3.8 %collective-permute-start.12 = (bf16[8,64,128]{2,1,0:T(8,128)(2,1)S(1)}, bf16[8,64,128]{2,1,0:T(8,128)(2,1)S(1)}, u32[]{:S(2)}, u32[]{:S(2)}) collective-permute-start(bf16[8,64,128]{2,1,0:T(8,128)(2,1)S(1)} %get-tuple-element.66), channel_id=1, source_target_pairs={{0,24},{8,0},{16,8},{24,16},{32,56},{40,32},{48,40},{56,48},{64,88... | collective-permute-start | bytes 393224 | tf_op jit(solution)/shard_map/ppermute | solution.py:19
  72.7 5.4 %collective-permute-start.13 = (bf16[8,64,128]{2,1,0:T(8,128)(2,1)S(1)}, bf16[8,64,128]{2,1,0:T(8,128)(2,1)S(1)}, u32[]{:S(2)}, u32[]{:S(2)}) collective-permute-start(bf16[8,64,128]{2,1,0:T(8,128)(2,1)S(1)} %get-tuple-element.67), channel_id=1, source_target_pairs={{0,16},{8,24},{16,0},{24,8},{32,48},{40,56},{48,32},{56,40},{64,80... | collective-permute-start | bytes 393224 | tf_op jit(solution)/shard_map/ppermute | solution.py:19
  73.9 6.0 %collective-permute-start.14 = (bf16[8,64,128]{2,1,0:T(8,128)(2,1)S(1)}, bf16[8,64,128]{2,1,0:T(8,128)(2,1)S(1)}, u32[]{:S(2)}, u32[]{:S(2)}) collective-permute-start(bf16[8,64,128]{2,1,0:T(8,128)(2,1)S(1)} %get-tuple-element.68), channel_id=1, source_target_pairs={{0,8},{8,16},{16,24},{24,0},{32,40},{40,48},{48,56},{56,32},{64,72... | collective-permute-start | bytes 393224 | tf_op jit(solution)/shard_map/ppermute | solution.py:19
  80.6 5.2 %collective-permute-start.18 = (bf16[8,64,128]{2,1,0:T(8,128)(2,1)S(1)}, bf16[8,64,128]{2,1,0:T(8,128)(2,1)S(1)}, u32[]{:S(2)}, u32[]{:S(2)}) collective-permute-start(bf16[8,64,128]{2,1,0:T(8,128)(2,1)S(1)} %get-tuple-element.74), channel_id=1, source_target_pairs={{0,1},{1,0},{2,3},{3,2},{4,5},{5,4},{6,7},{7,6},{8,9},{9,8},{10,11... | collective-permute-start | bytes 393224 | tf_op jit(solution)/shard_map/ppermute | solution.py:33
  83.7 7.9 %collective-permute-start.22 = (bf16[8,128,128]{2,1,0:T(8,128)(2,1)S(1)}, bf16[8,128,128]{2,1,0:T(8,128)(2,1)S(1)}, u32[]{:S(2)}, u32[]{:S(2)}) collective-permute-start(bf16[8,128,128]{2,1,0:T(8,128)(2,1)S(1)} %get-tuple-element.76), channel_id=1, source_target_pairs={{0,24},{8,0},{16,8},{24,16},{32,56},{40,32},{48,40},{56,48},{64,88... | collective-permute-start | bytes 786440 | tf_op jit(solution)/shard_map/ppermute | solution.py:19
  84.0 10.5 %collective-permute-start.23 = (bf16[8,128,128]{2,1,0:T(8,128)(2,1)}, bf16[8,128,128]{2,1,0:T(8,128)(2,1)S(1)}, u32[]{:S(2)}, u32[]{:S(2)}) collective-permute-start(bf16[8,128,128]{2,1,0:T(8,128)(2,1)} %get-tuple-element.77), channel_id=1, source_target_pairs={{0,16},{8,24},{16,0},{24,8},{32,48},{40,56},{48,32},{56,40},{64,80... | collective-permute-start | bytes 786440 | tf_op jit(solution)/shard_map/ppermute | solution.py:19
  85.2 14.4 %collective-permute-start.24 = (bf16[8,128,128]{2,1,0:T(8,128)(2,1)}, bf16[8,128,128]{2,1,0:T(8,128)(2,1)S(1)}, u32[]{:S(2)}, u32[]{:S(2)}) collective-permute-start(bf16[8,128,128]{2,1,0:T(8,128)(2,1)} %get-tuple-element.78), channel_id=1, source_target_pairs={{0,8},{8,16},{16,24},{24,0},{32,40},{40,48},{48,56},{56,32},{64,72... | collective-permute-start | bytes 786440 | tf_op jit(solution)/shard_map/ppermute | solution.py:19
  85.8 13.7 %collective-permute-start.19 = (bf16[8,64,128]{2,1,0:T(8,128)(2,1)S(1)}, bf16[8,64,128]{2,1,0:T(8,128)(2,1)S(1)}, u32[]{:S(2)}, u32[]{:S(2)}) collective-permute-start(bf16[8,64,128]{2,1,0:T(8,128)(2,1)S(1)} %add_convert_fusion.1), channel_id=1, source_target_pairs={{0,2},{1,3},{2,4},{3,5},{4,6},{5,7},{6,0},{7,1},{8,10},{9,11},{10,... | collective-permute-start | bytes 393224 | tf_op jit(solution)/shard_map/ppermute | solution.py:29
  87.2 12.4 %collective-permute-start.20 = (bf16[8,64,128]{2,1,0:T(8,128)(2,1)S(1)}, bf16[8,64,128]{2,1,0:T(8,128)(2,1)S(1)}, u32[]{:S(2)}, u32[]{:S(2)}) collective-permute-start(bf16[8,64,128]{2,1,0:T(8,128)(2,1)S(1)} %add_convert_fusion.1), channel_id=1, source_target_pairs={{0,4},{1,5},{2,6},{3,7},{4,0},{5,1},{6,2},{7,3},{8,12},{9,13},{10,... | collective-permute-start | bytes 393224 | tf_op jit(solution)/shard_map/ppermute | solution.py:29
  91.6 8.0 %collective-permute-start.21 = (bf16[8,64,128]{2,1,0:T(8,128)(2,1)S(1)}, bf16[8,64,128]{2,1,0:T(8,128)(2,1)S(1)}, u32[]{:S(2)}, u32[]{:S(2)}) collective-permute-start(bf16[8,64,128]{2,1,0:T(8,128)(2,1)S(1)} %add_convert_fusion.1), channel_id=1, source_target_pairs={{0,6},{1,7},{2,0},{3,1},{4,2},{5,3},{6,4},{7,5},{8,14},{9,15},{10,... | collective-permute-start | bytes 393224 | tf_op jit(solution)/shard_map/ppermute | solution.py:29
  99.7 2.7 %collective-permute-start.25 = (bf16[8,64,128]{2,1,0:T(8,128)(2,1)S(1)}, bf16[8,64,128]{2,1,0:T(8,128)(2,1)S(1)}, u32[]{:S(2)}, u32[]{:S(2)}) collective-permute-start(bf16[8,64,128]{2,1,0:T(8,128)(2,1)S(1)} %add_convert_fusion.mine), channel_id=1, source_target_pairs={{0,1},{1,0},{2,3},{3,2},{4,5},{5,4},{6,7},{7,6},{8,9},{9,8},{10,11... | collective-permute-start | bytes 393224 | tf_op jit(solution)/shard_map/ppermute | solution.py:33
